TPU v7x, 128 devices: a whole 4x4x4 slice. The times are simulated.
128 devices in a mesh: section: 8 (over y, core), table: 16 (over x, z).
Axes of the slice: x: 4, y: 4, z: 4, core: 2. Of those that a mesh axis runs over, the one named last changes fastest.
Arguments:
- emb_table: bfloat16 [524288, 128], P(('section', 'table')), may hold values from -6 to 6
- lcb_weight: bfloat16 [8, 512], replicated, may hold values from -0.25 to 0.25
- fm_proj: bfloat16 [8, 8, 128], P('section'), may hold values from -2 to 2
- norm_gain: bfloat16 [8, 1024], P('section'), may hold values from 0.25 to 1.75
- w_up: bfloat16 [8, 1024, 4096], P('section'), may hold values from -0.1875 to 0.1875
- w_down: bfloat16 [8, 4096, 1024], P('section'), may hold values from -0.09375 to 0.09375
- top_grad: bfloat16 [16, 4, 64, 1024], P('table'), may hold values from -12 to 12
- lookup_slot: int32 [16, 256, 512], P('table', 'section'), may hold values from 0 to 16383, as said below
- wanted_rows: int32 [128, 128, 128], P(('section', 'table')), may hold values from 0 to 4095, as said below
- row_counts: int32 [128, 128], P(('section', 'table')), may hold values from 32 to 128, as said below
Outputs:
- table_grad: float32 [524288, 128], P(('section', 'table'))
Inputs may be any that keep to these rules, and one draw needn't show every extreme that they name: The first row_counts[o, q] entries of wanted_rows[o, q] are distinct rows; the others are also rows of the owner. `row_counts`: some owners have 128 live slots for every asking device. `lookup_slot`: A lookup of asking device q names slot o * 128 + c with c below row_counts[o, q].
All inputs are finite; a program needn't handle non-finite values.
Results may differ from a plain program's by a relative error of at most 0.025.
Values may be sent and summed in bfloat16 or wider, within the bound.
A program may use at most 128 MiB of HBM per device.

v0:
```python
import jax
import jax.numpy as jnp
from jax import lax
from jax.sharding import PartitionSpec as P

EPSILON = 1e-05
DECAY_WEIGHT = 0.5


def shifted(value, axis, steps):
    count = lax.axis_size(axis)
    first, last = (max(0, -steps), min(count, count - steps))
    return lax.ppermute(value, axis, [(source, source + steps) for source in range(first, last)])


def broadcast(block, axis, holder):
    block = jnp.where(lax.axis_index(axis) == holder, block, jnp.zeros_like(block))
    return lax.psum(block, axis)


def fm_forward(inputs, proj, gain, w_up, w_down):
    batch_rows = inputs.shape[0]
    embed_count = proj.shape[0]
    features = inputs.reshape(batch_rows, embed_count, -1)
    mixed_cols = jnp.einsum(
        "bke,kr->bre", features, proj, preferred_element_type=jnp.float32
    ).astype(jnp.bfloat16)
    interact = jnp.einsum(
        "bke,bre->bkr", features, mixed_cols, preferred_element_type=jnp.float32
    ).reshape(batch_rows, -1)
    inv_scale = lax.rsqrt(jnp.mean(interact * interact, axis=1, keepdims=True) + EPSILON)
    normed = (interact * inv_scale * gain.astype(jnp.float32)).astype(jnp.bfloat16)
    before = jnp.dot(normed, w_up, preferred_element_type=jnp.float32)
    hidden = jnp.maximum(before, 0.0).astype(jnp.bfloat16)
    output = inputs.astype(jnp.float32) + jnp.dot(
        hidden, w_down, preferred_element_type=jnp.float32
    )
    return (output.astype(jnp.bfloat16), (features, mixed_cols, interact, inv_scale, before))


def fm_backward(inputs, grad_out, proj, gain, w_up, w_down):
    batch_rows = inputs.shape[0]
    embed_count = proj.shape[0]
    unused, saved = fm_forward(inputs, proj, gain, w_up, w_down)
    features, mixed_cols, interact, inv_scale, before = saved
    last_dims = (((1,), (1,)), ((), ()))
    g_hidden = lax.dot_general(grad_out, w_down, last_dims, preferred_element_type=jnp.float32)
    g_before = jnp.where(before > 0.0, g_hidden, 0.0).astype(jnp.bfloat16)
    g_normed = lax.dot_general(g_before, w_up, last_dims, preferred_element_type=jnp.float32)
    weighted = g_normed * gain.astype(jnp.float32)
    g_interact = inv_scale * (
        weighted
        - interact * inv_scale * inv_scale * jnp.mean(weighted * interact, axis=1, keepdims=True)
    )
    g_interact = g_interact.astype(jnp.bfloat16).reshape(batch_rows, embed_count, -1)
    g_features = jnp.einsum(
        "bkr,bre->bke", g_interact, mixed_cols, preferred_element_type=jnp.float32
    )
    g_mixed = jnp.einsum(
        "bkr,bke->bre", g_interact, features, preferred_element_type=jnp.float32
    ).astype(jnp.bfloat16)
    g_features = g_features + jnp.einsum(
        "bre,kr->bke", g_mixed, proj, preferred_element_type=jnp.float32
    )
    return (grad_out.astype(jnp.float32) + g_features.reshape(batch_rows, -1)).astype(jnp.bfloat16)


def pass_on(payload, offset):
    return shifted(payload, "section", offset)


def per_device(
    emb_table,
    lcb_weight,
    fm_proj,
    norm_gain,
    w_up,
    w_down,
    top_grad,
    lookup_slot,
    wanted_rows,
    row_counts,
):
    section_count = lax.axis_size("section")
    shard_count = lax.axis_size("table")
    my_section = lax.axis_index("section")
    owners = section_count * shard_count
    cap = wanted_rows.shape[2]
    embed_width = emb_table.shape[1]
    picked_rows = wanted_rows[0]
    outgoing = jnp.take(emb_table, picked_rows.reshape(-1), axis=0).reshape(
        owners, cap, embed_width
    )
    fetched = lax.all_to_all(
        outgoing, ("section", "table"), split_axis=0, concat_axis=0, tiled=True
    )
    fetched = fetched.reshape(owners * cap, embed_width)
    lookup_slots = lookup_slot[0]
    look_dev = lookup_slots.shape[0]
    feature_count = lookup_slots.shape[1]
    embedded = jnp.take(fetched, lookup_slots.reshape(-1), axis=0).reshape(
        look_dev, feature_count, embed_width
    )
    compressed = jnp.einsum(
        "kf,bfe->bke", lcb_weight, embedded, preferred_element_type=jnp.float32
    ).astype(jnp.bfloat16)
    compressed = compressed.reshape(look_dev, -1)
    leading = lax.all_gather(compressed, "section", axis=0, tiled=True)
    micro_count = top_grad.shape[1]
    batch_rows = top_grad.shape[2]
    model_width = top_grad.shape[3]
    leading = leading.reshape(micro_count, batch_rows, model_width)
    weights = (fm_proj[0], norm_gain[0], w_up[0], w_down[0])
    tick_count = micro_count + section_count - 1

    def forward_tick(tick, state):
        incoming, stash = state
        micro_idx = tick - my_section
        is_valid = (micro_idx >= 0) & (micro_idx < micro_count)
        clipped = jnp.clip(micro_idx, 0, micro_count - 1)
        inputs = jnp.where(
            my_section == 0, lax.dynamic_index_in_dim(leading, clipped, 0, keepdims=False), incoming
        )
        outputs = lax.cond(
            is_valid,
            lambda value: fm_forward(value, *weights)[0],
            lambda value: jnp.zeros_like(value),
            inputs,
        )
        kept_rows = jnp.where(
            is_valid, inputs, lax.dynamic_index_in_dim(stash, clipped, 0, keepdims=False)
        )
        stash = lax.dynamic_update_index_in_dim(stash, kept_rows, clipped, 0)
        return (pass_on(outputs, 1), stash)

    empty_rows = jnp.zeros((batch_rows, model_width), jnp.bfloat16)
    empty_stash = jnp.zeros((micro_count, batch_rows, model_width), jnp.bfloat16)
    unused, stash = lax.fori_loop(0, tick_count, forward_tick, (empty_rows, empty_stash))
    grads_top = top_grad[0]

    def backward_tick(tick, state):
        incoming, lead_grad = state
        micro_idx = tick - (section_count - 1 - my_section)
        is_valid = (micro_idx >= 0) & (micro_idx < micro_count)
        clipped = jnp.clip(micro_idx, 0, micro_count - 1)
        given = jnp.where(
            my_section == section_count - 1,
            lax.dynamic_index_in_dim(grads_top, clipped, 0, keepdims=False),
            incoming,
        )
        saved_rows = lax.dynamic_index_in_dim(stash, clipped, 0, keepdims=False)
        result = lax.cond(
            is_valid,
            lambda pair: fm_backward(pair[0], pair[1], *weights),
            lambda pair: jnp.zeros_like(pair[0]),
            (saved_rows, given),
        )
        record = jnp.where(
            is_valid & (my_section == 0),
            result,
            lax.dynamic_index_in_dim(lead_grad, clipped, 0, keepdims=False),
        )
        lead_grad = lax.dynamic_update_index_in_dim(lead_grad, record, clipped, 0)
        return (pass_on(result, -1), lead_grad)

    unused, lead_grad = lax.fori_loop(0, tick_count, backward_tick, (empty_rows, empty_stash))
    whole_grad = broadcast(lead_grad, "section", 0).reshape(micro_count * batch_rows, model_width)
    lead_share = lax.dynamic_slice_in_dim(whole_grad, my_section * look_dev, look_dev, 0)
    embed_count = lcb_weight.shape[0]
    feature_grad = jnp.einsum(
        "kf,bke->bfe",
        lcb_weight,
        lead_share.reshape(look_dev, embed_count, embed_width),
        preferred_element_type=jnp.float32,
    )
    slot_grad = jax.ops.segment_sum(
        feature_grad.reshape(-1, embed_width), lookup_slots.reshape(-1), num_segments=owners * cap
    )
    slot_grad = slot_grad.reshape(owners, cap, embed_width)
    returned = lax.all_to_all(
        slot_grad.astype(jnp.bfloat16),
        ("section", "table"),
        split_axis=0,
        concat_axis=0,
        tiled=True,
    ).astype(slot_grad.dtype)
    live_slots = jnp.arange(cap)[None, :] < row_counts[0][:, None]
    decay_term = jnp.where(live_slots[..., None], DECAY_WEIGHT * outgoing.astype(jnp.float32), 0.0)
    table_grad = (
        jnp.zeros(emb_table.shape, jnp.float32)
        .at[picked_rows.reshape(-1)]
        .add((returned + decay_term).reshape(-1, embed_width))
    )
    return table_grad


def solution(mesh):
    in_specs = (
        P(("section", "table"), None),
        P(),
        P("section", None, None),
        P("section", None),
        P("section", None, None),
        P("section", None, None),
        P("table", None, None, None),
        P("table", "section", None),
        P(("section", "table"), None, None),
        P(("section", "table"), None),
    )
    out_specs = P(("section", "table"), None)
    return jax.shard_map(
        per_device, mesh=mesh, in_specs=in_specs, out_specs=out_specs, check_vma=False
    )
```

profile of v0, /device:TPU:1, one launch (start us, length us, event | category | flops | bytes accessed | tf_op | source)
XLA Modules:
  0.0 1030.2 jit_solution(13412543603261010200)
XLA Ops:
  8.4 57.4 %gather_fusion = bf16[16384,128]{1,0:T(8,128)(2,1)} fusion(bf16[4096,128]{1,0:T(8,128)(2,1)S(1)} %copy-done, s32[16384]{0:T(1024)S(1)} %broadcast_clamp_fusion.1), kind=kCustom, calls=%fused_computation | custom fusion | bytes 8454144 | tf_op jit(solution)/shard_map/jit(_take)/gather | solution.py:91
  65.8 7.7 broadcast_select_fusion
  73.5 11.9 %all-to-all-start = ((bf16[128,128,128]{2,1,0:T(8,128)(2,1)}), bf16[128,128,128]{2,1,0:T(8,128)(2,1)}, u32[]{:S(2)}, u32[]{:S(2)}) async-start(bf16[128,128,128]{2,1,0:T(8,128)(2,1)} %broadcast_select_fusion), calls=%async_computation | async-start | bytes 8388608 | tf_op jit(solution)/shard_map/all_to_all | solution.py:94
  85.8 51.8 %all-to-all-done = bf16[128,128,128]{2,1,0:T(8,128)(2,1)} async-done(((bf16[128,128,128]{2,1,0:T(8,128)(2,1)}), bf16[128,128,128]{2,1,0:T(8,128)(2,1)}, u32[]{:S(2)}, u32[]{:S(2)}) %all-to-all-start) | async-done | bytes 4194336 | tf_op jit(solution)/shard_map/all_to_all | solution.py:94
  137.6 57.7 %gather_fusion.1 = bf16[16384,128]{1,0:T(8,128)(2,1)} fusion(bf16[16384,128]{1,0:T(8,128)(2,1)} %bitcast.17, s32[16384]{0:T(1024)S(1)} %broadcast_clamp_fusion), kind=kCustom, calls=%fused_computation.1 | custom fusion | bytes 8454144 | tf_op jit(solution)/shard_map/jit(_take)/gather | solution.py:101
  195.2 4.7 fusion.45
  199.9 13.5 %all_gather.3 = bf16[256,1024]{1,0:T(8,128)(2,1)S(1)} all-gather(bf16[32,1024]{1,0:T(8,128)(2,1)S(1)} %bitcast.174), channel_id=1, replica_groups=mesh['section'=8,'table'=16] {'section'}, dimensions={0}, use_global_device_ids=true | all-gather | bytes 589824 | tf_op jit(solution)/shard_map/all_gather | solution.py:108
  214.3 158.9 %while.33 = (s32[]{:T(128)}, bf16[64,1024]{1,0:T(8,128)(2,1)S(1)}, bf16[4,64,1024]{2,1,0:T(8,128)(2,1)}, s32[]{:T(128)}, pred[]{:T(512)}, /*index=5*/bf16[4,64,1...) while((s32[]{:T(128)}, bf16[64,1024]{1,0:T(8,128)(2,1)S(1)}, ...), condition=%wide.region_4.5_spmd, body=%wide.region_0.4_spmd.sunk | while | flops 1109525504 | bytes 19412772 | solution.py:138
  216.0 2.0 collective-permute-start
  218.0 11.2 %collective-permute-done = bf16[64,1024]{1,0:T(8,128)(2,1)S(1)} collective-permute-done((bf16[64,1024]{1,0:T(8,128)(2,1)S(1)}, bf16[64,1024]{1,0:T(8,128)(2,1)S(1)}, u32[]{:S(2)}, u32[]{:S(2)}) %collective-permute-start) | collective-permute-done | bytes 131104 | tf_op jit(solution)/shard_map/while/body/eval_jaxpr/ppermute | solution.py:13
  230.8 10.9 %conditional.4 = (bf16[64,1024]{1,0:T(8,128)(2,1)S(1)}) conditional(s32[]{:T(128)} %convert_element_type.140, () %tuple.88, (bf16[64,1024]{1,0:T(8,128)(2,1)S(1)}, bf16[8,128]{1,0:T(8,128)(2,1)S(1)}, bf16[1024]{0:T(1024)(128)(2,1)S(1)}, bf16[1024,4096]{1,0:T(8,128)(2,1)}, bf16[4096,1024]{1,0:T(8,128)(2,1)}) %tuple.89), branch_computations={%region_1.1_spmd, %region_2.3_spmd} | conditional | flops 1109394432 | bytes 17970184 | solution.py:124
  232.7 8.9 fusion.6
  243.5 1.9 collective-permute-done
  247.1 10.9 %conditional.4 = (bf16[64,1024]{1,0:T(8,128)(2,1)S(1)}) conditional(s32[]{:T(128)} %convert_element_type.140, () %tuple.88, (bf16[64,1024]{1,0:T(8,128)(2,1)S(1)}, bf16[8,128]{1,0:T(8,128)(2,1)S(1)}, bf16[1024]{0:T(1024)(128)(2,1)S(1)}, bf16[1024,4096]{1,0:T(8,128)(2,1)}, bf16[4096,1024]{1,0:T(8,128)(2,1)}) %tuple.89), branch_computations={%region_1.1_spmd, %region_2.3_spmd} | conditional | flops 1109394432 | bytes 17970184 | solution.py:124
  249.1 8.9 fusion.6
  258.0 4.3 collective-permute-start
  262.3 1.9 collective-permute-done
  265.9 10.9 %conditional.4 = (bf16[64,1024]{1,0:T(8,128)(2,1)S(1)}) conditional(s32[]{:T(128)} %convert_element_type.140, () %tuple.88, (bf16[64,1024]{1,0:T(8,128)(2,1)S(1)}, bf16[8,128]{1,0:T(8,128)(2,1)S(1)}, bf16[1024]{0:T(1024)(128)(2,1)S(1)}, bf16[1024,4096]{1,0:T(8,128)(2,1)}, bf16[4096,1024]{1,0:T(8,128)(2,1)}) %tuple.89), branch_computations={%region_1.1_spmd, %region_2.3_spmd} | conditional | flops 1109394432 | bytes 17970184 | solution.py:124
  267.8 8.9 fusion.6
  276.7 4.4 collective-permute-start
  281.1 1.9 collective-permute-done
  284.7 10.9 %conditional.4 = (bf16[64,1024]{1,0:T(8,128)(2,1)S(1)}) conditional(s32[]{:T(128)} %convert_element_type.140, () %tuple.88, (bf16[64,1024]{1,0:T(8,128)(2,1)S(1)}, bf16[8,128]{1,0:T(8,128)(2,1)S(1)}, bf16[1024]{0:T(1024)(128)(2,1)S(1)}, bf16[1024,4096]{1,0:T(8,128)(2,1)}, bf16[4096,1024]{1,0:T(8,128)(2,1)}) %tuple.89), branch_computations={%region_1.1_spmd, %region_2.3_spmd} | conditional | flops 1109394432 | bytes 17970184 | solution.py:124
  286.6 8.9 fusion.6
  295.5 4.3 collective-permute-start
  299.9 1.9 collective-permute-done
  303.5 15.2 %collective-permute-start = (bf16[64,1024]{1,0:T(8,128)(2,1)S(1)}, bf16[64,1024]{1,0:T(8,128)(2,1)S(1)}, u32[]{:S(2)}, u32[]{:S(2)}) collective-permute-start(bf16[64,1024]{1,0:T(8,128)(2,1)S(1)} %get-tuple-element.833), channel_id=1, source_target_pairs={{0,16},{16,32},{32,48},{48,64},{64,80},{80,96},{96,112},{1,17},{17... | collective-permute-start | bytes 393224 | tf_op jit(solution)/shard_map/while/body/eval_jaxpr/ppermute | solution.py:13
  322.3 4.4 collective-permute-start
  330.2 8.8 collective-permute-start
  342.6 4.4 collective-permute-start
  350.5 12.8 %collective-permute-start = (bf16[64,1024]{1,0:T(8,128)(2,1)S(1)}, bf16[64,1024]{1,0:T(8,128)(2,1)S(1)}, u32[]{:S(2)}, u32[]{:S(2)}) collective-permute-start(bf16[64,1024]{1,0:T(8,128)(2,1)S(1)} %get-tuple-element.833), channel_id=1, source_target_pairs={{0,16},{16,32},{32,48},{48,64},{64,80},{80,96},{96,112},{1,17},{17... | collective-permute-start | bytes 393224 | tf_op jit(solution)/shard_map/while/body/eval_jaxpr/ppermute | solution.py:13
  366.9 4.4 collective-permute-start
  374.0 324.0 %while.34 = (s32[]{:T(128)}, bf16[64,1024]{1,0:T(8,128)(2,1)S(1)}, bf16[4,64,1024]{2,1,0:T(8,128)(2,1)}, s32[]{:T(128)}, pred[]{:T(512)}, /*index=5*/bf16[4,64,1...) while((s32[]{:T(128)}, bf16[64,1024]{1,0:T(8,128)(2,1)S(1)}, ...), condition=%wide.region_10.11_spmd, body=%wide.region_5.0_spmd.sunk | while | flops 1698759680 | bytes 38033496 | solution.py:166
  377.8 7.8 collective-permute-done.1
  389.3 2.7 collective-permute-done.1
  395.6 11.7 %collective-permute-done.1 = bf16[64,1024]{1,0:T(8,128)(2,1)S(1)} collective-permute-done((bf16[64,1024]{1,0:T(8,128)(2,1)S(1)}, bf16[64,1024]{1,0:T(8,128)(2,1)S(1)}, u32[]{:S(2)}, u32[]{:S(2)}) %collective-permute-start.1) | collective-permute-done | bytes 131104 | tf_op jit(solution)/shard_map/while/body/eval_jaxpr/ppermute | solution.py:13
  410.9 2.7 collective-permute-done.1
  417.2 7.7 collective-permute-done.1
  428.5 132.5 %collective-permute-done.1 = bf16[64,1024]{1,0:T(8,128)(2,1)S(1)} collective-permute-done((bf16[64,1024]{1,0:T(8,128)(2,1)S(1)}, bf16[64,1024]{1,0:T(8,128)(2,1)S(1)}, u32[]{:S(2)}, u32[]{:S(2)}) %collective-permute-start.1) | collective-permute-done | bytes 131104 | tf_op jit(solution)/shard_map/while/body/eval_jaxpr/ppermute | solution.py:13
  561.0 22.3 %conditional.5 = (bf16[64,1024]{1,0:T(8,128)(2,1)S(1)}) conditional(s32[]{:T(128)} %convert_element_type.141, () %tuple.91, (pred[]{:T(512)}, bf16[4,64,1024]{2,1,0:T(8,128)(2,1)}, s32[]{:T(128)}, bf16[64,1024]{1,0:T(8,128)(2,1)S(1)}, bf16[4,64,1024]{2,1,0:T(8,128)(2,1)}, /*index=5*/bf16[8,128]{1,0:T(8,128)(2,1)S(1)}, bf16[1024]{0:T(1024)(128)(2,1)S(1)}, ...), branch_computations={%region_6.6_spmd, %region_7.9_spmd} | conditional | flops 1698694144 | bytes 36853008 | solution.py:152
  563.7 5.1 convolution_compare_fusion
  568.8 11.1 %fusion.30 = (f32[64]{0:T(128)S(1)}, f32[64,1024]{1,0:T(8,128)S(1)}) fusion(f32[8,8,8,128]{3,2,1,0:T(8,128)S(1)} %bitcast.151, f32[1024]{0:T(1024)S(1)} %convert_element_type.85, bf16[1024,4096]{1,0:T(8,128)(2,1)} %get-tuple-element.534, pred[64,4096]{1,0:T(32,128)(4,1)S(1)} %convolution_compare_fusion, bf16[4096,1024]{1,0:T(8,128)(2,1)} %get-tuple-element.535, ...), kind=kOutput, calls=%fused_computation.42 | convolution fusion | flops 1074528256 | bytes 17831168 | tf_op jit(solution)/shard_map/while/body/eval_jaxpr/cond/branch_1_fun/dot_general | solution.py:49
  586.8 2.7 collective-permute-done.1
  589.6 22.3 %conditional.5 = (bf16[64,1024]{1,0:T(8,128)(2,1)S(1)}) conditional(s32[]{:T(128)} %convert_element_type.141, () %tuple.91, (pred[]{:T(512)}, bf16[4,64,1024]{2,1,0:T(8,128)(2,1)}, s32[]{:T(128)}, bf16[64,1024]{1,0:T(8,128)(2,1)S(1)}, bf16[4,64,1024]{2,1,0:T(8,128)(2,1)}, /*index=5*/bf16[8,128]{1,0:T(8,128)(2,1)S(1)}, bf16[1024]{0:T(1024)(128)(2,1)S(1)}, ...), branch_computations={%region_6.6_spmd, %region_7.9_spmd} | conditional | flops 1698694144 | bytes 36853008 | solution.py:152
  592.3 5.1 convolution_compare_fusion
  597.3 11.1 %fusion.30 = (f32[64]{0:T(128)S(1)}, f32[64,1024]{1,0:T(8,128)S(1)}) fusion(f32[8,8,8,128]{3,2,1,0:T(8,128)S(1)} %bitcast.151, f32[1024]{0:T(1024)S(1)} %convert_element_type.85, bf16[1024,4096]{1,0:T(8,128)(2,1)} %get-tuple-element.534, pred[64,4096]{1,0:T(32,128)(4,1)S(1)} %convolution_compare_fusion, bf16[4096,1024]{1,0:T(8,128)(2,1)} %get-tuple-element.535, ...), kind=kOutput, calls=%fused_computation.42 | convolution fusion | flops 1074528256 | bytes 17831168 | tf_op jit(solution)/shard_map/while/body/eval_jaxpr/cond/branch_1_fun/dot_general | solution.py:49
  615.4 2.7 collective-permute-done.1
  618.1 22.3 %conditional.5 = (bf16[64,1024]{1,0:T(8,128)(2,1)S(1)}) conditional(s32[]{:T(128)} %convert_element_type.141, () %tuple.91, (pred[]{:T(512)}, bf16[4,64,1024]{2,1,0:T(8,128)(2,1)}, s32[]{:T(128)}, bf16[64,1024]{1,0:T(8,128)(2,1)S(1)}, bf16[4,64,1024]{2,1,0:T(8,128)(2,1)}, /*index=5*/bf16[8,128]{1,0:T(8,128)(2,1)S(1)}, bf16[1024]{0:T(1024)(128)(2,1)S(1)}, ...), branch_computations={%region_6.6_spmd, %region_7.9_spmd} | conditional | flops 1698694144 | bytes 36853008 | solution.py:152
  620.8 5.1 convolution_compare_fusion
  625.9 11.1 %fusion.30 = (f32[64]{0:T(128)S(1)}, f32[64,1024]{1,0:T(8,128)S(1)}) fusion(f32[8,8,8,128]{3,2,1,0:T(8,128)S(1)} %bitcast.151, f32[1024]{0:T(1024)S(1)} %convert_element_type.85, bf16[1024,4096]{1,0:T(8,128)(2,1)} %get-tuple-element.534, pred[64,4096]{1,0:T(32,128)(4,1)S(1)} %convolution_compare_fusion, bf16[4096,1024]{1,0:T(8,128)(2,1)} %get-tuple-element.535, ...), kind=kOutput, calls=%fused_computation.42 | convolution fusion | flops 1074528256 | bytes 17831168 | tf_op jit(solution)/shard_map/while/body/eval_jaxpr/cond/branch_1_fun/dot_general | solution.py:49
  644.0 2.7 collective-permute-done.1
  646.7 22.3 %conditional.5 = (bf16[64,1024]{1,0:T(8,128)(2,1)S(1)}) conditional(s32[]{:T(128)} %convert_element_type.141, () %tuple.91, (pred[]{:T(512)}, bf16[4,64,1024]{2,1,0:T(8,128)(2,1)}, s32[]{:T(128)}, bf16[64,1024]{1,0:T(8,128)(2,1)S(1)}, bf16[4,64,1024]{2,1,0:T(8,128)(2,1)}, /*index=5*/bf16[8,128]{1,0:T(8,128)(2,1)S(1)}, bf16[1024]{0:T(1024)(128)(2,1)S(1)}, ...), branch_computations={%region_6.6_spmd, %region_7.9_spmd} | conditional | flops 1698694144 | bytes 36853008 | solution.py:152
  649.4 5.1 convolution_compare_fusion
  654.5 11.1 %fusion.30 = (f32[64]{0:T(128)S(1)}, f32[64,1024]{1,0:T(8,128)S(1)}) fusion(f32[8,8,8,128]{3,2,1,0:T(8,128)S(1)} %bitcast.151, f32[1024]{0:T(1024)S(1)} %convert_element_type.85, bf16[1024,4096]{1,0:T(8,128)(2,1)} %get-tuple-element.534, pred[64,4096]{1,0:T(32,128)(4,1)S(1)} %convolution_compare_fusion, bf16[4096,1024]{1,0:T(8,128)(2,1)} %get-tuple-element.535, ...), kind=kOutput, calls=%fused_computation.42 | convolution fusion | flops 1074528256 | bytes 17831168 | tf_op jit(solution)/shard_map/while/body/eval_jaxpr/cond/branch_1_fun/dot_general | solution.py:49
  672.5 2.7 collective-permute-done.1
  675.3 21.1 %collective-permute-start.1 = (bf16[64,1024]{1,0:T(8,128)(2,1)S(1)}, bf16[64,1024]{1,0:T(8,128)(2,1)S(1)}, u32[]{:S(2)}, u32[]{:S(2)}) collective-permute-start(bf16[64,1024]{1,0:T(8,128)(2,1)S(1)} %get-tuple-element.834), channel_id=1, source_target_pairs={{16,0},{32,16},{48,32},{64,48},{80,64},{96,80},{112,96},{17,1},{33... | collective-permute-start | bytes 393224 | tf_op jit(solution)/shard_map/while/body/eval_jaxpr/ppermute | solution.py:13
  699.0 54.9 %all-reduce.2.cloned.1.call-done = bf16[256,1024]{1,0:T(8,128)(2,1)} async-done(((bf16[256,1024]{1,0:T(8,128)(2,1)}), bf16[256,1024]{1,0:T(8,128)(2,1)}) %all-reduce.2.cloned.1.call-update) | async-done | bytes 524304 | tf_op jit(solution)/shard_map/psum | solution.py:18
  754.7 4.5 convolution_bitcast_fusion
  759.2 9.0 copy.11
  768.1 91.3 %scatter_custom_fusion = f32[16384,128]{1,0:T(8,128)} fusion(s32[16384]{0:T(1024)S(1)} %bitcast.180, f32[16384,128]{1,0:T(8,128)} %bitcast.164, f32[]{:T(128)} %constant.174.clone.1), kind=kCustom, calls=%fused_computation.63 | custom fusion | flops 2097152 | bytes 8389120 | tf_op jit(solution)/shard_map/scatter-add | solution.py:176
  859.5 5.1 convert_element_type.100
  864.6 10.0 all-to-all-start.1
  874.6 52.0 %all-to-all-done.1 = bf16[128,128,128]{2,1,0:T(8,128)(2,1)} async-done(((bf16[128,128,128]{2,1,0:T(8,128)(2,1)}), bf16[128,128,128]{2,1,0:T(8,128)(2,1)}, u32[]{:S(2)}, u32[]{:S(2)}) %all-to-all-start.1) | async-done | bytes 4194336 | tf_op jit(solution)/shard_map/all_to_all | solution.py:180
  926.6 7.8 select_add_fusion
  934.4 89.0 %scatter_custom_fusion.1 = f32[4096,128]{1,0:T(8,128)} fusion(s32[16384]{0:T(1024)S(1)} %bitcast.177, f32[16384,128]{1,0:T(8,128)} %bitcast.163, f32[]{:T(128)} %constant.174.clone.1), kind=kCustom, calls=%fused_computation.70 | custom fusion | flops 2097152 | bytes 2097664 | tf_op jit(solution)/shard_map/scatter-add | solution.py:192
  (188 shorter events, 106.4 us)
Async XLA Ops:
  6.5 1.9 copy-start
  73.5 12.0 %copy-start.2 = (s32[1,32,512]{2,1,0:T(8,128)S(1)}, s32[1,32,512]{2,1,0:T(8,128)}, u32[]{:S(2)}) copy-start(s32[1,32,512]{2,1,0:T(8,128)} %param.25) | copy-start | bytes 196612
  73.5 12.1 %copy-start.5 = (bf16[1,1024]{1,0:T(2,128)(2,1)S(1)}, bf16[1,1024]{1,0:T(2,128)(2,1)}, u32[]{:S(2)}) copy-start(bf16[1,1024]{1,0:T(2,128)(2,1)} %param.21) | copy-start | bytes 6148
  73.5 64.0 %all-to-all-start = ((bf16[128,128,128]{2,1,0:T(8,128)(2,1)}), bf16[128,128,128]{2,1,0:T(8,128)(2,1)}, u32[]{:S(2)}, u32[]{:S(2)}) async-start(bf16[128,128,128]{2,1,0:T(8,128)(2,1)} %broadcast_select_fusion), calls=%async_computation | async-start | bytes 8388608 | tf_op jit(solution)/shard_map/all_to_all | solution.py:94
  85.5 668.3 %all-reduce.2.cloned.1.call-start = ((), (), s32[]{:S(2)}) async-start(), calls=%async_computation.2 | async-start | bytes 1048576 | tf_op jit(solution)/shard_map/psum | solution.py:18
  137.5 57.7 %copy-start.4 = (bf16[8,512]{1,0:T(8,128)(2,1)S(1)}, bf16[8,512]{1,0:T(8,128)(2,1)}, u32[]{:S(2)}) copy-start(bf16[8,512]{1,0:T(8,128)(2,1)} %param.19) | copy-start | bytes 24580
  195.2 19.1 %copy-start.3 = (bf16[1,8,128]{2,1,0:T(8,128)(2,1)S(1)}, bf16[1,8,128]{2,1,0:T(8,128)(2,1)}, u32[]{:S(2)}) copy-start(bf16[1,8,128]{2,1,0:T(8,128)(2,1)} %param.20) | copy-start | bytes 6148
  216.0 13.1 %collective-permute-start = (bf16[64,1024]{1,0:T(8,128)(2,1)S(1)}, bf16[64,1024]{1,0:T(8,128)(2,1)S(1)}, u32[]{:S(2)}, u32[]{:S(2)}) collective-permute-start(bf16[64,1024]{1,0:T(8,128)(2,1)S(1)} %get-tuple-element.833), channel_id=1, source_target_pairs={{0,16},{16,32},{32,48},{48,64},{64,80},{80,96},{96,112},{1,17},{17... | collective-permute-start | bytes 393224 | tf_op jit(solution)/shard_map/while/body/eval_jaxpr/ppermute | solution.py:13
  241.6 3.9 collective-permute-start
  258.0 6.3 collective-permute-start
  276.7 6.3 collective-permute-start
  295.5 6.3 collective-permute-start
  303.5 17.1 %collective-permute-start = (bf16[64,1024]{1,0:T(8,128)(2,1)S(1)}, bf16[64,1024]{1,0:T(8,128)(2,1)S(1)}, u32[]{:S(2)}, u32[]{:S(2)}) collective-permute-start(bf16[64,1024]{1,0:T(8,128)(2,1)S(1)} %get-tuple-element.833), channel_id=1, source_target_pairs={{0,16},{16,32},{32,48},{48,64},{64,80},{80,96},{96,112},{1,17},{17... | collective-permute-start | bytes 393224 | tf_op jit(solution)/shard_map/while/body/eval_jaxpr/ppermute | solution.py:13
  322.3 6.3 collective-permute-start
  330.2 10.7 %collective-permute-start = (bf16[64,1024]{1,0:T(8,128)(2,1)S(1)}, bf16[64,1024]{1,0:T(8,128)(2,1)S(1)}, u32[]{:S(2)}, u32[]{:S(2)}) collective-permute-start(bf16[64,1024]{1,0:T(8,128)(2,1)S(1)} %get-tuple-element.833), channel_id=1, source_target_pairs={{0,16},{16,32},{32,48},{48,64},{64,80},{80,96},{96,112},{1,17},{17... | collective-permute-start | bytes 393224 | tf_op jit(solution)/shard_map/while/body/eval_jaxpr/ppermute | solution.py:13
  342.6 6.3 collective-permute-start
  350.5 14.7 %collective-permute-start = (bf16[64,1024]{1,0:T(8,128)(2,1)S(1)}, bf16[64,1024]{1,0:T(8,128)(2,1)S(1)}, u32[]{:S(2)}, u32[]{:S(2)}) collective-permute-start(bf16[64,1024]{1,0:T(8,128)(2,1)S(1)} %get-tuple-element.833), channel_id=1, source_target_pairs={{0,16},{16,32},{32,48},{48,64},{64,80},{80,96},{96,112},{1,17},{17... | collective-permute-start | bytes 393224 | tf_op jit(solution)/shard_map/while/body/eval_jaxpr/ppermute | solution.py:13
  366.9 6.3 collective-permute-start
  374.3 11.4 %collective-permute-start.1 = (bf16[64,1024]{1,0:T(8,128)(2,1)S(1)}, bf16[64,1024]{1,0:T(8,128)(2,1)S(1)}, u32[]{:S(2)}, u32[]{:S(2)}) collective-permute-start(bf16[64,1024]{1,0:T(8,128)(2,1)S(1)} %get-tuple-element.834), channel_id=1, source_target_pairs={{16,0},{32,16},{48,32},{64,48},{80,64},{96,80},{112,96},{17,1},{33... | collective-permute-start | bytes 393224 | tf_op jit(solution)/shard_map/while/body/eval_jaxpr/ppermute | solution.py:13
  385.7 6.3 collective-permute-start.1
  392.0 15.3 %collective-permute-start.1 = (bf16[64,1024]{1,0:T(8,128)(2,1)S(1)}, bf16[64,1024]{1,0:T(8,128)(2,1)S(1)}, u32[]{:S(2)}, u32[]{:S(2)}) collective-permute-start(bf16[64,1024]{1,0:T(8,128)(2,1)S(1)} %get-tuple-element.834), channel_id=1, source_target_pairs={{16,0},{32,16},{48,32},{64,48},{80,64},{96,80},{112,96},{17,1},{33... | collective-permute-start | bytes 393224 | tf_op jit(solution)/shard_map/while/body/eval_jaxpr/ppermute | solution.py:13
  407.3 6.3 collective-permute-start.1
  413.6 11.3 %collective-permute-start.1 = (bf16[64,1024]{1,0:T(8,128)(2,1)S(1)}, bf16[64,1024]{1,0:T(8,128)(2,1)S(1)}, u32[]{:S(2)}, u32[]{:S(2)}) collective-permute-start(bf16[64,1024]{1,0:T(8,128)(2,1)S(1)} %get-tuple-element.834), channel_id=1, source_target_pairs={{16,0},{32,16},{48,32},{64,48},{80,64},{96,80},{112,96},{17,1},{33... | collective-permute-start | bytes 393224 | tf_op jit(solution)/shard_map/while/body/eval_jaxpr/ppermute | solution.py:13
  424.9 136.1 %collective-permute-start.1 = (bf16[64,1024]{1,0:T(8,128)(2,1)S(1)}, bf16[64,1024]{1,0:T(8,128)(2,1)S(1)}, u32[]{:S(2)}, u32[]{:S(2)}) collective-permute-start(bf16[64,1024]{1,0:T(8,128)(2,1)S(1)} %get-tuple-element.834), channel_id=1, source_target_pairs={{16,0},{32,16},{48,32},{64,48},{80,64},{96,80},{112,96},{17,1},{33... | collective-permute-start | bytes 393224 | tf_op jit(solution)/shard_map/while/body/eval_jaxpr/ppermute | solution.py:13
  583.3 6.3 collective-permute-start.1
  611.8 6.3 collective-permute-start.1
  640.4 6.3 collective-permute-start.1
  669.0 6.3 collective-permute-start.1
  675.3 22.8 %collective-permute-start.1 = (bf16[64,1024]{1,0:T(8,128)(2,1)S(1)}, bf16[64,1024]{1,0:T(8,128)(2,1)S(1)}, u32[]{:S(2)}, u32[]{:S(2)}) collective-permute-start(bf16[64,1024]{1,0:T(8,128)(2,1)S(1)} %get-tuple-element.834), channel_id=1, source_target_pairs={{16,0},{32,16},{48,32},{64,48},{80,64},{96,80},{112,96},{17,1},{33... | collective-permute-start | bytes 393224 | tf_op jit(solution)/shard_map/while/body/eval_jaxpr/ppermute | solution.py:13
  864.6 10.0 copy-start.6
  864.6 62.0 %all-to-all-start.1 = ((bf16[128,128,128]{2,1,0:T(8,128)(2,1)}), bf16[128,128,128]{2,1,0:T(8,128)(2,1)}, u32[]{:S(2)}, u32[]{:S(2)}) async-start(bf16[128,128,128]{2,1,0:T(8,128)(2,1)} %bitcast.160), calls=%async_computation.1 | async-start | bytes 8388608 | tf_op jit(solution)/shard_map/all_to_all | solution.py:180
  926.6 96.8 %copy-start.1 = (bf16[4096,128]{1,0:T(8,128)(2,1)S(1)}, bf16[4096,128]{1,0:T(8,128)(2,1)}, u32[]{:S(2)}) copy-start(bf16[4096,128]{1,0:T(8,128)(2,1)} %param.18) | copy-start | bytes 3145732
Sparse Core Ops, SparseCore 0:
  699.0 54.7 all-reduce.1
where the time goes:
time: 1030 us
  waiting for transfers between devices  365 us (35%)
  other arithmetic  224 us (22%)
  local copies, waits for them, and re-layouts  151 us (15%)
  matrix products  133 us (13%)
  starting transfers between devices  129 us (13%)
  between operations  13.6 us (1%)
  blocking collectives  13.5 us (1%)
    ppermute x22, waiting for transfers between devices, shifted(): lax.ppermute(value, axis, [(source, source + steps) for source in range(f...  207 us
    ppermute x22, starting transfers between devices, shifted(): lax.ppermute(value, axis, [(source, source + steps) for source in range(f...  107 us
    scatter-add x1, other arithmetic, per_device(): jax.ops.segment_sum(feature_grad.reshape(-1, embed_width), lookup_slots.r...  91.3 us
    scatter-add x1, other arithmetic, per_device(): table_grad = jnp.zeros(emb_table.shape, jnp.float32).at[picked_rows.resha...  89 us
    gather x1, local copies, waits for them, and re-layouts, per_device(): jnp.take(fetched, lookup_slots.reshape(-1), axis=0)  57.7 us
    gather x1, local copies, waits for them, and re-layouts, per_device(): jnp.take(emb_table, picked_rows.reshape(-1), axis=0)  57.4 us
    psum x1, waiting for transfers between devices, broadcast(): return lax.psum(block, axis)  54.9 us
    all_to_all x1, waiting for transfers between devices, per_device(): lax.all_to_all(slot_grad.astype(jnp.bfloat16), ('section', 'table'), spli...  52 us
  transfers between devices with their start and end apart: 25, of which 24 were waited for; matrix products, arithmetic and copies ran while one was open for 2% of the time, Pallas kernels for 0%

commit v1 on v0

--- a/solution.py
+++ b/solution.py
@@ -1,7 +1,201 @@
 import jax
 import jax.numpy as jnp
 from jax import lax
+from jax.experimental import pallas as pl
+from jax.experimental.pallas import tpu as pltpu
 from jax.sharding import PartitionSpec as P
+
+BF = jnp.bfloat16
+F32 = jnp.float32
+NT = (((1,), (1,)), ((), ()))
+TN = (((0,), (0,)), ((), ()))
+
+
+def gather_rows(table, ids):
+    rows, width = table.shape
+    count = ids.shape[0]
+    block = 1024
+    chunk = 128
+
+    def body(idx, tab, out, wide, tmp):
+        step = pl.program_id(0)
+
+        @pl.when(step == 0)
+        def _():
+            wide[...] = tab[...].astype(F32)
+
+        @pl.loop(0, block // chunk)
+        def _(part):
+            base = step * block + part * chunk
+            for j in range(chunk):
+                tmp[pl.ds(j, 1), :] = wide[pl.ds(idx[base + j], 1), :]
+            out[pl.ds(pl.multiple_of(part * chunk, chunk), chunk), :] = tmp[...].astype(BF)
+
+    return pl.pallas_call(
+        body,
+        grid=(count // block,),
+        in_specs=[
+            pl.BlockSpec(memory_space=pltpu.SMEM),
+            pl.BlockSpec((rows, width), lambda i: (0, 0)),
+        ],
+        out_specs=pl.BlockSpec((block, width), lambda i: (i, 0)),
+        out_shape=jax.ShapeDtypeStruct((count, width), BF),
+        scratch_shapes=[pltpu.VMEM((rows, width), F32), pltpu.VMEM((chunk, width), F32)],
+        name="gather_rows",
+    )(ids, table)
+
+
+def scatter_rows(values, ids, rows):
+    count, width = values.shape
+    block = 1024
+    group = 16
+
+    def body(idx, val, out, acc, wide, sem):
+        step = pl.program_id(0)
+
+        @pl.when(step == 0)
+        def _():
+            acc[...] = jnp.zeros_like(acc)
+
+        wide[...] = val[...].astype(F32)
+
+        @pl.loop(0, block // (4 * group))
+        def _(part):
+            for sub in range(4):
+                at = part * (4 * group) + sub * group
+                base = step * block + at
+                where = [idx[base + j] for j in range(group)]
+                new = [
+                    acc[pl.ds(where[j], 1), :] + wide[pl.ds(at + j, 1), :]
+                    for j in range(group)
+                ]
+                for j in range(group):
+                    acc[pl.ds(where[j], 1), :] = new[j]
+
+        @pl.when(step == pl.num_programs(0) - 1)
+        def _():
+            copy = pltpu.make_async_copy(acc.at[pl.ds(0, rows), :], out, sem)
+            copy.start()
+            copy.wait()
+
+    return pl.pallas_call(
+        body,
+        grid=(count // block,),
+        in_specs=[
+            pl.BlockSpec(memory_space=pltpu.SMEM),
+            pl.BlockSpec((block, width), lambda i: (i, 0)),
+        ],
+        out_specs=pl.BlockSpec(memory_space=pl.ANY),
+        out_shape=jax.ShapeDtypeStruct((rows, width), F32),
+        scratch_shapes=[
+            pltpu.VMEM((rows + 8, width), F32),
+            pltpu.VMEM((block, width), F32),
+            pltpu.SemaphoreType.DMA,
+        ],
+        name="scatter_rows",
+    )(ids, values)
+
+
+def lookup_matrix(slots, lcb, owners, cap):
+    samples, features = slots.shape
+    embeds = lcb.shape[0]
+    shift = cap.bit_length() - 1
+
+    def body(slot_ref, lcb_ref, out_ref):
+        tiled = jnp.concatenate([lcb_ref[...].astype(F32)] * 2, axis=0).astype(BF)
+        zero = jnp.zeros((), BF)
+        lane_c = lax.broadcasted_iota(jnp.int32, (cap, features), 0)
+        parts = []
+        for h in range(2):
+            slot = slot_ref[0, pl.ds(h, 1), :]
+            owner = lax.shift_right_logical(slot, shift)
+            col = slot & (cap - 1)
+            picks = jnp.where(lane_c == col, 1.0, 0.0).astype(BF)
+            owner16 = jnp.broadcast_to(owner.astype(F32), (16, features)).astype(BF)
+            row = (lax.broadcasted_iota(jnp.int32, (16, features), 0) // embeds).astype(F32).astype(BF)
+            rows = []
+            for o in range(0, owners, 2):
+                rows.append(jnp.where(owner16 == row + jnp.asarray(float(o), BF), tiled, zero))
+            spread = jnp.concatenate(rows, axis=0)
+            got = lax.dot_general(spread, picks, NT, preferred_element_type=F32)
+            parts.append(got.reshape(owners // 2, 2, embeds, cap))
+        for par in range(2):
+            both = jnp.concatenate([parts[0][:, par], parts[1][:, par]], axis=1)
+            out_ref[:, :, par * cap : (par + 1) * cap] = both.astype(BF)
+
+    return pl.pallas_call(
+        body,
+        grid=(samples // 2,),
+        in_specs=[
+            pl.BlockSpec((1, 2, features), lambda i: (i, 0, 0)),
+            pl.BlockSpec((embeds, features), lambda i: (0, 0)),
+        ],
+        out_specs=pl.BlockSpec((owners // 2, 2 * embeds, 2 * cap), lambda i: (0, i, 0)),
+        out_shape=jax.ShapeDtypeStruct((owners // 2, samples * embeds, 2 * cap), BF),
+        cost_estimate=pl.CostEstimate(flops=2 * samples * owners * embeds * cap * features, bytes_accessed=16 << 20, transcendentals=0),
+        name="lookup_matrix",
+    )(slots.reshape(samples // 2, 2, features), lcb)
+
+
+def compress(matrix, fetched):
+    pairs, outs, slots = matrix.shape
+    width = fetched.shape[1]
+    step_pairs = 8
+
+    def body(mat, rows, out, acc):
+        step = pl.program_id(0)
+
+        @pl.when(step == 0)
+        def _():
+            acc[...] = jnp.zeros_like(acc)
+
+        total = acc[...]
+        for i in range(step_pairs):
+            total += jnp.dot(mat[i], rows[pl.ds(i * slots, slots), :], preferred_element_type=F32)
+        acc[...] = total
+
+        @pl.when(step == pl.num_programs(0) - 1)
+        def _():
+            out[...] = acc[...].astype(BF)
+
+    return pl.pallas_call(
+        body,
+        grid=(pairs // step_pairs,),
+        in_specs=[
+            pl.BlockSpec((step_pairs, outs, slots), lambda i: (i, 0, 0)),
+            pl.BlockSpec((step_pairs * slots, width), lambda i: (i, 0)),
+        ],
+        out_specs=pl.BlockSpec((outs, width), lambda i: (0, 0)),
+        out_shape=jax.ShapeDtypeStruct((outs, width), BF),
+        scratch_shapes=[pltpu.VMEM((outs, width), F32)],
+        name="compress",
+    )(matrix, fetched)
+
+
+def expand(matrix, grads, fetched, decay):
+    pairs, outs, slots = matrix.shape
+    width = fetched.shape[1]
+    step_pairs = 8
+
+    def body(mat, grad, rows, out):
+        for i in range(step_pairs):
+            at = pl.ds(i * slots, slots)
+            got = lax.dot_general(mat[i], grad[...], TN, preferred_element_type=F32)
+            out[at, :] = (got + decay * rows[at, :].astype(F32)).astype(BF)
+
+    return pl.pallas_call(
+        body,
+        grid=(pairs // step_pairs,),
+        in_specs=[
+            pl.BlockSpec((step_pairs, outs, slots), lambda i: (i, 0, 0)),
+            pl.BlockSpec((outs, width), lambda i: (0, 0)),
+            pl.BlockSpec((step_pairs * slots, width), lambda i: (i, 0)),
+        ],
+        out_specs=pl.BlockSpec((step_pairs * slots, width), lambda i: (i, 0)),
+        out_shape=jax.ShapeDtypeStruct((pairs * slots, width), BF),
+        name="expand",
+    )(matrix, grads, fetched)
+
 
 EPSILON = 1e-05
 DECAY_WEIGHT = 0.5
@@ -88,23 +282,15 @@
     cap = wanted_rows.shape[2]
     embed_width = emb_table.shape[1]
     picked_rows = wanted_rows[0]
-    outgoing = jnp.take(emb_table, picked_rows.reshape(-1), axis=0).reshape(
-        owners, cap, embed_width
-    )
+    outgoing = gather_rows(emb_table, picked_rows.reshape(-1)).reshape(owners, cap, embed_width)
     fetched = lax.all_to_all(
         outgoing, ("section", "table"), split_axis=0, concat_axis=0, tiled=True
     )
     fetched = fetched.reshape(owners * cap, embed_width)
     lookup_slots = lookup_slot[0]
     look_dev = lookup_slots.shape[0]
-    feature_count = lookup_slots.shape[1]
-    embedded = jnp.take(fetched, lookup_slots.reshape(-1), axis=0).reshape(
-        look_dev, feature_count, embed_width
-    )
-    compressed = jnp.einsum(
-        "kf,bfe->bke", lcb_weight, embedded, preferred_element_type=jnp.float32
-    ).astype(jnp.bfloat16)
-    compressed = compressed.reshape(look_dev, -1)
+    matrix = lookup_matrix(lookup_slots, lcb_weight, owners, cap)
+    compressed = compress(matrix, fetched).reshape(look_dev, -1)
     leading = lax.all_gather(compressed, "section", axis=0, tiled=True)
     micro_count = top_grad.shape[1]
     batch_rows = top_grad.shape[2]
@@ -166,32 +352,18 @@
     unused, lead_grad = lax.fori_loop(0, tick_count, backward_tick, (empty_rows, empty_stash))
     whole_grad = broadcast(lead_grad, "section", 0).reshape(micro_count * batch_rows, model_width)
     lead_share = lax.dynamic_slice_in_dim(whole_grad, my_section * look_dev, look_dev, 0)
-    embed_count = lcb_weight.shape[0]
-    feature_grad = jnp.einsum(
-        "kf,bke->bfe",
-        lcb_weight,
-        lead_share.reshape(look_dev, embed_count, embed_width),
-        preferred_element_type=jnp.float32,
-    )
-    slot_grad = jax.ops.segment_sum(
-        feature_grad.reshape(-1, embed_width), lookup_slots.reshape(-1), num_segments=owners * cap
-    )
-    slot_grad = slot_grad.reshape(owners, cap, embed_width)
+    slot_grad = expand(matrix, lead_share.reshape(-1, embed_width), fetched, DECAY_WEIGHT)
     returned = lax.all_to_all(
-        slot_grad.astype(jnp.bfloat16),
+        slot_grad.reshape(owners, cap, embed_width),
         ("section", "table"),
         split_axis=0,
         concat_axis=0,
         tiled=True,
-    ).astype(slot_grad.dtype)
+    ).reshape(owners * cap, embed_width)
+    rows_here = emb_table.shape[0]
     live_slots = jnp.arange(cap)[None, :] < row_counts[0][:, None]
-    decay_term = jnp.where(live_slots[..., None], DECAY_WEIGHT * outgoing.astype(jnp.float32), 0.0)
-    table_grad = (
-        jnp.zeros(emb_table.shape, jnp.float32)
-        .at[picked_rows.reshape(-1)]
-        .add((returned + decay_term).reshape(-1, embed_width))
-    )
-    return table_grad
+    targets = jnp.where(live_slots, picked_rows, rows_here).reshape(-1)
+    return scatter_rows(returned, targets, rows_here)
 
 
 def solution(mesh):

time: 1030 us -> 763 us (0.74)
  other arithmetic: 224 us -> 21.7 us
  local copies, waits for them, and re-layouts: 151 us -> 29 us
  Pallas kernels: 0 us -> 78.8 us
  waiting for transfers between devices: 365 us -> 350 us
    scatter-add x2 -> x0, other arithmetic: 180 us -> none  [the longest x1 91.3 us: per_device(): jax.ops.segment_sum(feature_grad.reshape(-1, embed_width), lookup_slots.r...]
    gather x2 -> x0, local copies, waits for them, and re-layouts: 115 us -> none  [the longest x1 57.7 us: per_device(): jnp.take(fetched, lookup_slots.reshape(-1), axis=0)]
    pallas_call x0 -> x5, Pallas kernels: none -> 78.8 us  [the longest x1 27.7 us: scatter_rows(): pl.pallas_call(body, grid=(count // block,), in_specs=[pl.BlockSpec(memor...]
    all_to_all x1, waiting for transfers between devices: 51.8 us -> 37.3 us  [per_device(): lax.all_to_all(outgoing, ('section', 'table'), split_axis=0, concat_axis=...]
  transfers between devices with their start and end apart: 25 -> 25, of which waited for: 24 -> 24; matrix products, arithmetic and copies ran while one was open for 2% -> 3% of each run, Pallas kernels for 0% -> 2%
where the time goes in v1:
time: 763 us; the launch traced here: 761 us
  waiting for transfers between devices  350 us (46%)
  starting transfers between devices  129 us (17%)
  matrix products  124 us (16%)
  Pallas kernels  78.8 us (10%)
  local copies, waits for them, and re-layouts  29 us (4%)
  other arithmetic  21.7 us (3%)
  blocking collectives  13.5 us (2%)
  between operations  13.5 us (2%)
    ppermute x22, waiting for transfers between devices, shifted(): lax.ppermute(value, axis, [(source, source + steps) for source in range(f...  207 us
    ppermute x22, starting transfers between devices, shifted(): lax.ppermute(value, axis, [(source, source + steps) for source in range(f...  107 us
    psum x1, waiting for transfers between devices, broadcast(): return lax.psum(block, axis)  54.9 us
    all_to_all x1, waiting for transfers between devices, per_device(): lax.all_to_all(slot_grad.reshape(owners, cap, embed_width), ('section', '...  51.4 us
    dot_general x4, matrix products, fm_backward(): lax.dot_general(g_before, w_up, last_dims, preferred_element_type=jnp.flo...  44.4 us
    all_to_all x1, waiting for transfers between devices, per_device(): lax.all_to_all(outgoing, ('section', 'table'), split_axis=0, concat_axis=...  37.3 us
    dot_general x4, matrix products, fm_forward(): jnp.dot(hidden, w_down, preferred_element_type=jnp.float32)  35.6 us
    pallas_call x1, Pallas kernels, scatter_rows(): pl.pallas_call(body, grid=(count // block,), in_specs=[pl.BlockSpec(memor...  27.7 us
  transfers between devices with their start and end apart: 25, of which 24 were waited for; matrix products, arithmetic and copies ran while one was open for 3% of the time, Pallas kernels for 2%

profile of v1, /device:TPU:1, one launch (start us, length us, event | category | flops | bytes accessed | tf_op | source)
XLA Modules:
  0.0 760.6 jit_solution(397896212563667130)
XLA Ops:
  6.5 18.6 %gather_rows.1 = bf16[16384,128]{1,0:T(8,128)(2,1)} custom-call(s32[16384]{0:T(1024)} %bitcast.139, bf16[4096,128]{1,0:T(8,128)(2,1)} %tab.1), custom_call_target="tpu_custom_call" | custom-call | tf_op jit(solution)/shard_map/gather_rows/pallas_call | solution.py:34
  25.1 11.9 %all-to-all-start = ((bf16[128,128,128]{2,1,0:T(8,128)(2,1)}), bf16[128,128,128]{2,1,0:T(8,128)(2,1)}, u32[]{:S(2)}, u32[]{:S(2)}) async-start(bf16[128,128,128]{2,1,0:T(8,128)(2,1)} %bitcast.130), calls=%async_computation | async-start | bytes 8388608 | tf_op jit(solution)/shard_map/all_to_all | solution.py:286
  37.8 14.0 %lookup_matrix.1.mat = bf16[64,256,256]{2,1,0:T(8,128)(2,1)} custom-call(s32[16,2,512]{2,1,0:T(2,128)} %reshape_squeeze.4.slot_ref, bf16[8,512]{1,0:T(8,128)(2,1)} %lcb_ref.1), custom_call_target="tpu_custom_call" | custom-call | flops 4294967296 | bytes 16777216 | tf_op jit(solution)/shard_map/lookup_matrix/pallas_call | solution.py:126
  51.8 37.3 %all-to-all-done = bf16[128,128,128]{2,1,0:T(8,128)(2,1)} async-done(((bf16[128,128,128]{2,1,0:T(8,128)(2,1)}), bf16[128,128,128]{2,1,0:T(8,128)(2,1)}, u32[]{:S(2)}, u32[]{:S(2)}) %all-to-all-start) | async-done | bytes 4194336 | tf_op jit(solution)/shard_map/all_to_all | solution.py:286
  89.1 8.6 %compress.1 = bf16[256,128]{1,0:T(8,128)(2,1)} custom-call(bf16[64,256,256]{2,1,0:T(8,128)(2,1)} %lookup_matrix.1.mat, bf16[16384,128]{1,0:T(8,128)(2,1)} %bitcast.16.rows), custom_call_target="tpu_custom_call" | custom-call | tf_op jit(solution)/shard_map/compress/pallas_call | solution.py:161
  98.6 13.5 %all_gather.3 = bf16[256,1024]{1,0:T(8,128)(2,1)S(1)} all-gather(bf16[32,1024]{1,0:T(8,128)(2,1)S(1)} %reshape.84), channel_id=1, replica_groups=mesh['section'=8,'table'=16] {'section'}, dimensions={0}, use_global_device_ids=true | all-gather | bytes 589824 | tf_op jit(solution)/shard_map/all_gather | solution.py:294
  113.0 158.9 %while.33 = (s32[]{:T(128)}, bf16[64,1024]{1,0:T(8,128)(2,1)S(1)}, bf16[4,64,1024]{2,1,0:T(8,128)(2,1)}, s32[]{:T(128)}, pred[]{:T(512)}, /*index=5*/bf16[4,64,1...) while((s32[]{:T(128)}, bf16[64,1024]{1,0:T(8,128)(2,1)S(1)}, ...), condition=%wide.region_4.5_spmd, body=%wide.region_0.4_spmd.sunk | while | flops 1109525504 | bytes 19412772 | solution.py:324
  114.7 2.0 collective-permute-start
  116.7 11.1 %collective-permute-done = bf16[64,1024]{1,0:T(8,128)(2,1)S(1)} collective-permute-done((bf16[64,1024]{1,0:T(8,128)(2,1)S(1)}, bf16[64,1024]{1,0:T(8,128)(2,1)S(1)}, u32[]{:S(2)}, u32[]{:S(2)}) %collective-permute-start) | collective-permute-done | bytes 131104 | tf_op jit(solution)/shard_map/while/body/eval_jaxpr/ppermute | solution.py:207
  129.4 10.9 %conditional.4 = (bf16[64,1024]{1,0:T(8,128)(2,1)S(1)}) conditional(s32[]{:T(128)} %convert_element_type.113, () %tuple.88, (bf16[64,1024]{1,0:T(8,128)(2,1)S(1)}, bf16[8,128]{1,0:T(8,128)(2,1)S(1)}, bf16[1024]{0:T(1024)(128)(2,1)S(1)}, bf16[1024,4096]{1,0:T(8,128)(2,1)}, bf16[4096,1024]{1,0:T(8,128)(2,1)}) %tuple.89), branch_computations={%region_1.1_spmd, %region_2.3_spmd} | conditional | flops 1109394432 | bytes 17970184 | solution.py:310
  131.4 8.9 %fusion.6 = bf16[64,1024]{1,0:T(8,128)(2,1)S(1)} fusion(bf16[4096,1024]{1,0:T(8,128)(2,1)} %get-tuple-element.515, bf16[1024,4096]{1,0:T(8,128)(2,1)} %get-tuple-element.514, bf16[64,1024]{1,0:T(8,128)(2,1)S(1)} %get-tuple-element.511, f32[8,8,8,128]{3,2,1,0:T(8,128)S(1)} %bitcast.134, f32[1024]{0:T(1024)S(1)} %convert_element_type.66, f32[64]{0:T(128)S(1)} %add_rsqrt_fusion), kind=kOutput, calls=%fused_computation.7 | convolution fusion | flops 1074659328 | bytes 17305856 | tf_op jit(solution)/shard_map/while/body/eval_jaxpr/cond/branch_1_fun/dot_general | solution.py:229
  142.2 1.9 collective-permute-done
  145.8 10.9 %conditional.4 = (bf16[64,1024]{1,0:T(8,128)(2,1)S(1)}) conditional(s32[]{:T(128)} %convert_element_type.113, () %tuple.88, (bf16[64,1024]{1,0:T(8,128)(2,1)S(1)}, bf16[8,128]{1,0:T(8,128)(2,1)S(1)}, bf16[1024]{0:T(1024)(128)(2,1)S(1)}, bf16[1024,4096]{1,0:T(8,128)(2,1)}, bf16[4096,1024]{1,0:T(8,128)(2,1)}) %tuple.89), branch_computations={%region_1.1_spmd, %region_2.3_spmd} | conditional | flops 1109394432 | bytes 17970184 | solution.py:310
  147.7 8.9 %fusion.6 = bf16[64,1024]{1,0:T(8,128)(2,1)S(1)} fusion(bf16[4096,1024]{1,0:T(8,128)(2,1)} %get-tuple-element.515, bf16[1024,4096]{1,0:T(8,128)(2,1)} %get-tuple-element.514, bf16[64,1024]{1,0:T(8,128)(2,1)S(1)} %get-tuple-element.511, f32[8,8,8,128]{3,2,1,0:T(8,128)S(1)} %bitcast.134, f32[1024]{0:T(1024)S(1)} %convert_element_type.66, f32[64]{0:T(128)S(1)} %add_rsqrt_fusion), kind=kOutput, calls=%fused_computation.7 | convolution fusion | flops 1074659328 | bytes 17305856 | tf_op jit(solution)/shard_map/while/body/eval_jaxpr/cond/branch_1_fun/dot_general | solution.py:229
  156.7 4.4 collective-permute-start
  161.0 1.9 collective-permute-done
  164.6 10.9 %conditional.4 = (bf16[64,1024]{1,0:T(8,128)(2,1)S(1)}) conditional(s32[]{:T(128)} %convert_element_type.113, () %tuple.88, (bf16[64,1024]{1,0:T(8,128)(2,1)S(1)}, bf16[8,128]{1,0:T(8,128)(2,1)S(1)}, bf16[1024]{0:T(1024)(128)(2,1)S(1)}, bf16[1024,4096]{1,0:T(8,128)(2,1)}, bf16[4096,1024]{1,0:T(8,128)(2,1)}) %tuple.89), branch_computations={%region_1.1_spmd, %region_2.3_spmd} | conditional | flops 1109394432 | bytes 17970184 | solution.py:310
  164.6 1.9 fusion.10
  166.5 8.9 %fusion.6 = bf16[64,1024]{1,0:T(8,128)(2,1)S(1)} fusion(bf16[4096,1024]{1,0:T(8,128)(2,1)} %get-tuple-element.515, bf16[1024,4096]{1,0:T(8,128)(2,1)} %get-tuple-element.514, bf16[64,1024]{1,0:T(8,128)(2,1)S(1)} %get-tuple-element.511, f32[8,8,8,128]{3,2,1,0:T(8,128)S(1)} %bitcast.134, f32[1024]{0:T(1024)S(1)} %convert_element_type.66, f32[64]{0:T(128)S(1)} %add_rsqrt_fusion), kind=kOutput, calls=%fused_computation.7 | convolution fusion | flops 1074659328 | bytes 17305856 | tf_op jit(solution)/shard_map/while/body/eval_jaxpr/cond/branch_1_fun/dot_general | solution.py:229
  175.5 4.3 collective-permute-start
  179.8 1.9 collective-permute-done
  183.4 10.9 %conditional.4 = (bf16[64,1024]{1,0:T(8,128)(2,1)S(1)}) conditional(s32[]{:T(128)} %convert_element_type.113, () %tuple.88, (bf16[64,1024]{1,0:T(8,128)(2,1)S(1)}, bf16[8,128]{1,0:T(8,128)(2,1)S(1)}, bf16[1024]{0:T(1024)(128)(2,1)S(1)}, bf16[1024,4096]{1,0:T(8,128)(2,1)}, bf16[4096,1024]{1,0:T(8,128)(2,1)}) %tuple.89), branch_computations={%region_1.1_spmd, %region_2.3_spmd} | conditional | flops 1109394432 | bytes 17970184 | solution.py:310
  185.3 8.9 %fusion.6 = bf16[64,1024]{1,0:T(8,128)(2,1)S(1)} fusion(bf16[4096,1024]{1,0:T(8,128)(2,1)} %get-tuple-element.515, bf16[1024,4096]{1,0:T(8,128)(2,1)} %get-tuple-element.514, bf16[64,1024]{1,0:T(8,128)(2,1)S(1)} %get-tuple-element.511, f32[8,8,8,128]{3,2,1,0:T(8,128)S(1)} %bitcast.134, f32[1024]{0:T(1024)S(1)} %convert_element_type.66, f32[64]{0:T(128)S(1)} %add_rsqrt_fusion), kind=kOutput, calls=%fused_computation.7 | convolution fusion | flops 1074659328 | bytes 17305856 | tf_op jit(solution)/shard_map/while/body/eval_jaxpr/cond/branch_1_fun/dot_general | solution.py:229
  194.2 4.4 collective-permute-start
  198.6 1.9 collective-permute-done
  202.2 15.2 %collective-permute-start = (bf16[64,1024]{1,0:T(8,128)(2,1)S(1)}, bf16[64,1024]{1,0:T(8,128)(2,1)S(1)}, u32[]{:S(2)}, u32[]{:S(2)}) collective-permute-start(bf16[64,1024]{1,0:T(8,128)(2,1)S(1)} %get-tuple-element.833), channel_id=1, source_target_pairs={{0,16},{16,32},{32,48},{48,64},{64,80},{80,96},{96,112},{1,17},{17... | collective-permute-start | bytes 393224 | tf_op jit(solution)/shard_map/while/body/eval_jaxpr/ppermute | solution.py:207
  217.4 1.9 collective-permute-done
  221.0 4.4 collective-permute-start
  225.4 1.9 collective-permute-done
  228.9 8.8 %collective-permute-start = (bf16[64,1024]{1,0:T(8,128)(2,1)S(1)}, bf16[64,1024]{1,0:T(8,128)(2,1)S(1)}, u32[]{:S(2)}, u32[]{:S(2)}) collective-permute-start(bf16[64,1024]{1,0:T(8,128)(2,1)S(1)} %get-tuple-element.833), channel_id=1, source_target_pairs={{0,16},{16,32},{32,48},{48,64},{64,80},{80,96},{96,112},{1,17},{17... | collective-permute-start | bytes 393224 | tf_op jit(solution)/shard_map/while/body/eval_jaxpr/ppermute | solution.py:207
  237.7 1.9 collective-permute-done
  241.3 4.4 collective-permute-start
  245.7 1.9 collective-permute-done
  249.2 12.8 %collective-permute-start = (bf16[64,1024]{1,0:T(8,128)(2,1)S(1)}, bf16[64,1024]{1,0:T(8,128)(2,1)S(1)}, u32[]{:S(2)}, u32[]{:S(2)}) collective-permute-start(bf16[64,1024]{1,0:T(8,128)(2,1)S(1)} %get-tuple-element.833), channel_id=1, source_target_pairs={{0,16},{16,32},{32,48},{48,64},{64,80},{80,96},{96,112},{1,17},{17... | collective-permute-start | bytes 393224 | tf_op jit(solution)/shard_map/while/body/eval_jaxpr/ppermute | solution.py:207
  265.6 4.4 collective-permute-start
  272.8 324.1 %while.34 = (s32[]{:T(128)}, bf16[64,1024]{1,0:T(8,128)(2,1)S(1)}, bf16[4,64,1024]{2,1,0:T(8,128)(2,1)}, s32[]{:T(128)}, pred[]{:T(512)}, /*index=5*/bf16[4,64,1...) while((s32[]{:T(128)}, bf16[64,1024]{1,0:T(8,128)(2,1)S(1)}, ...), condition=%wide.region_10.11_spmd, body=%wide.region_5.10_spmd.sunk | while | flops 1698759680 | bytes 38033496 | solution.py:352
  276.6 7.9 %collective-permute-done.1 = bf16[64,1024]{1,0:T(8,128)(2,1)S(1)} collective-permute-done((bf16[64,1024]{1,0:T(8,128)(2,1)S(1)}, bf16[64,1024]{1,0:T(8,128)(2,1)S(1)}, u32[]{:S(2)}, u32[]{:S(2)}) %collective-permute-start.1) | collective-permute-done | bytes 131104 | tf_op jit(solution)/shard_map/while/body/eval_jaxpr/ppermute | solution.py:207
  288.0 2.7 collective-permute-done.1
  294.3 11.7 %collective-permute-done.1 = bf16[64,1024]{1,0:T(8,128)(2,1)S(1)} collective-permute-done((bf16[64,1024]{1,0:T(8,128)(2,1)S(1)}, bf16[64,1024]{1,0:T(8,128)(2,1)S(1)}, u32[]{:S(2)}, u32[]{:S(2)}) %collective-permute-start.1) | collective-permute-done | bytes 131104 | tf_op jit(solution)/shard_map/while/body/eval_jaxpr/ppermute | solution.py:207
  309.6 2.7 collective-permute-done.1
  315.9 7.7 %collective-permute-done.1 = bf16[64,1024]{1,0:T(8,128)(2,1)S(1)} collective-permute-done((bf16[64,1024]{1,0:T(8,128)(2,1)S(1)}, bf16[64,1024]{1,0:T(8,128)(2,1)S(1)}, u32[]{:S(2)}, u32[]{:S(2)}) %collective-permute-start.1) | collective-permute-done | bytes 131104 | tf_op jit(solution)/shard_map/while/body/eval_jaxpr/ppermute | solution.py:207
  327.2 132.5 %collective-permute-done.1 = bf16[64,1024]{1,0:T(8,128)(2,1)S(1)} collective-permute-done((bf16[64,1024]{1,0:T(8,128)(2,1)S(1)}, bf16[64,1024]{1,0:T(8,128)(2,1)S(1)}, u32[]{:S(2)}, u32[]{:S(2)}) %collective-permute-start.1) | collective-permute-done | bytes 131104 | tf_op jit(solution)/shard_map/while/body/eval_jaxpr/ppermute | solution.py:207
  459.7 22.3 %conditional.5 = (bf16[64,1024]{1,0:T(8,128)(2,1)S(1)}) conditional(s32[]{:T(128)} %convert_element_type.114, () %tuple.91, (pred[]{:T(512)}, bf16[4,64,1024]{2,1,0:T(8,128)(2,1)}, s32[]{:T(128)}, bf16[64,1024]{1,0:T(8,128)(2,1)S(1)}, bf16[4,64,1024]{2,1,0:T(8,128)(2,1)}, /*index=5*/bf16[8,128]{1,0:T(8,128)(2,1)S(1)}, bf16[1024]{0:T(1024)(128)(2,1)S(1)}, ...), branch_computations={%region_6.6_spmd, %region_7.9_spmd} | conditional | flops 1698694144 | bytes 36853008 | solution.py:338
  462.4 5.1 convolution_compare_fusion
  467.5 11.1 %fusion.30 = (f32[64]{0:T(128)S(1)}, f32[64,1024]{1,0:T(8,128)S(1)}) fusion(f32[8,8,8,128]{3,2,1,0:T(8,128)S(1)} %bitcast.123, f32[1024]{0:T(1024)S(1)} %convert_element_type.73, bf16[1024,4096]{1,0:T(8,128)(2,1)} %get-tuple-element.534, pred[64,4096]{1,0:T(32,128)(4,1)S(1)} %convolution_compare_fusion, bf16[4096,1024]{1,0:T(8,128)(2,1)} %get-tuple-element.535, ...), kind=kOutput, calls=%fused_computation.38 | convolution fusion | flops 1074528256 | bytes 17831168 | tf_op jit(solution)/shard_map/while/body/eval_jaxpr/cond/branch_1_fun/dot_general | solution.py:243
  485.6 2.7 collective-permute-done.1
  488.3 22.3 %conditional.5 = (bf16[64,1024]{1,0:T(8,128)(2,1)S(1)}) conditional(s32[]{:T(128)} %convert_element_type.114, () %tuple.91, (pred[]{:T(512)}, bf16[4,64,1024]{2,1,0:T(8,128)(2,1)}, s32[]{:T(128)}, bf16[64,1024]{1,0:T(8,128)(2,1)S(1)}, bf16[4,64,1024]{2,1,0:T(8,128)(2,1)}, /*index=5*/bf16[8,128]{1,0:T(8,128)(2,1)S(1)}, bf16[1024]{0:T(1024)(128)(2,1)S(1)}, ...), branch_computations={%region_6.6_spmd, %region_7.9_spmd} | conditional | flops 1698694144 | bytes 36853008 | solution.py:338
  491.0 5.1 convolution_compare_fusion
  496.1 11.1 %fusion.30 = (f32[64]{0:T(128)S(1)}, f32[64,1024]{1,0:T(8,128)S(1)}) fusion(f32[8,8,8,128]{3,2,1,0:T(8,128)S(1)} %bitcast.123, f32[1024]{0:T(1024)S(1)} %convert_element_type.73, bf16[1024,4096]{1,0:T(8,128)(2,1)} %get-tuple-element.534, pred[64,4096]{1,0:T(32,128)(4,1)S(1)} %convolution_compare_fusion, bf16[4096,1024]{1,0:T(8,128)(2,1)} %get-tuple-element.535, ...), kind=kOutput, calls=%fused_computation.38 | convolution fusion | flops 1074528256 | bytes 17831168 | tf_op jit(solution)/shard_map/while/body/eval_jaxpr/cond/branch_1_fun/dot_general | solution.py:243
  514.2 2.7 collective-permute-done.1
  516.9 22.3 %conditional.5 = (bf16[64,1024]{1,0:T(8,128)(2,1)S(1)}) conditional(s32[]{:T(128)} %convert_element_type.114, () %tuple.91, (pred[]{:T(512)}, bf16[4,64,1024]{2,1,0:T(8,128)(2,1)}, s32[]{:T(128)}, bf16[64,1024]{1,0:T(8,128)(2,1)S(1)}, bf16[4,64,1024]{2,1,0:T(8,128)(2,1)}, /*index=5*/bf16[8,128]{1,0:T(8,128)(2,1)S(1)}, bf16[1024]{0:T(1024)(128)(2,1)S(1)}, ...), branch_computations={%region_6.6_spmd, %region_7.9_spmd} | conditional | flops 1698694144 | bytes 36853008 | solution.py:338
  519.6 5.1 convolution_compare_fusion
  524.7 11.1 %fusion.30 = (f32[64]{0:T(128)S(1)}, f32[64,1024]{1,0:T(8,128)S(1)}) fusion(f32[8,8,8,128]{3,2,1,0:T(8,128)S(1)} %bitcast.123, f32[1024]{0:T(1024)S(1)} %convert_element_type.73, bf16[1024,4096]{1,0:T(8,128)(2,1)} %get-tuple-element.534, pred[64,4096]{1,0:T(32,128)(4,1)S(1)} %convolution_compare_fusion, bf16[4096,1024]{1,0:T(8,128)(2,1)} %get-tuple-element.535, ...), kind=kOutput, calls=%fused_computation.38 | convolution fusion | flops 1074528256 | bytes 17831168 | tf_op jit(solution)/shard_map/while/body/eval_jaxpr/cond/branch_1_fun/dot_general | solution.py:243
  542.7 2.7 collective-permute-done.1
  545.5 22.3 %conditional.5 = (bf16[64,1024]{1,0:T(8,128)(2,1)S(1)}) conditional(s32[]{:T(128)} %convert_element_type.114, () %tuple.91, (pred[]{:T(512)}, bf16[4,64,1024]{2,1,0:T(8,128)(2,1)}, s32[]{:T(128)}, bf16[64,1024]{1,0:T(8,128)(2,1)S(1)}, bf16[4,64,1024]{2,1,0:T(8,128)(2,1)}, /*index=5*/bf16[8,128]{1,0:T(8,128)(2,1)S(1)}, bf16[1024]{0:T(1024)(128)(2,1)S(1)}, ...), branch_computations={%region_6.6_spmd, %region_7.9_spmd} | conditional | flops 1698694144 | bytes 36853008 | solution.py:338
  548.2 5.1 convolution_compare_fusion
  553.2 11.1 %fusion.30 = (f32[64]{0:T(128)S(1)}, f32[64,1024]{1,0:T(8,128)S(1)}) fusion(f32[8,8,8,128]{3,2,1,0:T(8,128)S(1)} %bitcast.123, f32[1024]{0:T(1024)S(1)} %convert_element_type.73, bf16[1024,4096]{1,0:T(8,128)(2,1)} %get-tuple-element.534, pred[64,4096]{1,0:T(32,128)(4,1)S(1)} %convolution_compare_fusion, bf16[4096,1024]{1,0:T(8,128)(2,1)} %get-tuple-element.535, ...), kind=kOutput, calls=%fused_computation.38 | convolution fusion | flops 1074528256 | bytes 17831168 | tf_op jit(solution)/shard_map/while/body/eval_jaxpr/cond/branch_1_fun/dot_general | solution.py:243
  571.3 2.7 collective-permute-done.1
  574.1 21.1 %collective-permute-start.1 = (bf16[64,1024]{1,0:T(8,128)(2,1)S(1)}, bf16[64,1024]{1,0:T(8,128)(2,1)S(1)}, u32[]{:S(2)}, u32[]{:S(2)}) collective-permute-start(bf16[64,1024]{1,0:T(8,128)(2,1)S(1)} %get-tuple-element.834), channel_id=1, source_target_pairs={{16,0},{32,16},{48,32},{64,48},{80,64},{96,80},{112,96},{17,1},{33... | collective-permute-start | bytes 393224 | tf_op jit(solution)/shard_map/while/body/eval_jaxpr/ppermute | solution.py:207
  597.7 54.9 %all-reduce.2.cloned.1.call-done = bf16[256,1024]{1,0:T(8,128)(2,1)} async-done(((bf16[256,1024]{1,0:T(8,128)(2,1)}), bf16[256,1024]{1,0:T(8,128)(2,1)}) %all-reduce.2.cloned.1.call-update) | async-done | bytes 524304 | tf_op jit(solution)/shard_map/psum | solution.py:212
  654.1 10.0 %expand.1 = bf16[16384,128]{1,0:T(8,128)(2,1)} custom-call(bf16[64,256,256]{2,1,0:T(8,128)(2,1)} %lookup_matrix.1.mat, bf16[256,128]{1,0:T(8,128)(2,1)} %reshape.87.grad, bf16[16384,128]{1,0:T(8,128)(2,1)} %bitcast.16.rows), custom_call_target="tpu_custom_call" | custom-call | tf_op jit(solution)/shard_map/expand/pallas_call | solution.py:186
  664.1 10.0 %all-to-all-start.1 = ((bf16[128,128,128]{2,1,0:T(8,128)(2,1)}), bf16[128,128,128]{2,1,0:T(8,128)(2,1)}, u32[]{:S(2)}, u32[]{:S(2)}) async-start(bf16[128,128,128]{2,1,0:T(8,128)(2,1)} %bitcast.131), calls=%async_computation.1 | async-start | bytes 8388608 | tf_op jit(solution)/shard_map/all_to_all | solution.py:356
  674.7 51.4 %all-to-all-done.1 = bf16[128,128,128]{2,1,0:T(8,128)(2,1)} async-done(((bf16[128,128,128]{2,1,0:T(8,128)(2,1)}), bf16[128,128,128]{2,1,0:T(8,128)(2,1)}, u32[]{:S(2)}, u32[]{:S(2)}) %all-to-all-start.1) | async-done | bytes 4194336 | tf_op jit(solution)/shard_map/all_to_all | solution.py:356
  726.1 27.7 %scatter_rows.1 = f32[4096,128]{1,0:T(8,128)} custom-call(s32[16384]{0:T(1024)} %fusion.40.idx, bf16[16384,128]{1,0:T(8,128)(2,1)} %bitcast.23.val), custom_call_target="tpu_custom_call" | custom-call | tf_op jit(solution)/shard_map/scatter_rows/pallas_call | solution.py:81
  (172 shorter events, 97.6 us)
Async XLA Ops:
  6.5 30.6 %copy-start.1 = (s32[1,32,512]{2,1,0:T(8,128)S(1)}, s32[1,32,512]{2,1,0:T(8,128)}, u32[]{:S(2)}) copy-start(s32[1,32,512]{2,1,0:T(8,128)} %param.25) | copy-start | bytes 196612
  6.5 31.2 %copy-start.3 = (bf16[1,1024]{1,0:T(2,128)(2,1)S(1)}, bf16[1,1024]{1,0:T(2,128)(2,1)}, u32[]{:S(2)}) copy-start(bf16[1,1024]{1,0:T(2,128)(2,1)} %param.21) | copy-start | bytes 6148
  25.1 64.0 %all-to-all-start = ((bf16[128,128,128]{2,1,0:T(8,128)(2,1)}), bf16[128,128,128]{2,1,0:T(8,128)(2,1)}, u32[]{:S(2)}, u32[]{:S(2)}) async-start(bf16[128,128,128]{2,1,0:T(8,128)(2,1)} %bitcast.130), calls=%async_computation | async-start | bytes 8388608 | tf_op jit(solution)/shard_map/all_to_all | solution.py:286
  37.0 615.5 %all-reduce.2.cloned.1.call-start = ((), (), s32[]{:S(2)}) async-start(), calls=%async_computation.2 | async-start | bytes 1048576 | tf_op jit(solution)/shard_map/psum | solution.py:212
  51.8 61.2 %copy-start.2 = (bf16[1,8,128]{2,1,0:T(8,128)(2,1)S(1)}, bf16[1,8,128]{2,1,0:T(8,128)(2,1)}, u32[]{:S(2)}) copy-start(bf16[1,8,128]{2,1,0:T(8,128)(2,1)} %param.20) | copy-start | bytes 6148
  114.7 13.1 %collective-permute-start = (bf16[64,1024]{1,0:T(8,128)(2,1)S(1)}, bf16[64,1024]{1,0:T(8,128)(2,1)S(1)}, u32[]{:S(2)}, u32[]{:S(2)}) collective-permute-start(bf16[64,1024]{1,0:T(8,128)(2,1)S(1)} %get-tuple-element.833), channel_id=1, source_target_pairs={{0,16},{16,32},{32,48},{48,64},{64,80},{80,96},{96,112},{1,17},{17... | collective-permute-start | bytes 393224 | tf_op jit(solution)/shard_map/while/body/eval_jaxpr/ppermute | solution.py:207
  140.3 3.9 collective-permute-start
  156.7 6.3 collective-permute-start
  175.5 6.3 collective-permute-start
  194.2 6.3 collective-permute-start
  202.2 17.1 %collective-permute-start = (bf16[64,1024]{1,0:T(8,128)(2,1)S(1)}, bf16[64,1024]{1,0:T(8,128)(2,1)S(1)}, u32[]{:S(2)}, u32[]{:S(2)}) collective-permute-start(bf16[64,1024]{1,0:T(8,128)(2,1)S(1)} %get-tuple-element.833), channel_id=1, source_target_pairs={{0,16},{16,32},{32,48},{48,64},{64,80},{80,96},{96,112},{1,17},{17... | collective-permute-start | bytes 393224 | tf_op jit(solution)/shard_map/while/body/eval_jaxpr/ppermute | solution.py:207
  221.0 6.3 collective-permute-start
  228.9 10.7 %collective-permute-start = (bf16[64,1024]{1,0:T(8,128)(2,1)S(1)}, bf16[64,1024]{1,0:T(8,128)(2,1)S(1)}, u32[]{:S(2)}, u32[]{:S(2)}) collective-permute-start(bf16[64,1024]{1,0:T(8,128)(2,1)S(1)} %get-tuple-element.833), channel_id=1, source_target_pairs={{0,16},{16,32},{32,48},{48,64},{64,80},{80,96},{96,112},{1,17},{17... | collective-permute-start | bytes 393224 | tf_op jit(solution)/shard_map/while/body/eval_jaxpr/ppermute | solution.py:207
  241.3 6.3 collective-permute-start
  249.2 14.7 %collective-permute-start = (bf16[64,1024]{1,0:T(8,128)(2,1)S(1)}, bf16[64,1024]{1,0:T(8,128)(2,1)S(1)}, u32[]{:S(2)}, u32[]{:S(2)}) collective-permute-start(bf16[64,1024]{1,0:T(8,128)(2,1)S(1)} %get-tuple-element.833), channel_id=1, source_target_pairs={{0,16},{16,32},{32,48},{48,64},{64,80},{80,96},{96,112},{1,17},{17... | collective-permute-start | bytes 393224 | tf_op jit(solution)/shard_map/while/body/eval_jaxpr/ppermute | solution.py:207
  265.6 6.3 collective-permute-start
  273.0 11.4 %collective-permute-start.1 = (bf16[64,1024]{1,0:T(8,128)(2,1)S(1)}, bf16[64,1024]{1,0:T(8,128)(2,1)S(1)}, u32[]{:S(2)}, u32[]{:S(2)}) collective-permute-start(bf16[64,1024]{1,0:T(8,128)(2,1)S(1)} %get-tuple-element.834), channel_id=1, source_target_pairs={{16,0},{32,16},{48,32},{64,48},{80,64},{96,80},{112,96},{17,1},{33... | collective-permute-start | bytes 393224 | tf_op jit(solution)/shard_map/while/body/eval_jaxpr/ppermute | solution.py:207
  284.4 6.3 collective-permute-start.1
  290.8 15.3 %collective-permute-start.1 = (bf16[64,1024]{1,0:T(8,128)(2,1)S(1)}, bf16[64,1024]{1,0:T(8,128)(2,1)S(1)}, u32[]{:S(2)}, u32[]{:S(2)}) collective-permute-start(bf16[64,1024]{1,0:T(8,128)(2,1)S(1)} %get-tuple-element.834), channel_id=1, source_target_pairs={{16,0},{32,16},{48,32},{64,48},{80,64},{96,80},{112,96},{17,1},{33... | collective-permute-start | bytes 393224 | tf_op jit(solution)/shard_map/while/body/eval_jaxpr/ppermute | solution.py:207
  306.1 6.3 collective-permute-start.1
  312.4 11.3 %collective-permute-start.1 = (bf16[64,1024]{1,0:T(8,128)(2,1)S(1)}, bf16[64,1024]{1,0:T(8,128)(2,1)S(1)}, u32[]{:S(2)}, u32[]{:S(2)}) collective-permute-start(bf16[64,1024]{1,0:T(8,128)(2,1)S(1)} %get-tuple-element.834), channel_id=1, source_target_pairs={{16,0},{32,16},{48,32},{64,48},{80,64},{96,80},{112,96},{17,1},{33... | collective-permute-start | bytes 393224 | tf_op jit(solution)/shard_map/while/body/eval_jaxpr/ppermute | solution.py:207
  323.7 136.1 %collective-permute-start.1 = (bf16[64,1024]{1,0:T(8,128)(2,1)S(1)}, bf16[64,1024]{1,0:T(8,128)(2,1)S(1)}, u32[]{:S(2)}, u32[]{:S(2)}) collective-permute-start(bf16[64,1024]{1,0:T(8,128)(2,1)S(1)} %get-tuple-element.834), channel_id=1, source_target_pairs={{16,0},{32,16},{48,32},{64,48},{80,64},{96,80},{112,96},{17,1},{33... | collective-permute-start | bytes 393224 | tf_op jit(solution)/shard_map/while/body/eval_jaxpr/ppermute | solution.py:207
  482.0 6.3 collective-permute-start.1
  510.6 6.3 collective-permute-start.1
  539.2 6.3 collective-permute-start.1
  567.7 6.3 collective-permute-start.1
  574.1 22.8 %collective-permute-start.1 = (bf16[64,1024]{1,0:T(8,128)(2,1)S(1)}, bf16[64,1024]{1,0:T(8,128)(2,1)S(1)}, u32[]{:S(2)}, u32[]{:S(2)}) collective-permute-start(bf16[64,1024]{1,0:T(8,128)(2,1)S(1)} %get-tuple-element.834), channel_id=1, source_target_pairs={{16,0},{32,16},{48,32},{64,48},{80,64},{96,80},{112,96},{17,1},{33... | collective-permute-start | bytes 393224 | tf_op jit(solution)/shard_map/while/body/eval_jaxpr/ppermute | solution.py:207
  664.1 10.0 %copy-start = (s32[1,128,128]{2,1,0:T(8,128)S(1)}, s32[1,128,128]{2,1,0:T(8,128)}, u32[]{:S(2)}) copy-start(s32[1,128,128]{2,1,0:T(8,128)} %param.26) | copy-start | bytes 196612
  664.1 10.0 %copy-start.4 = (s32[1,128]{1,0:T(1,128)S(1)}, s32[1,128]{1,0:T(1,128)}, u32[]{:S(2)}) copy-start(s32[1,128]{1,0:T(1,128)} %param.27) | copy-start | bytes 1540
  664.1 62.0 %all-to-all-start.1 = ((bf16[128,128,128]{2,1,0:T(8,128)(2,1)}), bf16[128,128,128]{2,1,0:T(8,128)(2,1)}, u32[]{:S(2)}, u32[]{:S(2)}) async-start(bf16[128,128,128]{2,1,0:T(8,128)(2,1)} %bitcast.131), calls=%async_computation.1 | async-start | bytes 8388608 | tf_op jit(solution)/shard_map/all_to_all | solution.py:356
Sparse Core Ops, SparseCore 0:
  597.8 54.7 all-reduce.1

commit v2 on v1

--- a/solution.py
+++ b/solution.py
@@ -9,6 +9,9 @@
 F32 = jnp.float32
 NT = (((1,), (1,)), ((), ()))
 TN = (((0,), (0,)), ((), ()))
+EPSILON = 1e-05
+DECAY_WEIGHT = 0.5
+MICRO_ROWS = 64
 
 
 def gather_rows(table, ids):
@@ -197,70 +200,288 @@
     )(matrix, grads, fetched)
 
 
-EPSILON = 1e-05
-DECAY_WEIGHT = 0.5
-
-
-def shifted(value, axis, steps):
-    count = lax.axis_size(axis)
-    first, last = (max(0, -steps), min(count, count - steps))
-    return lax.ppermute(value, axis, [(source, source + steps) for source in range(first, last)])
-
-
-def broadcast(block, axis, holder):
-    block = jnp.where(lax.axis_index(axis) == holder, block, jnp.zeros_like(block))
-    return lax.psum(block, axis)
-
-
-def fm_forward(inputs, proj, gain, w_up, w_down):
-    batch_rows = inputs.shape[0]
-    embed_count = proj.shape[0]
-    features = inputs.reshape(batch_rows, embed_count, -1)
-    mixed_cols = jnp.einsum(
-        "bke,kr->bre", features, proj, preferred_element_type=jnp.float32
-    ).astype(jnp.bfloat16)
-    interact = jnp.einsum(
-        "bke,bre->bkr", features, mixed_cols, preferred_element_type=jnp.float32
-    ).reshape(batch_rows, -1)
-    inv_scale = lax.rsqrt(jnp.mean(interact * interact, axis=1, keepdims=True) + EPSILON)
-    normed = (interact * inv_scale * gain.astype(jnp.float32)).astype(jnp.bfloat16)
-    before = jnp.dot(normed, w_up, preferred_element_type=jnp.float32)
-    hidden = jnp.maximum(before, 0.0).astype(jnp.bfloat16)
-    output = inputs.astype(jnp.float32) + jnp.dot(
-        hidden, w_down, preferred_element_type=jnp.float32
-    )
-    return (output.astype(jnp.bfloat16), (features, mixed_cols, interact, inv_scale, before))
-
-
-def fm_backward(inputs, grad_out, proj, gain, w_up, w_down):
-    batch_rows = inputs.shape[0]
-    embed_count = proj.shape[0]
-    unused, saved = fm_forward(inputs, proj, gain, w_up, w_down)
-    features, mixed_cols, interact, inv_scale, before = saved
-    last_dims = (((1,), (1,)), ((), ()))
-    g_hidden = lax.dot_general(grad_out, w_down, last_dims, preferred_element_type=jnp.float32)
-    g_before = jnp.where(before > 0.0, g_hidden, 0.0).astype(jnp.bfloat16)
-    g_normed = lax.dot_general(g_before, w_up, last_dims, preferred_element_type=jnp.float32)
-    weighted = g_normed * gain.astype(jnp.float32)
-    g_interact = inv_scale * (
-        weighted
-        - interact * inv_scale * inv_scale * jnp.mean(weighted * interact, axis=1, keepdims=True)
-    )
-    g_interact = g_interact.astype(jnp.bfloat16).reshape(batch_rows, embed_count, -1)
-    g_features = jnp.einsum(
-        "bkr,bre->bke", g_interact, mixed_cols, preferred_element_type=jnp.float32
-    )
-    g_mixed = jnp.einsum(
-        "bkr,bke->bre", g_interact, features, preferred_element_type=jnp.float32
-    ).astype(jnp.bfloat16)
-    g_features = g_features + jnp.einsum(
-        "bre,kr->bke", g_mixed, proj, preferred_element_type=jnp.float32
-    )
-    return (grad_out.astype(jnp.float32) + g_features.reshape(batch_rows, -1)).astype(jnp.bfloat16)
-
-
-def pass_on(payload, offset):
-    return shifted(payload, "section", offset)
+def layer_forward(a_ref, proj, gain, w_up, w_down, keep, out_ref, last):
+    interact, inv_keep, hidden, wide, unit = keep
+    rows = a_ref.shape[0]
+    embeds, width = proj.shape
+    model = gain.shape[1]
+    inner = w_up.shape[1]
+    wide[...] = a_ref[...].astype(F32)
+
+    def block(i, carry):
+        at = pl.ds(pl.multiple_of(i * 8, 8), 8)
+        p = [jnp.broadcast_to(proj[k : k + 1, :], (8, width)) for k in range(embeds)]
+        a = [wide[at, k * width : (k + 1) * width] for k in range(embeds)]
+        gram = {}
+        for k in range(embeds):
+            for q in range(k, embeds):
+                gram[k, q] = gram[q, k] = jnp.sum(a[k] * a[q], axis=1, keepdims=True)
+        square = None
+        mixed = []
+        for k in range(embeds):
+            total = gram[k, 0] * p[0]
+            for q in range(1, embeds):
+                total += gram[k, q] * p[q]
+            mixed.append(total)
+            interact[at, k * width : (k + 1) * width] = total
+            square = total * total if square is None else square + total * total
+        inv = lax.rsqrt(jnp.sum(square, axis=1, keepdims=True) * (1.0 / model) + EPSILON)
+        inv_keep[at, :] = jnp.broadcast_to(inv, (8, width))
+        for k in range(embeds):
+            cols = slice(k * width, (k + 1) * width)
+            unit[at, cols] = mixed[k] * inv * gain[:, cols]
+        return carry
+
+    lax.fori_loop(0, rows // 8, block, 0, unroll=2)
+    normed = unit[...].astype(BF)
+    tile = min(512, inner)
+    for n in range(0, inner, tile):
+        before = jnp.dot(normed, w_up[:, n : n + tile], preferred_element_type=F32)
+        hidden[:, n : n + tile] = jnp.maximum(before, 0.0).astype(BF)
+
+    @pl.when(jnp.logical_not(last))
+    def _():
+        tile = 256
+        for n in range(0, model, tile):
+            got = jnp.dot(hidden[...], w_down[:, n : n + tile], preferred_element_type=F32)
+            out_ref[:, n : n + tile] = (got + a_ref[:, n : n + tile].astype(F32)).astype(BF)
+
+
+def layer_backward(a_ref, g_ref, proj, gain, up_t, down_t, keep, gated, out_ref):
+    interact, inv_keep, hidden, wide, unit = keep
+    rows = a_ref.shape[0]
+    embeds, width = proj.shape
+    model = gain.shape[1]
+    inner = down_t.shape[1]
+    g = g_ref[...]
+    tile = min(512, inner)
+    for n in range(0, inner, tile):
+        up = jnp.dot(g, down_t[:, n : n + tile], preferred_element_type=F32)
+        gated[:, n : n + tile] = jnp.where(hidden[:, n : n + tile].astype(F32) > 0.0, up, 0.0).astype(BF)
+    tile = 256
+    for n in range(0, model, tile):
+        unit[:, n : n + tile] = jnp.dot(gated[...], up_t[:, n : n + tile], preferred_element_type=F32)
+    wide[...] = a_ref[...].astype(F32)
+
+    def block(i, carry):
+        at = pl.ds(pl.multiple_of(i * 8, 8), 8)
+        cols = [slice(k * width, (k + 1) * width) for k in range(embeds)]
+        weighted = [unit[at, cols[k]] * gain[:, cols[k]] for k in range(embeds)]
+        mixed = [interact[at, cols[k]] for k in range(embeds)]
+        cross = weighted[0] * mixed[0]
+        for k in range(1, embeds):
+            cross += weighted[k] * mixed[k]
+        mean = jnp.sum(cross, axis=1, keepdims=True) * (1.0 / model)
+        inv = inv_keep[at, :]
+        slope = inv * inv * mean
+        grad = [inv * (weighted[k] - mixed[k] * slope) for k in range(embeds)]
+        p = [jnp.broadcast_to(proj[k : k + 1, :], (8, width)) for k in range(embeds)]
+        pair = {}
+        for k in range(embeds):
+            for q in range(k, embeds):
+                term = grad[k] * p[q] + grad[q] * p[k]
+                pair[k, q] = pair[q, k] = jnp.sum(term, axis=1, keepdims=True)
+        a = [wide[at, cols[k]] for k in range(embeds)]
+        for k in range(embeds):
+            total = pair[k, 0] * a[0]
+            for q in range(1, embeds):
+                total += pair[k, q] * a[q]
+            unit[at, cols[k]] = total
+        return carry
+
+    lax.fori_loop(0, rows // 8, block, 0, unroll=2)
+    out_ref[...] = (unit[...] + g_ref[...].astype(F32)).astype(BF)
+
+
+def layer_pipeline(shares, top, proj, gain, w_up, w_down, up_t, down_t, stages, rows):
+    look, model = shares.shape
+    micro = top.shape[0] // rows
+    per = rows // look
+    inner = w_up.shape[1]
+    width = proj.shape[1]
+    copy_to = pltpu.make_async_remote_copy
+    copy_here = pltpu.make_async_copy
+
+    def body(
+        share_in, top_in, proj_ref, gain_ref, up_in, down_in, up_t_in, down_t_in, out,
+        acts, cots, acts_out, cots_out, share, up_v, down_v, up_tv, down_tv,
+        interact, inv_keep, hidden, wide, unit, gated,
+        wsem, tsem, fsend, frecv, gsend, grecv, isend, irecv, osend, orecv, lsem,
+    ):
+        me = lax.axis_index("section")
+        first, last = me == 0, me == stages - 1
+        loads = [
+            copy_here(src, dst, wsem.at[i])
+            for i, (src, dst) in enumerate(
+                [(up_in, up_v), (down_in, down_v), (down_t_in, down_tv), (up_t_in, up_tv)]
+            )
+        ]
+        loads[0].start()
+        loads[1].start()
+        tops = [copy_here(top_in.at[pl.ds(m * rows, rows), :], cots.at[m], tsem.at[m]) for m in range(micro)]
+
+        @pl.when(last)
+        def _():
+            for m in range(micro):
+                tops[m].start()
+
+        barrier = pltpu.get_barrier_semaphore()
+        for d in range(1, stages):
+            pl.semaphore_signal(
+                barrier, inc=1, device_id={"section": lax.rem(me + d, stages)},
+                device_id_type=pl.DeviceIdType.MESH,
+            )
+        pl.semaphore_wait(barrier, stages - 1)
+
+        def entry(section):
+            slot, off = section // per, lax.rem(section, per) * look
+            return copy_to(
+                src_ref=share_in, dst_ref=acts.at[slot, pl.ds(pl.multiple_of(off, look), look), :],
+                send_sem=isend, recv_sem=irecv.at[section],
+                device_id={"section": 0}, device_id_type=pl.DeviceIdType.MESH,
+            )
+
+        own = copy_here(share_in, acts.at[0, pl.ds(0, look), :], irecv.at[0])
+
+        @pl.when(first)
+        def _():
+            own.start()
+            own.wait()
+            for section in range(1, stages):
+                entry(jnp.int32(section)).wait_recv()
+
+        @pl.when(jnp.logical_not(first))
+        def _():
+            entry(me).start()
+
+        def onward(m):
+            return copy_to(
+                src_ref=acts_out.at[m], dst_ref=acts.at[m], send_sem=fsend.at[m], recv_sem=frecv.at[m],
+                device_id={"section": lax.rem(me + 1, stages)}, device_id_type=pl.DeviceIdType.MESH,
+            )
+
+        def back(m):
+            return copy_to(
+                src_ref=cots_out.at[m], dst_ref=cots.at[m], send_sem=gsend.at[m], recv_sem=grecv.at[m],
+                device_id={"section": lax.rem(me + stages - 1, stages)}, device_id_type=pl.DeviceIdType.MESH,
+            )
+
+        def leave(m, j, section):
+            return copy_to(
+                src_ref=cots_out.at[m, pl.ds(j * look, look), :], dst_ref=share,
+                send_sem=osend.at[section], recv_sem=orecv,
+                device_id={"section": section}, device_id_type=pl.DeviceIdType.MESH,
+            )
+
+        keep_own = copy_here(cots_out.at[0, pl.ds(0, look), :], share, lsem)
+        loads[0].wait()
+        loads[1].wait()
+        loads[2].start()
+        loads[3].start()
+
+        def step(i, carry):
+            ahead = jnp.where(last, lax.rem(i, 2) == 0, i < micro)
+            m = jnp.where(last, i // 2, lax.rem(i, micro))
+            keep = (interact.at[m], inv_keep.at[m], hidden.at[m], wide, unit)
+
+            @pl.when(ahead)
+            def _():
+                @pl.when(jnp.logical_not(first))
+                def _():
+                    onward(m).wait_recv()
+
+                layer_forward(acts.at[m], proj_ref, gain_ref, up_v, down_v, keep, acts_out.at[m], last)
+
+                @pl.when(jnp.logical_not(last))
+                def _():
+                    onward(m).start()
+
+            @pl.when(jnp.logical_not(ahead))
+            def _():
+                @pl.when(m == 0)
+                def _():
+                    loads[2].wait()
+                    loads[3].wait()
+
+                @pl.when(last)
+                def _():
+                    copy_here(top_in.at[pl.ds(pl.multiple_of(m * rows, rows), rows), :], cots.at[m], tsem.at[m]).wait()
+
+                @pl.when(jnp.logical_not(last))
+                def _():
+                    back(m).wait_recv()
+
+                layer_backward(
+                    acts.at[m], cots.at[m], proj_ref, gain_ref, up_tv, down_tv, keep, gated, cots_out.at[m]
+                )
+
+                @pl.when(jnp.logical_not(first))
+                def _():
+                    back(m).start()
+
+                @pl.when(first)
+                def _():
+                    for j in range(per):
+                        section = m * per + j
+                        if j == 0:
+                            @pl.when(section == 0)
+                            def _():
+                                keep_own.start()
+
+                            @pl.when(section > 0)
+                            def _():
+                                leave(m, j, section).start()
+                        else:
+                            leave(m, j, section).start()
+
+            return carry
+
+        lax.fori_loop(0, 2 * micro, step, 0)
+
+        @pl.when(first)
+        def _():
+            keep_own.wait()
+            for section in range(1, stages):
+                leave(section // per, section % per, jnp.int32(section)).wait_send()
+
+        @pl.when(jnp.logical_not(first))
+        def _():
+            leave(0, 0, jnp.int32(0)).wait_recv()
+            entry(me).wait_send()
+            for m in range(micro):
+                back(m).wait_send()
+
+        @pl.when(jnp.logical_not(last))
+        def _():
+            for m in range(micro):
+                onward(m).wait_send()
+
+        out[...] = share[...]
+
+    vmem = pl.BlockSpec(memory_space=pltpu.VMEM)
+    hbm = pl.BlockSpec(memory_space=pl.ANY)
+    dma = pltpu.SemaphoreType.DMA
+    block = (micro, rows, model)
+    return pl.pallas_call(
+        body,
+        in_specs=[vmem, hbm, vmem, vmem, hbm, hbm, hbm, hbm],
+        out_specs=vmem,
+        out_shape=jax.ShapeDtypeStruct((look, model), BF),
+        scratch_shapes=[
+            pltpu.VMEM(block, BF), pltpu.VMEM(block, BF), pltpu.VMEM(block, BF), pltpu.VMEM(block, BF),
+            pltpu.VMEM((look, model), BF),
+            pltpu.VMEM((model, inner), BF), pltpu.VMEM((inner, model), BF),
+            pltpu.VMEM((inner, model), BF), pltpu.VMEM((model, inner), BF),
+            pltpu.VMEM(block, F32), pltpu.VMEM((micro, rows, width), F32), pltpu.VMEM((micro, rows, inner), BF),
+            pltpu.VMEM((rows, model), F32), pltpu.VMEM((rows, model), F32), pltpu.VMEM((rows, inner), BF),
+            dma((4,)), dma((micro,)), dma((micro,)), dma((micro,)), dma((micro,)), dma((micro,)),
+            dma, dma((stages,)), dma((stages,)), dma, dma,
+        ],
+        compiler_params=pltpu.CompilerParams(
+            collective_id=0, has_side_effects=True, vmem_limit_bytes=60 << 20
+        ),
+        name="layer_pipeline",
+    )(shares, top, proj, gain, w_up, w_down, up_t, down_t)
 
 
 def per_device(
@@ -276,91 +497,36 @@
     row_counts,
 ):
     section_count = lax.axis_size("section")
-    shard_count = lax.axis_size("table")
-    my_section = lax.axis_index("section")
-    owners = section_count * shard_count
+    owners = section_count * lax.axis_size("table")
     cap = wanted_rows.shape[2]
-    embed_width = emb_table.shape[1]
+    rows_here, embed_width = emb_table.shape
     picked_rows = wanted_rows[0]
-    outgoing = gather_rows(emb_table, picked_rows.reshape(-1)).reshape(owners, cap, embed_width)
-    fetched = lax.all_to_all(
-        outgoing, ("section", "table"), split_axis=0, concat_axis=0, tiled=True
-    )
-    fetched = fetched.reshape(owners * cap, embed_width)
+
+    def exchange(rows):
+        rows = rows.reshape(owners, cap, embed_width)
+        rows = lax.all_to_all(rows, ("section", "table"), split_axis=0, concat_axis=0, tiled=True)
+        return rows.reshape(owners * cap, embed_width)
+
+    fetched = exchange(gather_rows(emb_table, picked_rows.reshape(-1)))
     lookup_slots = lookup_slot[0]
     look_dev = lookup_slots.shape[0]
     matrix = lookup_matrix(lookup_slots, lcb_weight, owners, cap)
-    compressed = compress(matrix, fetched).reshape(look_dev, -1)
-    leading = lax.all_gather(compressed, "section", axis=0, tiled=True)
-    micro_count = top_grad.shape[1]
-    batch_rows = top_grad.shape[2]
+    shares = compress(matrix, fetched).reshape(look_dev, -1)
     model_width = top_grad.shape[3]
-    leading = leading.reshape(micro_count, batch_rows, model_width)
-    weights = (fm_proj[0], norm_gain[0], w_up[0], w_down[0])
-    tick_count = micro_count + section_count - 1
-
-    def forward_tick(tick, state):
-        incoming, stash = state
-        micro_idx = tick - my_section
-        is_valid = (micro_idx >= 0) & (micro_idx < micro_count)
-        clipped = jnp.clip(micro_idx, 0, micro_count - 1)
-        inputs = jnp.where(
-            my_section == 0, lax.dynamic_index_in_dim(leading, clipped, 0, keepdims=False), incoming
-        )
-        outputs = lax.cond(
-            is_valid,
-            lambda value: fm_forward(value, *weights)[0],
-            lambda value: jnp.zeros_like(value),
-            inputs,
-        )
-        kept_rows = jnp.where(
-            is_valid, inputs, lax.dynamic_index_in_dim(stash, clipped, 0, keepdims=False)
-        )
-        stash = lax.dynamic_update_index_in_dim(stash, kept_rows, clipped, 0)
-        return (pass_on(outputs, 1), stash)
-
-    empty_rows = jnp.zeros((batch_rows, model_width), jnp.bfloat16)
-    empty_stash = jnp.zeros((micro_count, batch_rows, model_width), jnp.bfloat16)
-    unused, stash = lax.fori_loop(0, tick_count, forward_tick, (empty_rows, empty_stash))
-    grads_top = top_grad[0]
-
-    def backward_tick(tick, state):
-        incoming, lead_grad = state
-        micro_idx = tick - (section_count - 1 - my_section)
-        is_valid = (micro_idx >= 0) & (micro_idx < micro_count)
-        clipped = jnp.clip(micro_idx, 0, micro_count - 1)
-        given = jnp.where(
-            my_section == section_count - 1,
-            lax.dynamic_index_in_dim(grads_top, clipped, 0, keepdims=False),
-            incoming,
-        )
-        saved_rows = lax.dynamic_index_in_dim(stash, clipped, 0, keepdims=False)
-        result = lax.cond(
-            is_valid,
-            lambda pair: fm_backward(pair[0], pair[1], *weights),
-            lambda pair: jnp.zeros_like(pair[0]),
-            (saved_rows, given),
-        )
-        record = jnp.where(
-            is_valid & (my_section == 0),
-            result,
-            lax.dynamic_index_in_dim(lead_grad, clipped, 0, keepdims=False),
-        )
-        lead_grad = lax.dynamic_update_index_in_dim(lead_grad, record, clipped, 0)
-        return (pass_on(result, -1), lead_grad)
-
-    unused, lead_grad = lax.fori_loop(0, tick_count, backward_tick, (empty_rows, empty_stash))
-    whole_grad = broadcast(lead_grad, "section", 0).reshape(micro_count * batch_rows, model_width)
-    lead_share = lax.dynamic_slice_in_dim(whole_grad, my_section * look_dev, look_dev, 0)
+    lead_share = layer_pipeline(
+        shares,
+        top_grad.reshape(-1, model_width),
+        fm_proj[0].astype(F32),
+        norm_gain.astype(F32),
+        w_up[0],
+        w_down[0],
+        w_up[0].T,
+        w_down[0].T,
+        section_count,
+        MICRO_ROWS,
+    )
     slot_grad = expand(matrix, lead_share.reshape(-1, embed_width), fetched, DECAY_WEIGHT)
-    returned = lax.all_to_all(
-        slot_grad.reshape(owners, cap, embed_width),
-        ("section", "table"),
-        split_axis=0,
-        concat_axis=0,
-        tiled=True,
-    ).reshape(owners * cap, embed_width)
-    rows_here = emb_table.shape[0]
+    returned = exchange(slot_grad)
     live_slots = jnp.arange(cap)[None, :] < row_counts[0][:, None]
     targets = jnp.where(live_slots, picked_rows, rows_here).reshape(-1)
     return scatter_rows(returned, targets, rows_here)

time: 763 us -> 325 us (0.43)
  waiting for transfers between devices: 350 us -> 64.2 us
  Pallas kernels: 78.8 us -> 204 us
  matrix products: 124 us -> 0 us
  starting transfers between devices: 129 us -> 25.9 us
  other arithmetic: 21.7 us -> 1.89 us
  blocking collectives: 13.5 us -> 0 us
  between operations: 13.5 us -> 0.06 us
    ppermute x22 -> x0, waiting for transfers between devices: 207 us -> none  [shifted(): lax.ppermute(value, axis, [(source, source + steps) for source in range(f...]
    pallas_call x0 -> x1, Pallas kernels: none -> 125 us  [layer_pipeline(): pl.pallas_call(body, in_specs=[vmem, hbm, vmem, vmem, hbm, hbm, hbm, hbm]...]
    dot_general x32 -> x0, matrix products: 124 us -> none  [the longest x4 44.4 us: fm_backward(): lax.dot_general(g_before, w_up, last_dims, preferred_element_type=jnp.flo...]
    ppermute x22 -> x0, starting transfers between devices: 107 us -> none  [shifted(): lax.ppermute(value, axis, [(source, source + steps) for source in range(f...]
    psum x1 -> x0, waiting for transfers between devices: 54.9 us -> none  [broadcast(): return lax.psum(block, axis)]
    all_to_all x2, waiting for transfers between devices: 88.7 us -> 64.2 us  [exchange(): lax.all_to_all(rows, ('section', 'table'), split_axis=0, concat_axis=0, t...]
    unnamed x10 -> x12, local copies, waits for them, and re-layouts: 0.02 us -> 23.3 us
    dynamic_slice x23 -> x0, local copies, waits for them, and re-layouts: 21 us -> none  [the longest x11 10.1 us: backward_tick(): lax.dynamic_index_in_dim(lead_grad, clipped, 0, keepdims=False)]
  transfers between devices with their start and end apart: 25 -> 2, of which waited for: 24 -> 2; matrix products, arithmetic and copies ran while one was open for 3% -> 8% of each run, Pallas kernels for 2% -> 4%
where the time goes in v2:
time: 325 us; the launch traced here: 323 us
  Pallas kernels  204 us (63%)
  waiting for transfers between devices  64.2 us (20%)
  local copies, waits for them, and re-layouts  27 us (8%)
  starting transfers between devices  25.9 us (8%)
    pallas_call x1, Pallas kernels, layer_pipeline(): pl.pallas_call(body, in_specs=[vmem, hbm, vmem, vmem, hbm, hbm, hbm, hbm]...  125 us
    all_to_all x2, waiting for transfers between devices, exchange(): lax.all_to_all(rows, ('section', 'table'), split_axis=0, concat_axis=0, t...  64.2 us
    pallas_call x1, Pallas kernels, scatter_rows(): pl.pallas_call(body, grid=(count // block,), in_specs=[pl.BlockSpec(memor...  27.7 us
    all_to_all x2, starting transfers between devices, exchange(): lax.all_to_all(rows, ('section', 'table'), split_axis=0, concat_axis=0, t...  25.9 us
    unnamed x12, local copies, waits for them, and re-layouts  23.3 us
    pallas_call x1, Pallas kernels, gather_rows(): pl.pallas_call(body, grid=(count // block,), in_specs=[pl.BlockSpec(memor...  18.6 us
    pallas_call x1, Pallas kernels, lookup_matrix(): pl.pallas_call(body, grid=(samples // 2,), in_specs=[pl.BlockSpec((1, 2,...  14.1 us
    pallas_call x1, Pallas kernels, expand(): pl.pallas_call(body, grid=(pairs // step_pairs,), in_specs=[pl.BlockSpec(...  9.96 us
  transfers between devices with their start and end apart: 2, of which 2 were waited for; matrix products, arithmetic and copies ran while one was open for 8% of the time, Pallas kernels for 4%

profile of v2, /device:TPU:1, one launch (start us, length us, event | category | flops | bytes accessed | tf_op | source)
XLA Modules:
  0.0 323.2 jit_solution(12140268620759544785)
XLA Ops:
  0.0 0.0 copy-start.1
  0.0 18.6 %gather_rows.1 = bf16[16384,128]{1,0:T(8,128)(2,1)} custom-call(s32[16384]{0:T(1024)} %bitcast.30, bf16[4096,128]{1,0:T(8,128)(2,1)} %tab.1), custom_call_target="tpu_custom_call" | custom-call | tf_op jit(solution)/shard_map/gather_rows/pallas_call | solution.py:37
  18.6 11.9 %all-to-all-start = ((bf16[128,128,128]{2,1,0:T(8,128)(2,1)}), bf16[128,128,128]{2,1,0:T(8,128)(2,1)}, u32[]{:S(2)}, u32[]{:S(2)}) async-start(bf16[128,128,128]{2,1,0:T(8,128)(2,1)} %bitcast.27), calls=%async_computation | async-start | bytes 8388608 | tf_op jit(solution)/shard_map/all_to_all | solution.py:507
  30.5 0.0 copy-done.1
  30.5 0.7 reshape_squeeze.4.slot_ref
  31.2 11.9 %copy.11 = bf16[1,1024,4096]{1,2,0:T(8,128)(2,1)} copy(bf16[1,1024,4096]{2,1,0:T(8,128)(2,1)} %param.14) | data formatting | bytes 16777216 | tf_op args[4]
  43.1 0.0 copy-start.2
  43.1 0.0 copy-start.3
  43.1 11.4 %copy.12 = bf16[1,4096,1024]{1,2,0:T(8,128)(2,1)} copy(bf16[1,4096,1024]{2,1,0:T(8,128)(2,1)} %param.15) | data formatting | bytes 16777216 | tf_op args[5]
  54.5 0.0 copy-done.2
  54.5 0.6 convert_element_type.10.gain_ref
  55.1 0.0 copy-done.3
  55.1 0.6 bitcast_convert_fusion.proj_ref
  55.7 14.1 %lookup_matrix.1.mat = bf16[64,256,256]{2,1,0:T(8,128)(2,1)} custom-call(s32[16,2,512]{2,1,0:T(2,128)} %reshape_squeeze.4.slot_ref, bf16[8,512]{1,0:T(8,128)(2,1)} %lcb_ref.1), custom_call_target="tpu_custom_call" | custom-call | flops 4294967296 | bytes 16777216 | tf_op jit(solution)/shard_map/lookup_matrix/pallas_call | solution.py:129
  69.7 12.8 %all-to-all-done = bf16[128,128,128]{2,1,0:T(8,128)(2,1)} async-done(((bf16[128,128,128]{2,1,0:T(8,128)(2,1)}), bf16[128,128,128]{2,1,0:T(8,128)(2,1)}, u32[]{:S(2)}, u32[]{:S(2)}) %all-to-all-start) | async-done | bytes 4194336 | tf_op jit(solution)/shard_map/all_to_all | solution.py:507
  82.6 8.6 %compress.1 = bf16[256,128]{1,0:T(8,128)(2,1)} custom-call(bf16[64,256,256]{2,1,0:T(8,128)(2,1)} %lookup_matrix.1.mat, bf16[16384,128]{1,0:T(8,128)(2,1)} %bitcast.4.rows), custom_call_target="tpu_custom_call" | custom-call | tf_op jit(solution)/shard_map/compress/pallas_call | solution.py:164
  91.2 1.5 reshape.31.share_in
  92.7 125.4 %layer_pipeline.1 = bf16[32,1024]{1,0:T(8,128)(2,1)} custom-call(bf16[32,1024]{1,0:T(8,128)(2,1)} %reshape.31.share_in, bf16[256,1024]{1,0:T(8,128)(2,1)} %bitcast.29, f32[8,128]{1,0:T(8,128)} %bitcast_convert_fusion.proj_ref, f32[1,1024]{1,0:T(1,128)} %convert_element_type.10.gain_ref, bf16[1024,4096]{1,0:T(8,128)(2,1)} %bitcast.23, ...), custom_call_target="tpu_custom_call" | custom-call | tf_op jit(solution)/shard_map/layer_pipeline/pallas_call | solution.py:465
  218.1 1.5 reshape.33.grad
  219.6 10.0 %expand.1 = bf16[16384,128]{1,0:T(8,128)(2,1)} custom-call(bf16[64,256,256]{2,1,0:T(8,128)(2,1)} %lookup_matrix.1.mat, bf16[256,128]{1,0:T(8,128)(2,1)} %reshape.33.grad, bf16[16384,128]{1,0:T(8,128)(2,1)} %bitcast.4.rows), custom_call_target="tpu_custom_call" | custom-call | tf_op jit(solution)/shard_map/expand/pallas_call | solution.py:189
  229.5 0.0 copy-start
  229.5 0.0 copy-start.4
  229.6 13.9 %all-to-all-start.1 = ((bf16[128,128,128]{2,1,0:T(8,128)(2,1)}), bf16[128,128,128]{2,1,0:T(8,128)(2,1)}, u32[]{:S(2)}, u32[]{:S(2)}) async-start(bf16[128,128,128]{2,1,0:T(8,128)(2,1)} %bitcast.28), calls=%async_computation.1 | async-start | bytes 8388608 | tf_op jit(solution)/shard_map/all_to_all | solution.py:507
  243.5 0.0 copy-done
  243.5 0.0 copy-done.4
  243.5 0.7 fusion.1.idx
  244.2 51.4 %all-to-all-done.1 = bf16[128,128,128]{2,1,0:T(8,128)(2,1)} async-done(((bf16[128,128,128]{2,1,0:T(8,128)(2,1)}), bf16[128,128,128]{2,1,0:T(8,128)(2,1)}, u32[]{:S(2)}, u32[]{:S(2)}) %all-to-all-start.1) | async-done | bytes 4194336 | tf_op jit(solution)/shard_map/all_to_all | solution.py:507
  295.5 27.7 %scatter_rows.1 = f32[4096,128]{1,0:T(8,128)} custom-call(s32[16384]{0:T(1024)} %fusion.1.idx, bf16[16384,128]{1,0:T(8,128)(2,1)} %bitcast.14.val), custom_call_target="tpu_custom_call" | custom-call | tf_op jit(solution)/shard_map/scatter_rows/pallas_call | solution.py:84
Async XLA Ops:
  0.0 30.5 %copy-start.1 = (s32[1,32,512]{2,1,0:T(8,128)S(1)}, s32[1,32,512]{2,1,0:T(8,128)}, u32[]{:S(2)}) copy-start(s32[1,32,512]{2,1,0:T(8,128)} %param.17) | copy-start | bytes 196612
  18.6 64.0 %all-to-all-start = ((bf16[128,128,128]{2,1,0:T(8,128)(2,1)}), bf16[128,128,128]{2,1,0:T(8,128)(2,1)}, u32[]{:S(2)}, u32[]{:S(2)}) async-start(bf16[128,128,128]{2,1,0:T(8,128)(2,1)} %bitcast.27), calls=%async_computation | async-start | bytes 8388608 | tf_op jit(solution)/shard_map/all_to_all | solution.py:507
  43.1 11.4 %copy-start.2 = (bf16[1,1024]{1,0:T(2,128)(2,1)S(1)}, bf16[1,1024]{1,0:T(2,128)(2,1)}, u32[]{:S(2)}) copy-start(bf16[1,1024]{1,0:T(2,128)(2,1)} %param.13) | copy-start | bytes 6148
  43.1 12.0 %copy-start.3 = (bf16[1,8,128]{2,1,0:T(8,128)(2,1)S(1)}, bf16[1,8,128]{2,1,0:T(8,128)(2,1)}, u32[]{:S(2)}) copy-start(bf16[1,8,128]{2,1,0:T(8,128)(2,1)} %param.12) | copy-start | bytes 6148
  229.5 13.9 %copy-start = (s32[1,128,128]{2,1,0:T(8,128)S(1)}, s32[1,128,128]{2,1,0:T(8,128)}, u32[]{:S(2)}) copy-start(s32[1,128,128]{2,1,0:T(8,128)} %param.18) | copy-start | bytes 196612
  229.5 13.9 %copy-start.4 = (s32[1,128]{1,0:T(1,128)S(1)}, s32[1,128]{1,0:T(1,128)}, u32[]{:S(2)}) copy-start(s32[1,128]{1,0:T(1,128)} %param.19) | copy-start | bytes 1540
  229.6 66.0 %all-to-all-start.1 = ((bf16[128,128,128]{2,1,0:T(8,128)(2,1)}), bf16[128,128,128]{2,1,0:T(8,128)(2,1)}, u32[]{:S(2)}, u32[]{:S(2)}) async-start(bf16[128,128,128]{2,1,0:T(8,128)(2,1)} %bitcast.28), calls=%async_computation.1 | async-start | bytes 8388608 | tf_op jit(solution)/shard_map/all_to_all | solution.py:507

commit v3 on v2

v3 whole, which is shorter than its diff:
```python
import jax
import jax.numpy as jnp
from jax import lax
from jax.experimental import pallas as pl
from jax.experimental.pallas import tpu as pltpu
from jax.sharding import PartitionSpec as P

BF = jnp.bfloat16
F32 = jnp.float32
NT = (((1,), (1,)), ((), ()))
TN = (((0,), (0,)), ((), ()))
EPSILON = 1e-05
DECAY_WEIGHT = 0.5
MICRO_ROWS = 64


def gather_rows(table, ids):
    rows, width = table.shape
    count = ids.shape[0]
    block = 1024
    chunk = 128

    def body(idx, tab, out, wide, tmp):
        step = pl.program_id(0)

        @pl.when(step == 0)
        def _():
            wide[...] = tab[...].astype(F32)

        @pl.loop(0, block // chunk)
        def _(part):
            base = step * block + part * chunk
            for j in range(chunk):
                tmp[pl.ds(j, 1), :] = wide[pl.ds(idx[base + j], 1), :]
            out[pl.ds(pl.multiple_of(part * chunk, chunk), chunk), :] = tmp[...].astype(BF)

    return pl.pallas_call(
        body,
        grid=(count // block,),
        in_specs=[
            pl.BlockSpec(memory_space=pltpu.SMEM),
            pl.BlockSpec((rows, width), lambda i: (0, 0)),
        ],
        out_specs=pl.BlockSpec((block, width), lambda i: (i, 0)),
        out_shape=jax.ShapeDtypeStruct((count, width), BF),
        scratch_shapes=[pltpu.VMEM((rows, width), F32), pltpu.VMEM((chunk, width), F32)],
        cost_estimate=pl.CostEstimate(flops=count * width, bytes_accessed=8 << 20, transcendentals=0),
        name="gather_rows",
    )(ids, table)


def scatter_rows(values, ids, rows, before=None):
    count, width = values.shape
    extra = [] if before is None else [before]
    block = 1024
    group = 16

    def body(idx, val, *refs):
        out, acc, wide, sem = refs[-4:]
        step = pl.program_id(0)

        @pl.when(step == 0)
        def _():
            if before is None:
                acc[...] = jnp.zeros_like(acc)
            else:
                acc[pl.ds(rows, 8), :] = jnp.zeros((8, width), F32)
                start = pltpu.make_async_copy(refs[0], acc.at[pl.ds(0, rows), :], sem)
                start.start()
                start.wait()

        wide[...] = val[...].astype(F32)

        @pl.loop(0, block // (4 * group))
        def _(part):
            for sub in range(4):
                at = part * (4 * group) + sub * group
                base = step * block + at
                where = [idx[base + j] for j in range(group)]
                new = [
                    acc[pl.ds(where[j], 1), :] + wide[pl.ds(at + j, 1), :]
                    for j in range(group)
                ]
                for j in range(group):
                    acc[pl.ds(where[j], 1), :] = new[j]

        @pl.when(step == pl.num_programs(0) - 1)
        def _():
            copy = pltpu.make_async_copy(acc.at[pl.ds(0, rows), :], out, sem)
            copy.start()
            copy.wait()

    return pl.pallas_call(
        body,
        grid=(count // block,),
        in_specs=[
            pl.BlockSpec(memory_space=pltpu.SMEM),
            pl.BlockSpec((block, width), lambda i: (i, 0)),
        ] + [pl.BlockSpec(memory_space=pl.ANY)] * len(extra),
        out_specs=pl.BlockSpec(memory_space=pl.ANY),
        out_shape=jax.ShapeDtypeStruct((rows, width), F32),
        scratch_shapes=[
            pltpu.VMEM((rows + 8, width), F32),
            pltpu.VMEM((block, width), F32),
            pltpu.SemaphoreType.DMA,
        ],
        cost_estimate=pl.CostEstimate(flops=count * width, bytes_accessed=16 << 20, transcendentals=0),
        name="scatter_rows",
    )(ids, values, *extra)


def lookup_matrix(slots, lcb, owners, cap):
    samples, features = slots.shape
    embeds = lcb.shape[0]
    shift = cap.bit_length() - 1
    half = cap // 2
    pairs = owners // 2

    def body(slot_ref, lcb_ref, out_ref):
        tiled = jnp.concatenate([lcb_ref[...].astype(F32)] * 2, axis=0).astype(BF)
        zero = jnp.zeros((), BF)
        lane = lax.broadcasted_iota(jnp.int32, (2 * cap, features), 0)
        row = (lax.broadcasted_iota(jnp.int32, (16, features), 0) // embeds).astype(F32).astype(BF)
        parts = []
        for h in range(2):
            slot = slot_ref[0, pl.ds(h, 1), :]
            pair = lax.shift_right_logical(slot, shift + 1)
            odd = lax.shift_right_logical(slot, shift) & 1
            col = slot & (cap - 1)
            place = lax.shift_right_logical(col, shift - 1) * cap + odd * half + (col & (half - 1))
            picks = jnp.where(lane == place, 1.0, 0.0).astype(BF)
            pair16 = jnp.broadcast_to(pair.astype(F32), (16, features)).astype(BF)
            rows = []
            for o in range(0, pairs, 2):
                rows.append(jnp.where(pair16 == row + jnp.asarray(float(o), BF), tiled, zero))
            spread = jnp.concatenate(rows, axis=0)
            got = lax.dot_general(spread, picks, NT, preferred_element_type=F32)
            parts.append(got.reshape(pairs, embeds, 2 * cap))
        out_ref[...] = jnp.concatenate(parts, axis=1).astype(BF)

    return pl.pallas_call(
        body,
        grid=(samples // 2,),
        in_specs=[
            pl.BlockSpec((1, 2, features), lambda i: (i, 0, 0)),
            pl.BlockSpec((embeds, features), lambda i: (0, 0)),
        ],
        out_specs=pl.BlockSpec((pairs, 2 * embeds, 2 * cap), lambda i: (0, i, 0)),
        out_shape=jax.ShapeDtypeStruct((pairs, samples * embeds, 2 * cap), BF),
        cost_estimate=pl.CostEstimate(
            flops=2 * samples * owners * embeds * cap * features, bytes_accessed=16 << 20, transcendentals=0
        ),
        name="lookup_matrix",
    )(slots.reshape(samples // 2, 2, features), lcb)


def compress(matrix, halves):
    pairs, outs, slots = matrix.shape
    width = halves[0].shape[1]
    part = slots // 2
    step_pairs = 8
    embeds = 8

    def half_sum(h, before):
        def body(mat, rows, *refs):
            out = refs[-1]
            step = pl.program_id(0)

            @pl.when(step == 0)
            def _():
                out[...] = jnp.zeros_like(out) if before is None else refs[0][...]

            total = out[...]
            for i in range(step_pairs):
                total += jnp.dot(mat[i], rows[pl.ds(i * part, part), :], preferred_element_type=F32)
            out[...] = total

        extra = [] if before is None else [before]
        return pl.pallas_call(
            body,
            grid=(pairs // step_pairs,),
            in_specs=[
                pl.BlockSpec((step_pairs, outs, part), lambda i: (i, 0, h)),
                pl.BlockSpec((step_pairs * part, width), lambda i: (i, 0)),
            ] + [pl.BlockSpec((outs, width), lambda i: (0, 0))] * len(extra),
            out_specs=pl.BlockSpec((outs, width), lambda i: (0, 0)),
            out_shape=jax.ShapeDtypeStruct((outs, width), F32),
            cost_estimate=pl.CostEstimate(flops=2 * outs * pairs * part * width, bytes_accessed=6 << 20, transcendentals=0),
            name="compress",
        )(matrix, halves[h], *extra)

    return half_sum(1, half_sum(0, None))


def expand(matrix, grads, rows, decay, h):
    pairs, outs, slots = matrix.shape
    width = rows.shape[1]
    part = slots // 2
    step_pairs = 8
    samples, model = grads.shape
    embeds = model // width

    def body(mat, grad, rows_ref, out, wide, tall):
        @pl.when(pl.program_id(0) == 0)
        def _():
            for k in range(embeds):
                wide[pl.ds(k, samples, stride=embeds), :] = grad[:, k * width : (k + 1) * width].astype(F32)
            tall[...] = wide[...].astype(BF)

        for i in range(step_pairs):
            at = pl.ds(i * part, part)
            got = lax.dot_general(mat[i], tall[...], TN, preferred_element_type=F32)
            out[at, :] = (got + decay * rows_ref[at, :].astype(F32)).astype(BF)

    return pl.pallas_call(
        body,
        grid=(pairs // step_pairs,),
        in_specs=[
            pl.BlockSpec((step_pairs, outs, part), lambda i: (i, 0, h)),
            pl.BlockSpec((samples, model), lambda i: (0, 0)),
            pl.BlockSpec((step_pairs * part, width), lambda i: (i, 0)),
        ],
        out_specs=pl.BlockSpec((step_pairs * part, width), lambda i: (i, 0)),
        out_shape=jax.ShapeDtypeStruct((pairs * part, width), BF),
        scratch_shapes=[pltpu.VMEM((outs, width), F32), pltpu.VMEM((outs, width), BF)],
        cost_estimate=pl.CostEstimate(flops=2 * outs * pairs * part * width, bytes_accessed=8 << 20, transcendentals=0),
        name="expand",
    )(matrix, grads, rows)


def layer_forward(a_ref, mix, gain, w_up, w_down, keep, out_ref, last, ready, send):
    interact, inv_keep, hidden, prod, normed = keep
    rows, model = a_ref.shape
    width = mix.shape[1]
    embeds = model // width
    inner = w_up.shape[1]
    cols = [slice(k * width, (k + 1) * width) for k in range(embeds)]
    for k in range(embeds):
        for q in range(k, embeds):
            both = a_ref[:, cols[k]] * a_ref[:, cols[q]]
            prod[k * rows : (k + 1) * rows, cols[q]] = both
            if q > k:
                prod[q * rows : (q + 1) * rows, cols[k]] = both
    interact[...] = jnp.dot(prod[...], mix[...], preferred_element_type=F32)
    square = None
    for k in range(embeds):
        part = interact[k * rows : (k + 1) * rows, :]
        square = part * part if square is None else square + part * part
    inv = lax.rsqrt(jnp.sum(square, axis=1, keepdims=True) * (1.0 / model) + EPSILON)
    inv_keep[...] = jnp.broadcast_to(inv, (rows, width))
    for k in range(embeds):
        part = interact[k * rows : (k + 1) * rows, :]
        normed[:, cols[k]] = (part * inv * gain[:, cols[k]]).astype(BF)
    tile = min(512, inner)
    for n in range(0, inner, tile):
        before = jnp.dot(normed[...], w_up[:, n : n + tile], preferred_element_type=F32)
        hidden[:, n : n + tile] = jnp.maximum(before, 0.0).astype(BF)
    ready()

    @pl.when(jnp.logical_not(last))
    def _():
        tile = 256
        for n in range(0, model, tile):
            got = jnp.dot(hidden[...], w_down[:, n : n + tile], preferred_element_type=F32)
            out_ref[:, n : n + tile] = (got + a_ref[:, n : n + tile].astype(F32)).astype(BF)
            send(n, tile)


def layer_backward(a_ref, g_ref, unmix, gain, up_t, down_t, keep, gated, unit, pulled, spread, out_ref, send):
    interact, inv_keep, hidden, prod, normed = keep
    rows, model = a_ref.shape
    width = unmix.shape[0]
    embeds = model // width
    inner = down_t.shape[1]
    cols = [slice(k * width, (k + 1) * width) for k in range(embeds)]
    tile = min(512, inner)
    for n in range(0, inner, tile):
        up = jnp.dot(g_ref[...], down_t[:, n : n + tile], preferred_element_type=F32)
        gated[:, n : n + tile] = jnp.where(hidden[:, n : n + tile].astype(F32) > 0.0, up, 0.0).astype(BF)
    tile = 256
    cross = None
    for n in range(0, model, tile):
        got = jnp.dot(gated[...], up_t[:, n : n + tile], preferred_element_type=F32)
        got = got * gain[:, n : n + tile]
        unit[:, n : n + tile] = got
        for k in range(n // width, (n + tile) // width):
            part = got[:, k * width - n : (k + 1) * width - n] * interact[k * rows : (k + 1) * rows, :]
            cross = part if cross is None else cross + part
    mean = jnp.sum(cross, axis=1, keepdims=True) * (1.0 / model)
    inv = inv_keep[...]
    slope = inv * inv * mean
    for k in range(embeds):
        part = inv * (unit[:, cols[k]] - interact[k * rows : (k + 1) * rows, :] * slope)
        pulled[k * rows : (k + 1) * rows, :] = part.astype(BF)
    for q in range(0, embeds, 2):
        both = slice(q * width, (q + 2) * width)
        spread[:, both] = jnp.dot(pulled[...], unmix[:, both], preferred_element_type=F32)
    part_rows = 16
    for b in range(0, rows, part_rows):
        here = pl.ds(b, part_rows)
        a = [a_ref[here, cols[k]].astype(F32) for k in range(embeds)]
        total = [g_ref[here, cols[k]].astype(F32) for k in range(embeds)]
        for k in range(embeds):
            for q in range(k, embeds):
                pair = spread[pl.ds(k * rows + b, part_rows), cols[q]] + spread[pl.ds(q * rows + b, part_rows), cols[k]]
                total[k] = total[k] + pair * a[q]
                if q > k:
                    total[q] = total[q] + pair * a[k]
        for k in range(embeds):
            out_ref[here, cols[k]] = total[k].astype(BF)
        if (b + part_rows) % 32 == 0:
            send((b + part_rows) // 32 - 1)


def layer_pipeline(shares, top, mix, unmix, gain, w_up, w_down, up_t, down_t, stages, rows):
    look, model = shares.shape
    micro = top.shape[0] // rows
    per = rows // look
    inner = w_up.shape[1]
    width = mix.shape[1]
    embeds = model // width
    chunks = model // 256
    copy_to = pltpu.make_async_remote_copy
    copy_here = pltpu.make_async_copy

    def body(
        share_in, top_in, mix_ref, unmix_ref, gain_ref, up_in, down_in, up_t_in, down_t_in, out,
        acts, cots, acts_out, cots_out, share, up_v, down_v, up_tv, down_tv,
        interact, inv_keep, hidden, prod, normed, gated, unit, pulled, spread,
        wsem, tsem, fsend, frecv, gsend, grecv, isend, irecv, osend, orecv, lsem,
    ):
        me = lax.axis_index("section")
        first, last = me == 0, me == stages - 1
        loads = [
            copy_here(src, dst, wsem.at[i])
            for i, (src, dst) in enumerate(
                [(up_in, up_v), (down_in, down_v), (down_t_in, down_tv), (up_t_in, up_tv)]
            )
        ]
        loads[0].start()
        loads[1].start()
        tops = [copy_here(top_in.at[pl.ds(m * rows, rows), :], cots.at[m], tsem.at[m]) for m in range(micro)]

        @pl.when(last)
        def _():
            for m in range(micro):
                tops[m].start()

        barrier = pltpu.get_barrier_semaphore()
        for d in range(1, stages):
            pl.semaphore_signal(
                barrier, inc=1, device_id={"section": lax.rem(me + d, stages)},
                device_id_type=pl.DeviceIdType.MESH,
            )
        pl.semaphore_wait(barrier, stages - 1)

        def entry(section):
            slot, off = section // per, lax.rem(section, per) * look
            return copy_to(
                src_ref=share_in, dst_ref=acts.at[slot, pl.ds(pl.multiple_of(off, look), look), :],
                send_sem=isend, recv_sem=irecv.at[section],
                device_id={"section": 0}, device_id_type=pl.DeviceIdType.MESH,
            )

        own = copy_here(share_in, acts.at[0, pl.ds(0, look), :], irecv.at[0])

        @pl.when(first)
        def _():
            own.start()
            own.wait()
            for section in range(1, stages):
                entry(jnp.int32(section)).wait_recv()

        @pl.when(jnp.logical_not(first))
        def _():
            entry(me).start()

        def onward(m, c):
            piece = pl.ds(c * 256, 256)
            return copy_to(
                src_ref=acts_out.at[m, :, piece], dst_ref=acts.at[m, :, piece],
                send_sem=fsend.at[m, c], recv_sem=frecv.at[m, c],
                device_id={"section": lax.rem(me + 1, stages)}, device_id_type=pl.DeviceIdType.MESH,
            )

        def back(m, j):
            piece = pl.ds(j * look, look)
            return copy_to(
                src_ref=cots_out.at[m, piece, :], dst_ref=cots.at[m, piece, :],
                send_sem=gsend.at[m, j], recv_sem=grecv.at[m, j],
                device_id={"section": lax.rem(me + stages - 1, stages)}, device_id_type=pl.DeviceIdType.MESH,
            )

        def leave(m, j, section):
            return copy_to(
                src_ref=cots_out.at[m, pl.ds(j * look, look), :], dst_ref=share,
                send_sem=osend.at[section], recv_sem=orecv,
                device_id={"section": section}, device_id_type=pl.DeviceIdType.MESH,
            )

        keep_own = copy_here(cots_out.at[0, pl.ds(0, look), :], share, lsem)
        loads[0].wait()

        def step(i, carry):
            ahead = jnp.where(last, lax.rem(i, 2) == 0, i < micro)
            m = jnp.where(last, i // 2, lax.rem(i, micro))
            keep = (interact.at[m], inv_keep.at[m], hidden.at[m], prod, normed)

            @pl.when(ahead)
            def _():
                @pl.when(jnp.logical_not(first))
                def _():
                    for c in range(chunks):
                        onward(m, c).wait_recv()

                def ready():
                    @pl.when(i == 0)
                    def _():
                        loads[1].wait()
                        loads[2].start()
                        loads[3].start()

                layer_forward(
                    acts.at[m], mix_ref, gain_ref, up_v, down_v, keep, acts_out.at[m], last, ready,
                    lambda n, tile: onward(m, n // 256).start(),
                )

            @pl.when(jnp.logical_not(ahead))
            def _():
                @pl.when(m == 0)
                def _():
                    loads[2].wait()
                    loads[3].wait()

                @pl.when(last)
                def _():
                    copy_here(top_in.at[pl.ds(pl.multiple_of(m * rows, rows), rows), :], cots.at[m], tsem.at[m]).wait()

                @pl.when(jnp.logical_not(last))
                def _():
                    for j in range(per):
                        back(m, j).wait_recv()

                def send(j):
                    @pl.when(jnp.logical_not(first))
                    def _():
                        back(m, j).start()

                    @pl.when(first)
                    def _():
                        section = m * per + j
                        if j == 0:
                            @pl.when(section == 0)
                            def _():
                                keep_own.start()

                            @pl.when(section > 0)
                            def _():
                                leave(m, j, section).start()
                        else:
                            leave(m, j, section).start()

                layer_backward(
                    acts.at[m], cots.at[m], unmix_ref, gain_ref, up_tv, down_tv, keep,
                    gated, unit, pulled, spread, cots_out.at[m], send,
                )

            return carry

        lax.fori_loop(0, 2 * micro, step, 0)

        @pl.when(first)
        def _():
            keep_own.wait()
            for section in range(1, stages):
                leave(section // per, section % per, jnp.int32(section)).wait_send()

        @pl.when(jnp.logical_not(first))
        def _():
            leave(0, 0, jnp.int32(0)).wait_recv()
            entry(me).wait_send()
            for m in range(micro):
                for j in range(per):
                    back(m, j).wait_send()

        @pl.when(jnp.logical_not(last))
        def _():
            for m in range(micro):
                for c in range(chunks):
                    onward(m, c).wait_send()

        out[...] = share[...]

    vmem = pl.BlockSpec(memory_space=pltpu.VMEM)
    hbm = pl.BlockSpec(memory_space=pl.ANY)
    dma = pltpu.SemaphoreType.DMA
    block = (micro, rows, model)
    tall = embeds * rows
    return pl.pallas_call(
        body,
        in_specs=[vmem, hbm, vmem, vmem, vmem, hbm, hbm, hbm, hbm],
        out_specs=vmem,
        out_shape=jax.ShapeDtypeStruct((look, model), BF),
        scratch_shapes=[
            pltpu.VMEM(block, BF), pltpu.VMEM(block, BF), pltpu.VMEM(block, BF), pltpu.VMEM(block, BF),
            pltpu.VMEM((look, model), BF),
            pltpu.VMEM((model, inner), BF), pltpu.VMEM((inner, model), BF),
            pltpu.VMEM((inner, model), BF), pltpu.VMEM((model, inner), BF),
            pltpu.VMEM((micro, tall, width), F32), pltpu.VMEM((micro, rows, width), F32),
            pltpu.VMEM((micro, rows, inner), BF),
            pltpu.VMEM((tall, model), BF), pltpu.VMEM((rows, model), BF), pltpu.VMEM((rows, inner), BF),
            pltpu.VMEM((rows, model), F32), pltpu.VMEM((tall, width), BF), pltpu.VMEM((tall, model), F32),
            dma((4,)), dma((micro,)), dma((micro, chunks)), dma((micro, chunks)),
            dma((micro, per)), dma((micro, per)),
            dma, dma((stages,)), dma((stages,)), dma, dma,
        ],
        compiler_params=pltpu.CompilerParams(
            collective_id=0, has_side_effects=True, vmem_limit_bytes=60 << 20
        ),
        name="layer_pipeline",
    )(shares, top, mix, unmix, gain, w_up, w_down, up_t, down_t)


def mixers(proj):
    embeds, width = proj.shape
    mix = jnp.broadcast_to(proj[:, None, :], (embeds, width, width)).reshape(embeds * width, width)
    unmix = jnp.broadcast_to(proj.T[:, :, None], (width, embeds, width)).reshape(width, embeds * width)
    return mix, unmix


def per_device(
    emb_table,
    lcb_weight,
    fm_proj,
    norm_gain,
    w_up,
    w_down,
    top_grad,
    lookup_slot,
    wanted_rows,
    row_counts,
):
    section_count = lax.axis_size("section")
    owners = section_count * lax.axis_size("table")
    cap = wanted_rows.shape[2]
    rows_here, embed_width = emb_table.shape
    picked_rows = wanted_rows[0]

    half = cap // 2

    def exchange(rows):
        rows = rows.reshape(owners, half, embed_width)
        rows = lax.all_to_all(rows, ("section", "table"), split_axis=0, concat_axis=0, tiled=True)
        return rows.reshape(owners * half, embed_width)

    def halves(ids):
        return [ids[:, h * half : (h + 1) * half].reshape(-1) for h in range(2)]

    fetched = [exchange(gather_rows(emb_table, ids)) for ids in halves(picked_rows)]
    lookup_slots = lookup_slot[0]
    look_dev = lookup_slots.shape[0]
    model_width = top_grad.shape[3]
    matrix = lookup_matrix(lookup_slots, lcb_weight, owners, cap)
    shares = compress(matrix, fetched).astype(BF).reshape(look_dev, -1)
    mix, unmix = mixers(fm_proj[0])
    lead_share = layer_pipeline(
        shares,
        top_grad.reshape(-1, model_width),
        mix,
        unmix,
        norm_gain.astype(F32),
        w_up[0],
        w_down[0],
        w_up[0].T,
        w_down[0].T,
        section_count,
        MICRO_ROWS,
    )
    live_slots = jnp.arange(cap)[None, :] < row_counts[0][:, None]
    targets = halves(jnp.where(live_slots, picked_rows, rows_here))
    returned = [exchange(expand(matrix, lead_share, fetched[h], DECAY_WEIGHT, h)) for h in range(2)]
    table_grad = scatter_rows(returned[0], targets[0], rows_here)
    return scatter_rows(returned[1], targets[1], rows_here, table_grad)


def solution(mesh):
    in_specs = (
        P(("section", "table"), None),
        P(),
        P("section", None, None),
        P("section", None),
        P("section", None, None),
        P("section", None, None),
        P("table", None, None, None),
        P("table", "section", None),
        P(("section", "table"), None, None),
        P(("section", "table"), None),
    )
    out_specs = P(("section", "table"), None)
    return jax.shard_map(
        per_device, mesh=mesh, in_specs=in_specs, out_specs=out_specs, check_vma=False
    )
```

time: 325 us -> 350 us (1.077)
  Pallas kernels: 204 us -> 220 us
  starting transfers between devices: 25.9 us -> 37.6 us
  waiting for transfers between devices: 64.2 us -> 54.1 us
  local copies, waits for them, and re-layouts: 27 us -> 34.8 us
    all_to_all x2 -> x4, starting transfers between devices: 25.9 us -> 37.6 us  [exchange(): lax.all_to_all(rows, ('section', 'table'), split_axis=0, concat_axis=0, t...]
    all_to_all x2 -> x4, waiting for transfers between devices: 64.2 us -> 54.1 us  [exchange(): lax.all_to_all(rows, ('section', 'table'), split_axis=0, concat_axis=0, t...]
    pallas_call x2 -> x3, Pallas kernels: 134 us -> 140 us  [the longest x1 127 us: layer_pipeline(): pl.pallas_call(body, in_specs=[vmem, hbm, vmem, vmem, vmem, hbm, hbm, hbm...]
    pallas_call x1 -> x2, Pallas kernels: 9.96 us -> 15.5 us  [expand(): pl.pallas_call(body, grid=(pairs // step_pairs,), in_specs=[pl.BlockSpec(...]
    unnamed x12 -> x19, local copies, waits for them, and re-layouts: 23.3 us -> 28.6 us
    pallas_call x1 -> x2, Pallas kernels: 27.7 us -> 31.4 us  [scatter_rows(): pl.pallas_call(body, grid=(count // block,), in_specs=[pl.BlockSpec(memor...]
    pallas_call x1 -> x2, Pallas kernels: 18.6 us -> 20.2 us  [gather_rows(): pl.pallas_call(body, grid=(count // block,), in_specs=[pl.BlockSpec(memor...]
  transfers between devices with their start and end apart: 2 -> 4, of which waited for: 2 -> 3; matrix products, arithmetic and copies ran while one was open for 8% -> 8% of each run, Pallas kernels for 4% -> 15%
where the time goes in v3:
time: 350 us; the launch traced here: 348 us
  Pallas kernels  220 us (63%)
  waiting for transfers between devices  54.1 us (15%)
  starting transfers between devices  37.6 us (11%)
  local copies, waits for them, and re-layouts  34.8 us (10%)
    pallas_call x1, Pallas kernels, layer_pipeline(): pl.pallas_call(body, in_specs=[vmem, hbm, vmem, vmem, vmem, hbm, hbm, hbm...  127 us
    all_to_all x4, waiting for transfers between devices, exchange(): lax.all_to_all(rows, ('section', 'table'), split_axis=0, concat_axis=0, t...  54.1 us
    all_to_all x4, starting transfers between devices, exchange(): lax.all_to_all(rows, ('section', 'table'), split_axis=0, concat_axis=0, t...  37.6 us
    pallas_call x2, Pallas kernels, scatter_rows(): pl.pallas_call(body, grid=(count // block,), in_specs=[pl.BlockSpec(memor...  31.4 us
    unnamed x19, local copies, waits for them, and re-layouts  28.6 us
    pallas_call x2, Pallas kernels, gather_rows(): pl.pallas_call(body, grid=(count // block,), in_specs=[pl.BlockSpec(memor...  20.2 us
    pallas_call x2, Pallas kernels, expand(): pl.pallas_call(body, grid=(pairs // step_pairs,), in_specs=[pl.BlockSpec(...  15.5 us
    pallas_call x2, Pallas kernels, half_sum(): pl.pallas_call(body, grid=(pairs // step_pairs,), in_specs=[pl.BlockSpec(...  13.5 us
  transfers between devices with their start and end apart: 4, of which 3 were waited for; matrix products, arithmetic and copies ran while one was open for 8% of the time, Pallas kernels for 15%

profile of v3, /device:TPU:1, one launch (start us, length us, event | category | flops | bytes accessed | tf_op | source)
XLA Modules:
  0.0 348.0 jit_solution(3450271797319932337)
XLA Ops:
  0.0 1.0 fusion.2
  1.0 0.7 reshape.55.idx
  1.7 10.1 %gather_rows.3 = bf16[8192,128]{1,0:T(8,128)(2,1)} custom-call(s32[8192]{0:T(1024)} %reshape.55.idx, bf16[4096,128]{1,0:T(8,128)(2,1)} %tab.3), custom_call_target="tpu_custom_call" | custom-call | flops 1048576 | bytes 8388608 | tf_op jit(solution)/shard_map/gather_rows/pallas_call | solution.py:37
  11.8 11.5 %all-to-all-start.1 = ((bf16[128,64,128]{2,1,0:T(8,128)(2,1)}), bf16[128,64,128]{2,1,0:T(8,128)(2,1)S(1)}, u32[]{:S(2)}, u32[]{:S(2)}) async-start(bf16[128,64,128]{2,1,0:T(8,128)(2,1)} %bitcast.37), calls=%async_computation.1 | async-start | bytes 4194304 | tf_op jit(solution)/shard_map/all_to_all | solution.py:553
  23.3 0.7 reshape.52.idx
  24.0 10.1 %gather_rows.2 = bf16[8192,128]{1,0:T(8,128)(2,1)} custom-call(s32[8192]{0:T(1024)} %reshape.52.idx, bf16[4096,128]{1,0:T(8,128)(2,1)} %tab.3), custom_call_target="tpu_custom_call" | custom-call | flops 1048576 | bytes 8388608 | tf_op jit(solution)/shard_map/gather_rows/pallas_call | solution.py:37
  34.1 18.9 %all-to-all-done.1 = bf16[128,64,128]{2,1,0:T(8,128)(2,1)S(1)} async-done(((bf16[128,64,128]{2,1,0:T(8,128)(2,1)}), bf16[128,64,128]{2,1,0:T(8,128)(2,1)S(1)}, u32[]{:S(2)}, u32[]{:S(2)}) %all-to-all-start.1) | async-done | bytes 2097184 | tf_op jit(solution)/shard_map/all_to_all | solution.py:553
  52.9 0.0 copy-start
  52.9 0.0 copy-start.4
  52.9 1.3 copy-done
  54.2 5.7 %all-to-all-start = ((bf16[128,64,128]{2,1,0:T(8,128)(2,1)}), bf16[128,64,128]{2,1,0:T(8,128)(2,1)}, u32[]{:S(2)}, u32[]{:S(2)}) async-start(bf16[128,64,128]{2,1,0:T(8,128)(2,1)} %bitcast.36), calls=%async_computation | async-start | bytes 4194304 | tf_op jit(solution)/shard_map/all_to_all | solution.py:553
  60.0 0.0 copy-done.4
  60.0 0.7 reshape_squeeze.3.slot_ref
  60.7 11.9 %copy.17 = bf16[1,1024,4096]{1,2,0:T(8,128)(2,1)} copy(bf16[1,1024,4096]{2,1,0:T(8,128)(2,1)} %param.14) | data formatting | bytes 16777216 | tf_op args[4]
  72.6 0.0 copy-start.5
  72.6 0.0 copy-start.6
  72.6 11.9 %copy.18 = bf16[1,4096,1024]{1,2,0:T(8,128)(2,1)} copy(bf16[1,4096,1024]{2,1,0:T(8,128)(2,1)} %param.15) | data formatting | bytes 16777216 | tf_op args[5]
  84.5 0.0 copy-done.5
  84.5 0.1 copy.16
  84.6 0.2 broadcast_in_dim.21
  84.9 0.8 copy.25
  85.6 0.0 copy-done.6
  85.6 0.6 convert_element_type.7.gain_ref
  86.2 12.2 %lookup_matrix.1.mat = bf16[64,256,256]{2,1,0:T(8,128)(2,1)} custom-call(s32[16,2,512]{2,1,0:T(2,128)} %reshape_squeeze.3.slot_ref, bf16[8,512]{1,0:T(8,128)(2,1)} %lcb_ref.1), custom_call_target="tpu_custom_call" | custom-call | flops 4294967296 | bytes 16777216 | tf_op jit(solution)/shard_map/lookup_matrix/pallas_call | solution.py:141
  98.5 6.7 %compress.2.refs_0_ = f32[256,128]{1,0:T(8,128)} custom-call(bf16[64,256,256]{2,1,0:T(8,128)(2,1)} %lookup_matrix.1.mat, bf16[8192,128]{1,0:T(8,128)(2,1)} %bitcast.32), custom_call_target="tpu_custom_call" | custom-call | flops 536870912 | bytes 6291456 | tf_op jit(solution)/shard_map/compress/pallas_call | solution.py:179
  105.2 0.0 all-to-all-done
  105.2 6.8 %compress.3 = f32[256,128]{1,0:T(8,128)} custom-call(bf16[64,256,256]{2,1,0:T(8,128)(2,1)} %lookup_matrix.1.mat, bf16[8192,128]{1,0:T(8,128)(2,1)} %bitcast.3.rows.rows_ref, f32[256,128]{1,0:T(8,128)} %compress.2.refs_0_), custom_call_target="tpu_custom_call" | custom-call | flops 536870912 | bytes 6291456 | tf_op jit(solution)/shard_map/compress/pallas_call | solution.py:179
  112.0 0.9 convert_element_type.6
  112.9 0.7 reshape.58.share_in
  113.6 0.7 broadcast_in_dim.20
  114.3 126.9 %layer_pipeline.1.grad = bf16[32,1024]{1,0:T(8,128)(2,1)} custom-call(bf16[32,1024]{1,0:T(8,128)(2,1)} %reshape.58.share_in, bf16[256,1024]{1,0:T(8,128)(2,1)} %bitcast.44, bf16[1024,128]{1,0:T(8,128)(2,1)} %bitcast.41, bf16[128,1024]{1,0:T(8,128)(2,1)} %bitcast.40, f32[1,1024]{1,0:T(1,128)} %convert_element_type.7.gain_ref, bf16[1024,4096]{1,0:T(8,128)(2,1)} %bitcast.28, ...), custom_call_target="tpu_custom_call" | custom-call | tf_op jit(solution)/shard_map/layer_pipeline/pallas_call | solution.py:499
  241.2 7.8 %expand.3 = bf16[8192,128]{1,0:T(8,128)(2,1)} custom-call(bf16[64,256,256]{2,1,0:T(8,128)(2,1)} %lookup_matrix.1.mat, bf16[32,1024]{1,0:T(8,128)(2,1)} %layer_pipeline.1.grad, bf16[8192,128]{1,0:T(8,128)(2,1)} %bitcast.33), custom_call_target="tpu_custom_call" | custom-call | flops 536870912 | bytes 8388608 | tf_op jit(solution)/shard_map/expand/pallas_call | solution.py:215
  249.1 15.7 %all-to-all-start.3 = ((bf16[128,64,128]{2,1,0:T(8,128)(2,1)}), bf16[128,64,128]{2,1,0:T(8,128)(2,1)S(1)}, u32[]{:S(2)}, u32[]{:S(2)}) async-start(bf16[128,64,128]{2,1,0:T(8,128)(2,1)} %bitcast.39), calls=%async_computation.3 | async-start | bytes 4194304 | tf_op jit(solution)/shard_map/all_to_all | solution.py:553
  264.8 7.7 %expand.2 = bf16[8192,128]{1,0:T(8,128)(2,1)} custom-call(bf16[64,256,256]{2,1,0:T(8,128)(2,1)} %lookup_matrix.1.mat, bf16[32,1024]{1,0:T(8,128)(2,1)} %layer_pipeline.1.grad, bf16[8192,128]{1,0:T(8,128)(2,1)} %bitcast.3.rows.rows_ref), custom_call_target="tpu_custom_call" | custom-call | flops 536870912 | bytes 8388608 | tf_op jit(solution)/shard_map/expand/pallas_call | solution.py:215
  272.5 21.9 %all-to-all-done.3 = bf16[128,64,128]{2,1,0:T(8,128)(2,1)S(1)} async-done(((bf16[128,64,128]{2,1,0:T(8,128)(2,1)}), bf16[128,64,128]{2,1,0:T(8,128)(2,1)S(1)}, u32[]{:S(2)}, u32[]{:S(2)}) %all-to-all-start.3) | async-done | bytes 2097184 | tf_op jit(solution)/shard_map/all_to_all | solution.py:553
  294.4 0.0 copy-start.2
  294.4 0.0 copy-start.3
  294.4 0.0 copy-start.7
  294.4 1.3 copy-done.2
  295.7 4.7 %all-to-all-start.2 = ((bf16[128,64,128]{2,1,0:T(8,128)(2,1)}), bf16[128,64,128]{2,1,0:T(8,128)(2,1)S(1)}, u32[]{:S(2)}, u32[]{:S(2)}) async-start(bf16[128,64,128]{2,1,0:T(8,128)(2,1)} %bitcast.38), calls=%async_computation.2 | async-start | bytes 4194304 | tf_op jit(solution)/shard_map/all_to_all | solution.py:553
  300.4 0.0 copy-done.3
  300.4 0.0 copy-done.7
  300.4 0.1 fusion
  300.5 0.1 fusion.1
  300.6 0.7 reshape.64.idx
  301.3 0.7 reshape.51.idx
  302.0 14.9 %scatter_rows.2.refs_0_ = f32[4096,128]{1,0:T(8,128)} custom-call(s32[8192]{0:T(1024)} %reshape.64.idx, bf16[8192,128]{1,0:T(8,128)(2,1)} %bitcast.35), custom_call_target="tpu_custom_call" | custom-call | flops 1048576 | bytes 16777216 | tf_op jit(solution)/shard_map/scatter_rows/pallas_call | solution.py:93
  316.8 13.3 %all-to-all-done.2 = bf16[128,64,128]{2,1,0:T(8,128)(2,1)S(1)} async-done(((bf16[128,64,128]{2,1,0:T(8,128)(2,1)}), bf16[128,64,128]{2,1,0:T(8,128)(2,1)S(1)}, u32[]{:S(2)}, u32[]{:S(2)}) %all-to-all-start.2) | async-done | bytes 2097184 | tf_op jit(solution)/shard_map/all_to_all | solution.py:553
  330.2 0.0 copy-start.1
  330.2 1.3 copy-done.1
  331.5 16.5 %scatter_rows.3 = f32[4096,128]{1,0:T(8,128)} custom-call(s32[8192]{0:T(1024)} %reshape.51.idx, bf16[8192,128]{1,0:T(8,128)(2,1)} %bitcast.34, f32[4096,128]{1,0:T(8,128)} %scatter_rows.2.refs_0_), custom_call_target="tpu_custom_call" | custom-call | flops 1048576 | bytes 16777216 | tf_op jit(solution)/shard_map/scatter_rows/pallas_call | solution.py:93
Async XLA Ops:
  11.8 41.1 %all-to-all-start.1 = ((bf16[128,64,128]{2,1,0:T(8,128)(2,1)}), bf16[128,64,128]{2,1,0:T(8,128)(2,1)S(1)}, u32[]{:S(2)}, u32[]{:S(2)}) async-start(bf16[128,64,128]{2,1,0:T(8,128)(2,1)} %bitcast.37), calls=%async_computation.1 | async-start | bytes 4194304 | tf_op jit(solution)/shard_map/all_to_all | solution.py:553
  52.9 1.3 copy-start
  52.9 7.1 %copy-start.4 = (s32[1,32,512]{2,1,0:T(8,128)S(1)}, s32[1,32,512]{2,1,0:T(8,128)}, u32[]{:S(2)}) copy-start(s32[1,32,512]{2,1,0:T(8,128)} %param.17) | copy-start | bytes 196612
  54.2 50.9 %all-to-all-start = ((bf16[128,64,128]{2,1,0:T(8,128)(2,1)}), bf16[128,64,128]{2,1,0:T(8,128)(2,1)}, u32[]{:S(2)}, u32[]{:S(2)}) async-start(bf16[128,64,128]{2,1,0:T(8,128)(2,1)} %bitcast.36), calls=%async_computation | async-start | bytes 4194304 | tf_op jit(solution)/shard_map/all_to_all | solution.py:553
  72.6 11.9 %copy-start.5 = (bf16[1,8,128]{2,1,0:T(8,128)(2,1)S(1)}, bf16[1,8,128]{2,1,0:T(8,128)(2,1)}, u32[]{:S(2)}) copy-start(bf16[1,8,128]{2,1,0:T(8,128)(2,1)} %param.12) | copy-start | bytes 6148
  72.6 13.0 %copy-start.6 = (bf16[1,1024]{1,0:T(2,128)(2,1)S(1)}, bf16[1,1024]{1,0:T(2,128)(2,1)}, u32[]{:S(2)}) copy-start(bf16[1,1024]{1,0:T(2,128)(2,1)} %param.13) | copy-start | bytes 6148
  249.1 45.4 %all-to-all-start.3 = ((bf16[128,64,128]{2,1,0:T(8,128)(2,1)}), bf16[128,64,128]{2,1,0:T(8,128)(2,1)S(1)}, u32[]{:S(2)}, u32[]{:S(2)}) async-start(bf16[128,64,128]{2,1,0:T(8,128)(2,1)} %bitcast.39), calls=%async_computation.3 | async-start | bytes 4194304 | tf_op jit(solution)/shard_map/all_to_all | solution.py:553
  294.4 1.3 copy-start.2
  294.4 6.0 %copy-start.3 = (s32[1,128,128]{2,1,0:T(8,128)S(1)}, s32[1,128,128]{2,1,0:T(8,128)}, u32[]{:S(2)}) copy-start(s32[1,128,128]{2,1,0:T(8,128)} %param.18) | copy-start | bytes 196612
  294.4 6.0 %copy-start.7 = (s32[1,128]{1,0:T(1,128)S(1)}, s32[1,128]{1,0:T(1,128)}, u32[]{:S(2)}) copy-start(s32[1,128]{1,0:T(1,128)} %param.19) | copy-start | bytes 1540
  295.7 34.4 %all-to-all-start.2 = ((bf16[128,64,128]{2,1,0:T(8,128)(2,1)}), bf16[128,64,128]{2,1,0:T(8,128)(2,1)S(1)}, u32[]{:S(2)}, u32[]{:S(2)}) async-start(bf16[128,64,128]{2,1,0:T(8,128)(2,1)} %bitcast.38), calls=%async_computation.2 | async-start | bytes 4194304 | tf_op jit(solution)/shard_map/all_to_all | solution.py:553
  330.2 1.3 copy-start.1

commit v4 on v3

--- a/solution.py
+++ b/solution.py
@@ -11,7 +11,8 @@
 TN = (((0,), (0,)), ((), ()))
 EPSILON = 1e-05
 DECAY_WEIGHT = 0.5
-MICRO_ROWS = 64
+MICRO_ROWS = 128
+CHUNK = 512
 
 
 def gather_rows(table, ids):
@@ -113,7 +114,6 @@
     samples, features = slots.shape
     embeds = lcb.shape[0]
     shift = cap.bit_length() - 1
-    half = cap // 2
     pairs = owners // 2
 
     def body(slot_ref, lcb_ref, out_ref):
@@ -125,9 +125,7 @@
         for h in range(2):
             slot = slot_ref[0, pl.ds(h, 1), :]
             pair = lax.shift_right_logical(slot, shift + 1)
-            odd = lax.shift_right_logical(slot, shift) & 1
-            col = slot & (cap - 1)
-            place = lax.shift_right_logical(col, shift - 1) * cap + odd * half + (col & (half - 1))
+            place = slot & (2 * cap - 1)
             picks = jnp.where(lane == place, 1.0, 0.0).astype(BF)
             pair16 = jnp.broadcast_to(pair.astype(F32), (16, features)).astype(BF)
             rows = []
@@ -154,48 +152,47 @@
     )(slots.reshape(samples // 2, 2, features), lcb)
 
 
-def compress(matrix, halves):
+def compress(matrix, fetched, embeds):
     pairs, outs, slots = matrix.shape
-    width = halves[0].shape[1]
-    part = slots // 2
+    width = fetched.shape[1]
+    samples = outs // embeds
     step_pairs = 8
-    embeds = 8
-
-    def half_sum(h, before):
-        def body(mat, rows, *refs):
-            out = refs[-1]
-            step = pl.program_id(0)
-
-            @pl.when(step == 0)
-            def _():
-                out[...] = jnp.zeros_like(out) if before is None else refs[0][...]
-
-            total = out[...]
-            for i in range(step_pairs):
-                total += jnp.dot(mat[i], rows[pl.ds(i * part, part), :], preferred_element_type=F32)
-            out[...] = total
-
-        extra = [] if before is None else [before]
-        return pl.pallas_call(
-            body,
-            grid=(pairs // step_pairs,),
-            in_specs=[
-                pl.BlockSpec((step_pairs, outs, part), lambda i: (i, 0, h)),
-                pl.BlockSpec((step_pairs * part, width), lambda i: (i, 0)),
-            ] + [pl.BlockSpec((outs, width), lambda i: (0, 0))] * len(extra),
-            out_specs=pl.BlockSpec((outs, width), lambda i: (0, 0)),
-            out_shape=jax.ShapeDtypeStruct((outs, width), F32),
-            cost_estimate=pl.CostEstimate(flops=2 * outs * pairs * part * width, bytes_accessed=6 << 20, transcendentals=0),
-            name="compress",
-        )(matrix, halves[h], *extra)
-
-    return half_sum(1, half_sum(0, None))
-
-
-def expand(matrix, grads, rows, decay, h):
+
+    def body(mat, rows, out, acc):
+        step = pl.program_id(0)
+
+        @pl.when(step == 0)
+        def _():
+            acc[...] = jnp.zeros_like(acc)
+
+        total = acc[...]
+        for i in range(step_pairs):
+            total += jnp.dot(mat[i], rows[pl.ds(i * slots, slots), :], preferred_element_type=F32)
+        acc[...] = total
+
+        @pl.when(step == pl.num_programs(0) - 1)
+        def _():
+            for k in range(embeds):
+                out[:, k * width : (k + 1) * width] = acc[pl.ds(k, samples, stride=embeds), :].astype(BF)
+
+    return pl.pallas_call(
+        body,
+        grid=(pairs // step_pairs,),
+        in_specs=[
+            pl.BlockSpec((step_pairs, outs, slots), lambda i: (i, 0, 0)),
+            pl.BlockSpec((step_pairs * slots, width), lambda i: (i, 0)),
+        ],
+        out_specs=pl.BlockSpec((samples, embeds * width), lambda i: (0, 0)),
+        out_shape=jax.ShapeDtypeStruct((samples, embeds * width), BF),
+        scratch_shapes=[pltpu.VMEM((outs, width), F32)],
+        name="compress",
+    )(matrix, fetched)
+
+
+def expand(matrix, grads, rows, decay):
     pairs, outs, slots = matrix.shape
     width = rows.shape[1]
-    part = slots // 2
+    part = slots
     step_pairs = 8
     samples, model = grads.shape
     embeds = model // width
@@ -216,7 +213,7 @@
         body,
         grid=(pairs // step_pairs,),
         in_specs=[
-            pl.BlockSpec((step_pairs, outs, part), lambda i: (i, 0, h)),
+            pl.BlockSpec((step_pairs, outs, part), lambda i: (i, 0, 0)),
             pl.BlockSpec((samples, model), lambda i: (0, 0)),
             pl.BlockSpec((step_pairs * part, width), lambda i: (i, 0)),
         ],
@@ -312,19 +309,19 @@
             send((b + part_rows) // 32 - 1)
 
 
-def layer_pipeline(shares, top, mix, unmix, gain, w_up, w_down, up_t, down_t, stages, rows):
+def layer_pipeline(shares, top, mix, unmix, gain, w_up, w_down, stages, rows):
     look, model = shares.shape
     micro = top.shape[0] // rows
     per = rows // look
     inner = w_up.shape[1]
     width = mix.shape[1]
     embeds = model // width
-    chunks = model // 256
+    chunks = model // CHUNK
     copy_to = pltpu.make_async_remote_copy
     copy_here = pltpu.make_async_copy
 
     def body(
-        share_in, top_in, mix_ref, unmix_ref, gain_ref, up_in, down_in, up_t_in, down_t_in, out,
+        share_in, top_in, mix_ref, unmix_ref, gain_ref, up_in, down_in, out,
         acts, cots, acts_out, cots_out, share, up_v, down_v, up_tv, down_tv,
         interact, inv_keep, hidden, prod, normed, gated, unit, pulled, spread,
         wsem, tsem, fsend, frecv, gsend, grecv, isend, irecv, osend, orecv, lsem,
@@ -334,7 +331,7 @@
         loads = [
             copy_here(src, dst, wsem.at[i])
             for i, (src, dst) in enumerate(
-                [(up_in, up_v), (down_in, down_v), (down_t_in, down_tv), (up_t_in, up_tv)]
+                [(up_in, up_v), (down_in, down_v)]
             )
         ]
         loads[0].start()
@@ -368,15 +365,13 @@
         def _():
             own.start()
             own.wait()
-            for section in range(1, stages):
-                entry(jnp.int32(section)).wait_recv()
 
         @pl.when(jnp.logical_not(first))
         def _():
             entry(me).start()
 
         def onward(m, c):
-            piece = pl.ds(c * 256, 256)
+            piece = pl.ds(c * CHUNK, CHUNK)
             return copy_to(
                 src_ref=acts_out.at[m, :, piece], dst_ref=acts.at[m, :, piece],
                 send_sem=fsend.at[m, c], recv_sem=frecv.at[m, c],
@@ -400,6 +395,21 @@
 
         keep_own = copy_here(cots_out.at[0, pl.ds(0, look), :], share, lsem)
         loads[0].wait()
+        late = me > stages // 2
+
+        def turn():
+            tile = 256
+
+            @pl.loop(0, inner // tile)
+            def _(n):
+                at = pl.ds(pl.multiple_of(n * tile, tile), tile)
+                up_tv[at, :] = up_v[:, at].T
+                down_tv[:, at] = down_v[at, :].T
+
+        @pl.when(late)
+        def _():
+            loads[1].wait()
+            turn()
 
         def step(i, carry):
             ahead = jnp.where(last, lax.rem(i, 2) == 0, i < micro)
@@ -413,24 +423,28 @@
                     for c in range(chunks):
                         onward(m, c).wait_recv()
 
+                @pl.when(first)
+                def _():
+                    for j in range(per):
+                        @pl.when(m * per + j > 0)
+                        def _():
+                            entry(m * per + j).wait_recv()
+
                 def ready():
-                    @pl.when(i == 0)
+                    @pl.when((i == 0) & jnp.logical_not(late))
                     def _():
                         loads[1].wait()
-                        loads[2].start()
-                        loads[3].start()
 
                 layer_forward(
                     acts.at[m], mix_ref, gain_ref, up_v, down_v, keep, acts_out.at[m], last, ready,
-                    lambda n, tile: onward(m, n // 256).start(),
+                    lambda n, tile: onward(m, n // CHUNK).start() if (n + tile) % CHUNK == 0 else None,
                 )
 
             @pl.when(jnp.logical_not(ahead))
             def _():
-                @pl.when(m == 0)
+                @pl.when((m == 0) & jnp.logical_not(late))
                 def _():
-                    loads[2].wait()
-                    loads[3].wait()
+                    turn()
 
                 @pl.when(last)
                 def _():
@@ -498,7 +512,7 @@
     tall = embeds * rows
     return pl.pallas_call(
         body,
-        in_specs=[vmem, hbm, vmem, vmem, vmem, hbm, hbm, hbm, hbm],
+        in_specs=[vmem, hbm, vmem, vmem, vmem, hbm, hbm],
         out_specs=vmem,
         out_shape=jax.ShapeDtypeStruct((look, model), BF),
         scratch_shapes=[
@@ -510,7 +524,7 @@
             pltpu.VMEM((micro, rows, inner), BF),
             pltpu.VMEM((tall, model), BF), pltpu.VMEM((rows, model), BF), pltpu.VMEM((rows, inner), BF),
             pltpu.VMEM((rows, model), F32), pltpu.VMEM((tall, width), BF), pltpu.VMEM((tall, model), F32),
-            dma((4,)), dma((micro,)), dma((micro, chunks)), dma((micro, chunks)),
+            dma((2,)), dma((micro,)), dma((micro, chunks)), dma((micro, chunks)),
             dma((micro, per)), dma((micro, per)),
             dma, dma((stages,)), dma((stages,)), dma, dma,
         ],
@@ -518,7 +532,7 @@
             collective_id=0, has_side_effects=True, vmem_limit_bytes=60 << 20
         ),
         name="layer_pipeline",
-    )(shares, top, mix, unmix, gain, w_up, w_down, up_t, down_t)
+    )(shares, top, mix, unmix, gain, w_up, w_down)
 
 
 def mixers(proj):
@@ -546,22 +560,16 @@
     rows_here, embed_width = emb_table.shape
     picked_rows = wanted_rows[0]
 
-    half = cap // 2
 
     def exchange(rows):
-        rows = rows.reshape(owners, half, embed_width)
+        rows = rows.reshape(owners, cap, embed_width)
         rows = lax.all_to_all(rows, ("section", "table"), split_axis=0, concat_axis=0, tiled=True)
-        return rows.reshape(owners * half, embed_width)
-
-    def halves(ids):
-        return [ids[:, h * half : (h + 1) * half].reshape(-1) for h in range(2)]
-
-    fetched = [exchange(gather_rows(emb_table, ids)) for ids in halves(picked_rows)]
-    lookup_slots = lookup_slot[0]
-    look_dev = lookup_slots.shape[0]
+        return rows.reshape(owners * cap, embed_width)
+
+    fetched = exchange(gather_rows(emb_table, picked_rows.reshape(-1)))
     model_width = top_grad.shape[3]
-    matrix = lookup_matrix(lookup_slots, lcb_weight, owners, cap)
-    shares = compress(matrix, fetched).astype(BF).reshape(look_dev, -1)
+    matrix = lookup_matrix(lookup_slot[0], lcb_weight, owners, cap)
+    shares = compress(matrix, fetched, lcb_weight.shape[0])
     mix, unmix = mixers(fm_proj[0])
     lead_share = layer_pipeline(
         shares,
@@ -571,16 +579,13 @@
         norm_gain.astype(F32),
         w_up[0],
         w_down[0],
-        w_up[0].T,
-        w_down[0].T,
         section_count,
         MICRO_ROWS,
     )
+    returned = exchange(expand(matrix, lead_share, fetched, DECAY_WEIGHT))
     live_slots = jnp.arange(cap)[None, :] < row_counts[0][:, None]
-    targets = halves(jnp.where(live_slots, picked_rows, rows_here))
-    returned = [exchange(expand(matrix, lead_share, fetched[h], DECAY_WEIGHT, h)) for h in range(2)]
-    table_grad = scatter_rows(returned[0], targets[0], rows_here)
-    return scatter_rows(returned[1], targets[1], rows_here, table_grad)
+    targets = jnp.where(live_slots, picked_rows, rows_here).reshape(-1)
+    return scatter_rows(returned, targets, rows_here)
 
 
 def solution(mesh):

time: 350 us -> 303 us (0.87)
  Pallas kernels: 220 us -> 185 us
  waiting for transfers between devices: 54.1 us -> 88.8 us
  local copies, waits for them, and re-layouts: 34.8 us -> 2.49 us
  starting transfers between devices: 37.6 us -> 24.3 us
    all_to_all x4 -> x2, waiting for transfers between devices: 54.1 us -> 88.8 us  [exchange(): lax.all_to_all(rows, ('section', 'table'), split_axis=0, concat_axis=0, t...]
    unnamed x19 -> x11, local copies, waits for them, and re-layouts: 28.6 us -> 0.76 us
    pallas_call x3 -> x2, Pallas kernels: 140 us -> 116 us  [the longest x1 108 us: layer_pipeline(): pl.pallas_call(body, in_specs=[vmem, hbm, vmem, vmem, vmem, hbm, hbm], ou...]
    all_to_all x4 -> x2, starting transfers between devices: 37.6 us -> 24.3 us  [exchange(): lax.all_to_all(rows, ('section', 'table'), split_axis=0, concat_axis=0, t...]
    pallas_call x2 -> x1, Pallas kernels: 15.5 us -> 10 us  [expand(): pl.pallas_call(body, grid=(pairs // step_pairs,), in_specs=[pl.BlockSpec(...]
    pallas_call x2 -> x1, Pallas kernels: 31.4 us -> 27.7 us  [scatter_rows(): pl.pallas_call(body, grid=(count // block,), in_specs=[pl.BlockSpec(memor...]
    pallas_call x2 -> x1, Pallas kernels: 20.2 us -> 18.5 us  [gather_rows(): pl.pallas_call(body, grid=(count // block,), in_specs=[pl.BlockSpec(memor...]
  transfers between devices with their start and end apart: 4 -> 2, of which waited for: 3 -> 2; matrix products, arithmetic and copies ran while one was open for 8% -> 1% of each run, Pallas kernels for 15% -> 4%
where the time goes in v4:
time: 303 us; the launch traced here: 302 us
  Pallas kernels  185 us (61%)
  waiting for transfers between devices  88.8 us (29%)
  starting transfers between devices  24.3 us (8%)
    pallas_call x1, Pallas kernels, layer_pipeline(): pl.pallas_call(body, in_specs=[vmem, hbm, vmem, vmem, vmem, hbm, hbm], ou...  108 us
    all_to_all x2, waiting for transfers between devices, exchange(): lax.all_to_all(rows, ('section', 'table'), split_axis=0, concat_axis=0, t...  88.8 us
    pallas_call x1, Pallas kernels, scatter_rows(): pl.pallas_call(body, grid=(count // block,), in_specs=[pl.BlockSpec(memor...  27.7 us
    all_to_all x2, starting transfers between devices, exchange(): lax.all_to_all(rows, ('section', 'table'), split_axis=0, concat_axis=0, t...  24.3 us
    pallas_call x1, Pallas kernels, gather_rows(): pl.pallas_call(body, grid=(count // block,), in_specs=[pl.BlockSpec(memor...  18.5 us
    pallas_call x1, Pallas kernels, lookup_matrix(): pl.pallas_call(body, grid=(samples // 2,), in_specs=[pl.BlockSpec((1, 2,...  12.3 us
    pallas_call x1, Pallas kernels, expand(): pl.pallas_call(body, grid=(pairs // step_pairs,), in_specs=[pl.BlockSpec(...  10 us
    pallas_call x1, Pallas kernels, compress(): pl.pallas_call(body, grid=(pairs // step_pairs,), in_specs=[pl.BlockSpec(...  8.61 us
  transfers between devices with their start and end apart: 2, of which 2 were waited for; matrix products, arithmetic and copies ran while one was open for 1% of the time, Pallas kernels for 4%

profile of v4, /device:TPU:1, one launch (start us, length us, event | category | flops | bytes accessed | tf_op | source)
XLA Modules:
  0.0 301.9 jit_solution(11578575328653072229)
XLA Ops:
  0.0 18.5 %gather_rows.1 = bf16[16384,128]{1,0:T(8,128)(2,1)} custom-call(s32[16384]{0:T(1024)} %bitcast.30, bf16[4096,128]{1,0:T(8,128)(2,1)} %tab.1), custom_call_target="tpu_custom_call" | custom-call | flops 2097152 | bytes 8388608 | tf_op jit(solution)/shard_map/gather_rows/pallas_call | solution.py:38
  18.5 0.0 copy-start.1
  18.5 0.0 copy-start.2
  18.6 0.0 copy-start.3
  18.6 11.9 %all-to-all-start = ((bf16[128,128,128]{2,1,0:T(8,128)(2,1)}), bf16[128,128,128]{2,1,0:T(8,128)(2,1)}, u32[]{:S(2)}, u32[]{:S(2)}) async-start(bf16[128,128,128]{2,1,0:T(8,128)(2,1)} %bitcast.22), calls=%async_computation | async-start | bytes 8388608 | tf_op jit(solution)/shard_map/all_to_all | solution.py:566
  30.5 0.0 copy-done.1
  30.5 0.7 reshape_squeeze.4.slot_ref
  31.2 0.0 copy-done.2
  31.2 0.1 copy.11
  31.3 0.2 broadcast_in_dim.21
  31.5 0.7 copy.14
  32.3 0.0 copy-done.3
  32.3 0.6 convert_element_type.3.gain_ref
  32.9 12.3 %lookup_matrix.1.mat = bf16[64,256,256]{2,1,0:T(8,128)(2,1)} custom-call(s32[16,2,512]{2,1,0:T(2,128)} %reshape_squeeze.4.slot_ref, bf16[8,512]{1,0:T(8,128)(2,1)} %lcb_ref.1), custom_call_target="tpu_custom_call" | custom-call | flops 4294967296 | bytes 16777216 | tf_op jit(solution)/shard_map/lookup_matrix/pallas_call | solution.py:139
  45.2 37.4 %all-to-all-done = bf16[128,128,128]{2,1,0:T(8,128)(2,1)} async-done(((bf16[128,128,128]{2,1,0:T(8,128)(2,1)}), bf16[128,128,128]{2,1,0:T(8,128)(2,1)}, u32[]{:S(2)}, u32[]{:S(2)}) %all-to-all-start) | async-done | bytes 4194336 | tf_op jit(solution)/shard_map/all_to_all | solution.py:566
  82.6 8.6 %compress.1.share_in = bf16[32,1024]{1,0:T(8,128)(2,1)} custom-call(bf16[64,256,256]{2,1,0:T(8,128)(2,1)} %lookup_matrix.1.mat, bf16[16384,128]{1,0:T(8,128)(2,1)} %bitcast.4.rows.rows_ref), custom_call_target="tpu_custom_call" | custom-call | tf_op jit(solution)/shard_map/compress/pallas_call | solution.py:178
  91.2 0.7 broadcast_in_dim.20
  91.9 107.8 %layer_pipeline.1.grad = bf16[32,1024]{1,0:T(8,128)(2,1)} custom-call(bf16[32,1024]{1,0:T(8,128)(2,1)} %compress.1.share_in, bf16[256,1024]{1,0:T(8,128)(2,1)} %bitcast.29, bf16[1024,128]{1,0:T(8,128)(2,1)} %bitcast.27, bf16[128,1024]{1,0:T(8,128)(2,1)} %bitcast.26, f32[1,1024]{1,0:T(1,128)} %convert_element_type.3.gain_ref, bf16[1024,4096]{1,0:T(8,128)(2,1)} %bitcast.24, ...), custom_call_target="tpu_custom_call" | custom-call | tf_op jit(solution)/shard_map/layer_pipeline/pallas_call | solution.py:513
  199.7 10.0 %expand.1 = bf16[16384,128]{1,0:T(8,128)(2,1)} custom-call(bf16[64,256,256]{2,1,0:T(8,128)(2,1)} %lookup_matrix.1.mat, bf16[32,1024]{1,0:T(8,128)(2,1)} %layer_pipeline.1.grad, bf16[16384,128]{1,0:T(8,128)(2,1)} %bitcast.4.rows.rows_ref), custom_call_target="tpu_custom_call" | custom-call | flops 1073741824 | bytes 8388608 | tf_op jit(solution)/shard_map/expand/pallas_call | solution.py:212
  209.7 0.0 copy-start
  209.7 0.0 copy-start.4
  209.7 12.4 %all-to-all-start.1 = ((bf16[128,128,128]{2,1,0:T(8,128)(2,1)}), bf16[128,128,128]{2,1,0:T(8,128)(2,1)}, u32[]{:S(2)}, u32[]{:S(2)}) async-start(bf16[128,128,128]{2,1,0:T(8,128)(2,1)} %bitcast.23), calls=%async_computation.1 | async-start | bytes 8388608 | tf_op jit(solution)/shard_map/all_to_all | solution.py:566
  222.1 0.0 copy-done
  222.1 0.0 copy-done.4
  222.1 0.7 fusion.1.idx
  222.8 51.4 %all-to-all-done.1 = bf16[128,128,128]{2,1,0:T(8,128)(2,1)} async-done(((bf16[128,128,128]{2,1,0:T(8,128)(2,1)}), bf16[128,128,128]{2,1,0:T(8,128)(2,1)}, u32[]{:S(2)}, u32[]{:S(2)}) %all-to-all-start.1) | async-done | bytes 4194336 | tf_op jit(solution)/shard_map/all_to_all | solution.py:566
  274.2 27.7 %scatter_rows.1 = f32[4096,128]{1,0:T(8,128)} custom-call(s32[16384]{0:T(1024)} %fusion.1.idx, bf16[16384,128]{1,0:T(8,128)(2,1)} %bitcast.12.val), custom_call_target="tpu_custom_call" | custom-call | flops 2097152 | bytes 16777216 | tf_op jit(solution)/shard_map/scatter_rows/pallas_call | solution.py:94
Async XLA Ops:
  18.5 12.0 %copy-start.1 = (s32[1,32,512]{2,1,0:T(8,128)S(1)}, s32[1,32,512]{2,1,0:T(8,128)}, u32[]{:S(2)}) copy-start(s32[1,32,512]{2,1,0:T(8,128)} %param.17) | copy-start | bytes 196612
  18.5 12.6 %copy-start.2 = (bf16[1,8,128]{2,1,0:T(8,128)(2,1)S(1)}, bf16[1,8,128]{2,1,0:T(8,128)(2,1)}, u32[]{:S(2)}) copy-start(bf16[1,8,128]{2,1,0:T(8,128)(2,1)} %param.12) | copy-start | bytes 6148
  18.6 13.7 %copy-start.3 = (bf16[1,1024]{1,0:T(2,128)(2,1)S(1)}, bf16[1,1024]{1,0:T(2,128)(2,1)}, u32[]{:S(2)}) copy-start(bf16[1,1024]{1,0:T(2,128)(2,1)} %param.13) | copy-start | bytes 6148
  18.6 64.0 %all-to-all-start = ((bf16[128,128,128]{2,1,0:T(8,128)(2,1)}), bf16[128,128,128]{2,1,0:T(8,128)(2,1)}, u32[]{:S(2)}, u32[]{:S(2)}) async-start(bf16[128,128,128]{2,1,0:T(8,128)(2,1)} %bitcast.22), calls=%async_computation | async-start | bytes 8388608 | tf_op jit(solution)/shard_map/all_to_all | solution.py:566
  209.7 12.4 %copy-start = (s32[1,128,128]{2,1,0:T(8,128)S(1)}, s32[1,128,128]{2,1,0:T(8,128)}, u32[]{:S(2)}) copy-start(s32[1,128,128]{2,1,0:T(8,128)} %param.18) | copy-start | bytes 196612
  209.7 12.4 %copy-start.4 = (s32[1,128]{1,0:T(1,128)S(1)}, s32[1,128]{1,0:T(1,128)}, u32[]{:S(2)}) copy-start(s32[1,128]{1,0:T(1,128)} %param.19) | copy-start | bytes 1540
  209.7 64.5 %all-to-all-start.1 = ((bf16[128,128,128]{2,1,0:T(8,128)(2,1)}), bf16[128,128,128]{2,1,0:T(8,128)(2,1)}, u32[]{:S(2)}, u32[]{:S(2)}) async-start(bf16[128,128,128]{2,1,0:T(8,128)(2,1)} %bitcast.23), calls=%async_computation.1 | async-start | bytes 8388608 | tf_op jit(solution)/shard_map/all_to_all | solution.py:566

commit v5 on v4

--- a/solution.py
+++ b/solution.py
@@ -15,62 +15,19 @@
 CHUNK = 512
 
 
-def gather_rows(table, ids):
-    rows, width = table.shape
-    count = ids.shape[0]
-    block = 1024
-    chunk = 128
-
-    def body(idx, tab, out, wide, tmp):
-        step = pl.program_id(0)
-
-        @pl.when(step == 0)
-        def _():
-            wide[...] = tab[...].astype(F32)
-
-        @pl.loop(0, block // chunk)
-        def _(part):
-            base = step * block + part * chunk
-            for j in range(chunk):
-                tmp[pl.ds(j, 1), :] = wide[pl.ds(idx[base + j], 1), :]
-            out[pl.ds(pl.multiple_of(part * chunk, chunk), chunk), :] = tmp[...].astype(BF)
-
-    return pl.pallas_call(
-        body,
-        grid=(count // block,),
-        in_specs=[
-            pl.BlockSpec(memory_space=pltpu.SMEM),
-            pl.BlockSpec((rows, width), lambda i: (0, 0)),
-        ],
-        out_specs=pl.BlockSpec((block, width), lambda i: (i, 0)),
-        out_shape=jax.ShapeDtypeStruct((count, width), BF),
-        scratch_shapes=[pltpu.VMEM((rows, width), F32), pltpu.VMEM((chunk, width), F32)],
-        cost_estimate=pl.CostEstimate(flops=count * width, bytes_accessed=8 << 20, transcendentals=0),
-        name="gather_rows",
-    )(ids, table)
-
-
-def scatter_rows(values, ids, rows, before=None):
+def scatter_rows(values, own, ids, rows, decay):
     count, width = values.shape
-    extra = [] if before is None else [before]
     block = 1024
     group = 16
 
-    def body(idx, val, *refs):
-        out, acc, wide, sem = refs[-4:]
+    def body(idx, val, mine, out, acc, wide, sem):
         step = pl.program_id(0)
 
         @pl.when(step == 0)
         def _():
-            if before is None:
-                acc[...] = jnp.zeros_like(acc)
-            else:
-                acc[pl.ds(rows, 8), :] = jnp.zeros((8, width), F32)
-                start = pltpu.make_async_copy(refs[0], acc.at[pl.ds(0, rows), :], sem)
-                start.start()
-                start.wait()
-
-        wide[...] = val[...].astype(F32)
+            acc[...] = jnp.zeros_like(acc)
+
+        wide[...] = val[...].astype(F32) + decay * mine[...].astype(F32)
 
         @pl.loop(0, block // (4 * group))
         def _(part):
@@ -97,7 +54,8 @@
         in_specs=[
             pl.BlockSpec(memory_space=pltpu.SMEM),
             pl.BlockSpec((block, width), lambda i: (i, 0)),
-        ] + [pl.BlockSpec(memory_space=pl.ANY)] * len(extra),
+            pl.BlockSpec((block, width), lambda i: (i, 0)),
+        ],
         out_specs=pl.BlockSpec(memory_space=pl.ANY),
         out_shape=jax.ShapeDtypeStruct((rows, width), F32),
         scratch_shapes=[
@@ -107,122 +65,7 @@
         ],
         cost_estimate=pl.CostEstimate(flops=count * width, bytes_accessed=16 << 20, transcendentals=0),
         name="scatter_rows",
-    )(ids, values, *extra)
-
-
-def lookup_matrix(slots, lcb, owners, cap):
-    samples, features = slots.shape
-    embeds = lcb.shape[0]
-    shift = cap.bit_length() - 1
-    pairs = owners // 2
-
-    def body(slot_ref, lcb_ref, out_ref):
-        tiled = jnp.concatenate([lcb_ref[...].astype(F32)] * 2, axis=0).astype(BF)
-        zero = jnp.zeros((), BF)
-        lane = lax.broadcasted_iota(jnp.int32, (2 * cap, features), 0)
-        row = (lax.broadcasted_iota(jnp.int32, (16, features), 0) // embeds).astype(F32).astype(BF)
-        parts = []
-        for h in range(2):
-            slot = slot_ref[0, pl.ds(h, 1), :]
-            pair = lax.shift_right_logical(slot, shift + 1)
-            place = slot & (2 * cap - 1)
-            picks = jnp.where(lane == place, 1.0, 0.0).astype(BF)
-            pair16 = jnp.broadcast_to(pair.astype(F32), (16, features)).astype(BF)
-            rows = []
-            for o in range(0, pairs, 2):
-                rows.append(jnp.where(pair16 == row + jnp.asarray(float(o), BF), tiled, zero))
-            spread = jnp.concatenate(rows, axis=0)
-            got = lax.dot_general(spread, picks, NT, preferred_element_type=F32)
-            parts.append(got.reshape(pairs, embeds, 2 * cap))
-        out_ref[...] = jnp.concatenate(parts, axis=1).astype(BF)
-
-    return pl.pallas_call(
-        body,
-        grid=(samples // 2,),
-        in_specs=[
-            pl.BlockSpec((1, 2, features), lambda i: (i, 0, 0)),
-            pl.BlockSpec((embeds, features), lambda i: (0, 0)),
-        ],
-        out_specs=pl.BlockSpec((pairs, 2 * embeds, 2 * cap), lambda i: (0, i, 0)),
-        out_shape=jax.ShapeDtypeStruct((pairs, samples * embeds, 2 * cap), BF),
-        cost_estimate=pl.CostEstimate(
-            flops=2 * samples * owners * embeds * cap * features, bytes_accessed=16 << 20, transcendentals=0
-        ),
-        name="lookup_matrix",
-    )(slots.reshape(samples // 2, 2, features), lcb)
-
-
-def compress(matrix, fetched, embeds):
-    pairs, outs, slots = matrix.shape
-    width = fetched.shape[1]
-    samples = outs // embeds
-    step_pairs = 8
-
-    def body(mat, rows, out, acc):
-        step = pl.program_id(0)
-
-        @pl.when(step == 0)
-        def _():
-            acc[...] = jnp.zeros_like(acc)
-
-        total = acc[...]
-        for i in range(step_pairs):
-            total += jnp.dot(mat[i], rows[pl.ds(i * slots, slots), :], preferred_element_type=F32)
-        acc[...] = total
-
-        @pl.when(step == pl.num_programs(0) - 1)
-        def _():
-            for k in range(embeds):
-                out[:, k * width : (k + 1) * width] = acc[pl.ds(k, samples, stride=embeds), :].astype(BF)
-
-    return pl.pallas_call(
-        body,
-        grid=(pairs // step_pairs,),
-        in_specs=[
-            pl.BlockSpec((step_pairs, outs, slots), lambda i: (i, 0, 0)),
-            pl.BlockSpec((step_pairs * slots, width), lambda i: (i, 0)),
-        ],
-        out_specs=pl.BlockSpec((samples, embeds * width), lambda i: (0, 0)),
-        out_shape=jax.ShapeDtypeStruct((samples, embeds * width), BF),
-        scratch_shapes=[pltpu.VMEM((outs, width), F32)],
-        name="compress",
-    )(matrix, fetched)
-
-
-def expand(matrix, grads, rows, decay):
-    pairs, outs, slots = matrix.shape
-    width = rows.shape[1]
-    part = slots
-    step_pairs = 8
-    samples, model = grads.shape
-    embeds = model // width
-
-    def body(mat, grad, rows_ref, out, wide, tall):
-        @pl.when(pl.program_id(0) == 0)
-        def _():
-            for k in range(embeds):
-                wide[pl.ds(k, samples, stride=embeds), :] = grad[:, k * width : (k + 1) * width].astype(F32)
-            tall[...] = wide[...].astype(BF)
-
-        for i in range(step_pairs):
-            at = pl.ds(i * part, part)
-            got = lax.dot_general(mat[i], tall[...], TN, preferred_element_type=F32)
-            out[at, :] = (got + decay * rows_ref[at, :].astype(F32)).astype(BF)
-
-    return pl.pallas_call(
-        body,
-        grid=(pairs // step_pairs,),
-        in_specs=[
-            pl.BlockSpec((step_pairs, outs, part), lambda i: (i, 0, 0)),
-            pl.BlockSpec((samples, model), lambda i: (0, 0)),
-            pl.BlockSpec((step_pairs * part, width), lambda i: (i, 0)),
-        ],
-        out_specs=pl.BlockSpec((step_pairs * part, width), lambda i: (i, 0)),
-        out_shape=jax.ShapeDtypeStruct((pairs * part, width), BF),
-        scratch_shapes=[pltpu.VMEM((outs, width), F32), pltpu.VMEM((outs, width), BF)],
-        cost_estimate=pl.CostEstimate(flops=2 * outs * pairs * part * width, bytes_accessed=8 << 20, transcendentals=0),
-        name="expand",
-    )(matrix, grads, rows)
+    )(ids, values, own)
 
 
 def layer_forward(a_ref, mix, gain, w_up, w_down, keep, out_ref, last, ready, send):
@@ -542,6 +385,269 @@
     return mix, unmix
 
 
+def partner(j, tables):
+    pairs = tables // 2
+    order = lax.rem(j * 37, pairs * lax.axis_size("section"))
+    return order // pairs, lax.rem(order, pairs)
+
+
+def place(j, sign):
+    sections, tables = lax.axis_size("section"), lax.axis_size("table")
+    pairs = tables // 2
+    step_s, step_t = partner(j, tables)
+    section = lax.rem(lax.axis_index("section") + sections + sign * step_s, sections)
+    pair = lax.rem(lax.axis_index("table") // 2 + pairs + sign * step_t, pairs)
+    return section, pair
+
+
+def greet(sections, tables):
+    barrier = pltpu.get_barrier_semaphore()
+    me_s, me_t = lax.axis_index("section"), lax.axis_index("table")
+
+    def signal(d, carry):
+        pl.semaphore_signal(
+            barrier, inc=1,
+            device_id=(lax.rem(me_s + d // tables, sections), lax.rem(me_t + lax.rem(d, tables), tables)),
+            device_id_type=pl.DeviceIdType.MESH,
+        )
+        return carry
+
+    lax.fori_loop(1, sections * tables, signal, 0)
+    pl.semaphore_wait(barrier, sections * tables - 1)
+
+
+def fetch_compress(table, ids, slots, lcb, cap):
+    sections, tables = lax.axis_size("section"), lax.axis_size("table")
+    owners = sections * tables
+    pairs = owners // 2
+    groups = 8
+    rows, width = table.shape
+    samples, features = slots.shape
+    embeds = lcb.shape[0]
+    shift = cap.bit_length() - 1
+
+    def body(idx, tab, slot_ref, lcb_ref, sent_out, mat_out, shares, wide, tmp, stage, landed, mat, acc, ssem, rsem, lsem, osem):
+        me_s, me_t = lax.axis_index("section"), lax.axis_index("table")
+        me = me_s * tables + me_t
+        wide[...] = tab[...].astype(F32)
+        greet(sections, tables)
+
+        def target(i):
+            section, pair = place(i // 2, 1)
+            return section, pair * 2 + lax.rem(me_t + lax.rem(i, 2), 2)
+
+        def block(o):
+            return pl.ds(pl.multiple_of(o * cap, cap), cap)
+
+        def send(i):
+            section, spot = target(i)
+            return pltpu.make_async_remote_copy(
+                src_ref=stage.at[block(section * tables + spot), :], dst_ref=landed.at[block(me), :],
+                send_sem=ssem, recv_sem=rsem.at[i // (2 * pairs // groups)],
+                device_id=(section, spot), device_id_type=pl.DeviceIdType.MESH,
+            )
+
+        own = pltpu.make_async_copy(stage.at[block(me), :], landed.at[block(me), :], lsem)
+
+        def gather(i, carry):
+            section, spot = target(i)
+            base = (section * tables + spot) * cap
+            for r in range(cap):
+                tmp[pl.ds(r, 1), :] = wide[pl.ds(idx[base + r], 1), :]
+            stage[pl.ds(pl.multiple_of(base, cap), cap), :] = tmp[...].astype(BF)
+
+            @pl.when(i == 1)
+            def _():
+                own.start()
+
+            @pl.when(i > 1)
+            def _():
+                send(i - 1).start()
+
+            return carry
+
+        lax.fori_loop(0, owners, gather, 0)
+        send(owners - 1).start()
+        keep = pltpu.make_async_copy(stage, sent_out, osem.at[0])
+        keep.start()
+
+        tiled = jnp.concatenate([lcb_ref[...].astype(F32)] * 2, axis=0).astype(BF)
+        zero = jnp.zeros((), BF)
+        lane = lax.broadcasted_iota(jnp.int32, (2 * cap, features), 0)
+        row = (lax.broadcasted_iota(jnp.int32, (16, features), 0) // embeds).astype(F32).astype(BF)
+
+        def select(p, carry):
+            parts = []
+            for h in range(2):
+                slot = slot_ref[p, pl.ds(h, 1), :]
+                pair = lax.shift_right_logical(slot, shift + 1)
+                spot = slot & (2 * cap - 1)
+                picks = jnp.where(lane == spot, 1.0, 0.0).astype(BF)
+                pair16 = jnp.broadcast_to(pair.astype(F32), (16, features)).astype(BF)
+                spread = jnp.concatenate(
+                    [jnp.where(pair16 == row + jnp.asarray(float(o), BF), tiled, zero) for o in range(0, pairs, 2)],
+                    axis=0,
+                )
+                got = lax.dot_general(spread, picks, NT, preferred_element_type=F32)
+                parts.append(got.reshape(pairs, embeds, 2 * cap))
+            mat[:, pl.ds(pl.multiple_of(p * 2 * embeds, 2 * embeds), 2 * embeds), :] = jnp.concatenate(parts, axis=1).astype(BF)
+            return carry
+
+        lax.fori_loop(0, samples // 2, select, 0)
+        save = pltpu.make_async_copy(mat, mat_out, osem.at[1])
+        save.start()
+        acc[...] = jnp.zeros_like(acc)
+        own.wait()
+
+        def collect(g, carry):
+            span = 2 * cap * (pairs // groups)
+
+            @pl.when(g == 0)
+            def _():
+                part = pl.ds(0, span - cap)
+                pltpu.make_async_copy(stage.at[part, :], landed.at[part, :], rsem.at[g]).wait()
+
+            @pl.when(g > 0)
+            def _():
+                part = pl.ds(0, span)
+                pltpu.make_async_copy(stage.at[part, :], landed.at[part, :], rsem.at[g]).wait()
+
+            total = acc[...]
+            for e in range(pairs // groups):
+                section, pair = place(g * (pairs // groups) + e, -1)
+                o = section * (tables // 2) + pair
+                total += jnp.dot(
+                    mat[o], landed[pl.ds(pl.multiple_of(o * 2 * cap, 2 * cap), 2 * cap), :],
+                    preferred_element_type=F32,
+                )
+            acc[...] = total
+            return carry
+
+        lax.fori_loop(0, groups, collect, 0)
+        for k in range(embeds):
+            shares[:, k * width : (k + 1) * width] = acc[pl.ds(k, samples, stride=embeds), :].astype(BF)
+        part = pl.ds(0, (owners - 1) * cap)
+        pltpu.make_async_copy(stage.at[part, :], landed.at[part, :], ssem).wait()
+        keep.wait()
+        save.wait()
+
+    vmem = pl.BlockSpec(memory_space=pltpu.VMEM)
+    hbm = pl.BlockSpec(memory_space=pl.ANY)
+    dma = pltpu.SemaphoreType.DMA
+    return pl.pallas_call(
+        body,
+        in_specs=[pl.BlockSpec(memory_space=pltpu.SMEM), vmem, vmem, vmem],
+        out_specs=[hbm, hbm, vmem],
+        out_shape=[
+            jax.ShapeDtypeStruct((owners * cap, width), BF),
+            jax.ShapeDtypeStruct((pairs, samples * embeds, 2 * cap), BF),
+            jax.ShapeDtypeStruct((samples, embeds * width), BF),
+        ],
+        scratch_shapes=[
+            pltpu.VMEM((rows, width), F32), pltpu.VMEM((cap, width), F32),
+            pltpu.VMEM((owners * cap, width), BF), pltpu.VMEM((owners * cap, width), BF),
+            pltpu.VMEM((pairs, samples * embeds, 2 * cap), BF), pltpu.VMEM((samples * embeds, width), F32),
+            dma, dma((groups,)), dma, dma((2,)),
+        ],
+        compiler_params=pltpu.CompilerParams(collective_id=1, has_side_effects=True, vmem_limit_bytes=60 << 20),
+        name="fetch_compress",
+    )(ids, table, slots.reshape(samples // 2, 2, features), lcb)
+
+
+def expand_return(matrix, grads, cap):
+    sections, tables = lax.axis_size("section"), lax.axis_size("table")
+    owners = sections * tables
+    pairs, outs, slots = matrix.shape
+    samples, model = grads.shape
+    embeds = outs // samples
+    width = model // embeds
+    groups = 8
+    per = pairs // groups
+
+    def body(mat_in, grad, landed, done, mat, wide, tall, stage, msem, ssem, rsem, lsem):
+        me_s, me_t = lax.axis_index("section"), lax.axis_index("table")
+        me = me_s * tables + me_t
+
+        def load(j):
+            section, pair = place(j, 1)
+            o = section * (tables // 2) + pair
+            return pltpu.make_async_copy(mat_in.at[o], mat.at[j], msem.at[j])
+
+        def begin(j, carry):
+            load(j).start()
+            return carry
+
+        lax.fori_loop(0, pairs, begin, 0)
+        for k in range(embeds):
+            wide[pl.ds(k, samples, stride=embeds), :] = grad[:, k * width : (k + 1) * width].astype(F32)
+        tall[...] = wide[...].astype(BF)
+        greet(sections, tables)
+
+        def block(o):
+            return pl.ds(pl.multiple_of(o * cap, cap), cap)
+
+        def send(section, spot):
+            return pltpu.make_async_remote_copy(
+                src_ref=stage.at[block(section * tables + spot), :], dst_ref=landed.at[block(me), :],
+                send_sem=ssem, recv_sem=rsem, device_id=(section, spot), device_id_type=pl.DeviceIdType.MESH,
+            )
+
+        own = pltpu.make_async_copy(stage.at[block(me), :], landed.at[block(me), :], lsem)
+
+        def pair_out(j):
+            section, pair = place(j, 1)
+
+            @pl.when(j == 0)
+            def _():
+                own.start()
+                send(me_s, me_t + 1 - 2 * lax.rem(me_t, 2)).start()
+
+            @pl.when(j > 0)
+            def _():
+                for b in range(2):
+                    send(section, pair * 2 + b).start()
+
+        def work(j, carry):
+            section, pair = place(j, 1)
+            o = section * (tables // 2) + pair
+            load(j).wait()
+            got = lax.dot_general(mat[j], tall[...], TN, preferred_element_type=F32)
+            stage[pl.ds(pl.multiple_of(o * slots, slots), slots), :] = got.astype(BF)
+
+            @pl.when(j > 0)
+            def _():
+                pair_out(j - 1)
+
+            return carry
+
+        lax.fori_loop(0, pairs, work, 0)
+        pair_out(jnp.int32(pairs - 1))
+        own.wait()
+        part = pl.ds(0, (owners - 1) * cap)
+        pltpu.make_async_copy(stage.at[part, :], landed.at[part, :], rsem).wait()
+        pltpu.make_async_copy(stage.at[part, :], landed.at[part, :], ssem).wait()
+        done[...] = jnp.zeros_like(done)
+
+    vmem = pl.BlockSpec(memory_space=pltpu.VMEM)
+    hbm = pl.BlockSpec(memory_space=pl.ANY)
+    dma = pltpu.SemaphoreType.DMA
+    return pl.pallas_call(
+        body,
+        in_specs=[hbm, vmem],
+        out_specs=[hbm, vmem],
+        out_shape=[
+            jax.ShapeDtypeStruct((owners * cap, width), BF),
+            jax.ShapeDtypeStruct((8, 128), F32),
+        ],
+        scratch_shapes=[
+            pltpu.VMEM(matrix.shape, BF), pltpu.VMEM((outs, width), F32), pltpu.VMEM((outs, width), BF),
+            pltpu.VMEM((owners * cap, width), BF), dma((pairs,)), dma, dma, dma,
+        ],
+        compiler_params=pltpu.CompilerParams(collective_id=2, has_side_effects=True, vmem_limit_bytes=60 << 20),
+        name="expand_return",
+    )(matrix, grads)[0]
+
+
 def per_device(
     emb_table,
     lcb_weight,
@@ -555,21 +661,14 @@
     row_counts,
 ):
     section_count = lax.axis_size("section")
-    owners = section_count * lax.axis_size("table")
     cap = wanted_rows.shape[2]
-    rows_here, embed_width = emb_table.shape
+    rows_here = emb_table.shape[0]
     picked_rows = wanted_rows[0]
 
-
-    def exchange(rows):
-        rows = rows.reshape(owners, cap, embed_width)
-        rows = lax.all_to_all(rows, ("section", "table"), split_axis=0, concat_axis=0, tiled=True)
-        return rows.reshape(owners * cap, embed_width)
-
-    fetched = exchange(gather_rows(emb_table, picked_rows.reshape(-1)))
     model_width = top_grad.shape[3]
-    matrix = lookup_matrix(lookup_slot[0], lcb_weight, owners, cap)
-    shares = compress(matrix, fetched, lcb_weight.shape[0])
+    sent, matrix, shares = fetch_compress(
+        emb_table, picked_rows.reshape(-1), lookup_slot[0], lcb_weight, cap
+    )
     mix, unmix = mixers(fm_proj[0])
     lead_share = layer_pipeline(
         shares,
@@ -582,10 +681,10 @@
         section_count,
         MICRO_ROWS,
     )
-    returned = exchange(expand(matrix, lead_share, fetched, DECAY_WEIGHT))
+    returned = expand_return(matrix, lead_share, cap)
     live_slots = jnp.arange(cap)[None, :] < row_counts[0][:, None]
     targets = jnp.where(live_slots, picked_rows, rows_here).reshape(-1)
-    return scatter_rows(returned, targets, rows_here)
+    return scatter_rows(returned, sent, targets, rows_here, DECAY_WEIGHT)
 
 
 def solution(mesh):

time: 303 us -> 280 us (0.924)
  waiting for transfers between devices: 88.8 us -> 0 us
  Pallas kernels: 185 us -> 272 us
  starting transfers between devices: 24.3 us -> 0 us
    all_to_all x2 -> x0, waiting for transfers between devices: 88.8 us -> none  [exchange(): lax.all_to_all(rows, ('section', 'table'), split_axis=0, concat_axis=0, t...]
    pallas_call x4 -> x2, Pallas kernels: 49.5 us -> 136 us  [the longest x1 70 us: expand_return(): pl.pallas_call(body, in_specs=[hbm, vmem], out_specs=[hbm, vmem], out_sha...]
    all_to_all x2 -> x0, starting transfers between devices: 24.3 us -> none  [exchange(): lax.all_to_all(rows, ('section', 'table'), split_axis=0, concat_axis=0, t...]
  transfers between devices with their start and end apart: 2 -> 0, of which waited for: 2 -> 0; matrix products, arithmetic and copies ran while one was open for 1% -> 0% of each run, Pallas kernels for 4% -> 0%
where the time goes in v5:
time: 280 us; the launch traced here: 279 us
  Pallas kernels  272 us (97%)
  local copies, waits for them, and re-layouts  4.69 us (2%)
    pallas_call x1, Pallas kernels, layer_pipeline(): pl.pallas_call(body, in_specs=[vmem, hbm, vmem, vmem, vmem, hbm, hbm], ou...  108 us
    pallas_call x1, Pallas kernels, expand_return(): pl.pallas_call(body, in_specs=[hbm, vmem], out_specs=[hbm, vmem], out_sha...  70 us
    pallas_call x1, Pallas kernels, fetch_compress(): pl.pallas_call(body, in_specs=[pl.BlockSpec(memory_space=pltpu.SMEM), vme...  66.5 us
    pallas_call x1, Pallas kernels, scatter_rows(): pl.pallas_call(body, grid=(count // block,), in_specs=[pl.BlockSpec(memor...  28.3 us

profile of v5, /device:TPU:1, one launch (start us, length us, event | category | flops | bytes accessed | tf_op | source)
XLA Modules:
  0.0 279.2 jit_solution(7297640027103347178)
XLA Ops:
  0.0 1.5 reshape_squeeze.4.slot_ref
  1.5 66.5 %fetch_compress.1 = (bf16[16384,128]{1,0:T(8,128)(2,1)}, bf16[64,256,256]{2,1,0:T(8,128)(2,1)}, bf16[32,1024]{1,0:T(8,128)(2,1)}) custom-call(s32[16384]{0:T(1024)} %bitcast.24, bf16[4096,128]{1,0:T(8,128)(2,1)} %tab.1, s32[16,2,512]{2,1,0:T(2,128)} %reshape_squeeze.4.slot_ref, bf16[8,512]{1,0:T(8,128)(2,1)} %lcb_ref.1), custom_call_target="tpu_custom_call" | custom-call | tf_op jit(solution)/shard_map/fetch_compress/pallas_call | solution.py:537
  68.0 0.8 copy.11
  68.8 0.2 broadcast_in_dim.21
  69.0 0.8 copy.14
  69.7 1.4 broadcast_in_dim.20
  71.2 1.3 convert_element_type.3.gain_ref
  72.4 107.7 %layer_pipeline.1.grad = bf16[32,1024]{1,0:T(8,128)(2,1)} custom-call(bf16[32,1024]{1,0:T(8,128)(2,1)} %get-tuple-element.10.share_in, bf16[256,1024]{1,0:T(8,128)(2,1)} %bitcast.23, bf16[1024,128]{1,0:T(8,128)(2,1)} %bitcast.21, bf16[128,1024]{1,0:T(8,128)(2,1)} %bitcast.20, f32[1,1024]{1,0:T(1,128)} %convert_element_type.3.gain_ref, ...), custom_call_target="tpu_custom_call" | custom-call | tf_op jit(solution)/shard_map/layer_pipeline/pallas_call | solution.py:356
  180.1 0.0 copy-start
  180.1 0.0 copy-start.1
  180.2 70.0 %expand_return.1 = (bf16[16384,128]{1,0:T(8,128)(2,1)}, f32[8,128]{1,0:T(8,128)}) custom-call(bf16[64,256,256]{2,1,0:T(8,128)(2,1)} %get-tuple-element.9.mat_in, bf16[32,1024]{1,0:T(8,128)(2,1)} %layer_pipeline.1.grad), custom_call_target="tpu_custom_call" | custom-call | tf_op jit(solution)/shard_map/expand_return/pallas_call | solution.py:634
  250.1 0.0 copy-done
  250.2 0.0 copy-done.1
  250.2 0.7 fusion.1.idx
  250.9 28.3 %scatter_rows.1 = f32[4096,128]{1,0:T(8,128)} custom-call(s32[16384]{0:T(1024)} %fusion.1.idx, bf16[16384,128]{1,0:T(8,128)(2,1)} %get-tuple-element.11.val, bf16[16384,128]{1,0:T(8,128)(2,1)} %get-tuple-element.12.mine), custom_call_target="tpu_custom_call" | custom-call | flops 2097152 | bytes 16777216 | tf_op jit(solution)/shard_map/scatter_rows/pallas_call | solution.py:51
Async XLA Ops:
  180.1 70.0 %copy-start = (s32[1,128,128]{2,1,0:T(8,128)S(1)}, s32[1,128,128]{2,1,0:T(8,128)}, u32[]{:S(2)}) copy-start(s32[1,128,128]{2,1,0:T(8,128)} %param.18) | copy-start | bytes 196612
  180.1 70.0 %copy-start.1 = (s32[1,128]{1,0:T(1,128)S(1)}, s32[1,128]{1,0:T(1,128)}, u32[]{:S(2)}) copy-start(s32[1,128]{1,0:T(1,128)} %param.19) | copy-start | bytes 1540

commit v6 on v5

--- a/solution.py
+++ b/solution.py
@@ -13,40 +13,54 @@
 DECAY_WEIGHT = 0.5
 MICRO_ROWS = 128
 CHUNK = 512
+WAYS = 4
+GROUP = 4
 
 
 def scatter_rows(values, own, ids, rows, decay):
     count, width = values.shape
     block = 1024
-    group = 16
-
-    def body(idx, val, mine, out, acc, wide, sem):
+    cap = 128
+    group = GROUP
+
+    def body(idx, val, mine, out, *scratch):
+        sums, (wide, sem) = scratch[:WAYS], scratch[WAYS:]
         step = pl.program_id(0)
 
         @pl.when(step == 0)
         def _():
-            acc[...] = jnp.zeros_like(acc)
+            for total in sums:
+                total[...] = jnp.zeros_like(total)
 
         wide[...] = val[...].astype(F32) + decay * mine[...].astype(F32)
 
-        @pl.loop(0, block // (4 * group))
+        @pl.loop(0, block // (WAYS * cap))
         def _(part):
-            for sub in range(4):
-                at = part * (4 * group) + sub * group
-                base = step * block + at
-                where = [idx[base + j] for j in range(group)]
-                new = [
-                    acc[pl.ds(where[j], 1), :] + wide[pl.ds(at + j, 1), :]
-                    for j in range(group)
-                ]
-                for j in range(group):
-                    acc[pl.ds(where[j], 1), :] = new[j]
+            for at in range(0, cap, group):
+                for h, total in enumerate(sums):
+                    start = part * (WAYS * cap) + h * cap + at
+                    base = step * block + start
+                    where = [idx[base + j] for j in range(group)]
+                    new = [
+                        total[pl.ds(where[j], 1), :] + wide[pl.ds(start + j, 1), :]
+                        for j in range(group)
+                    ]
+                    for j in range(group):
+                        total[pl.ds(where[j], 1), :] = new[j]
 
         @pl.when(step == pl.num_programs(0) - 1)
         def _():
-            copy = pltpu.make_async_copy(acc.at[pl.ds(0, rows), :], out, sem)
-            copy.start()
-            copy.wait()
+            tile = 512
+            copies = []
+            for n in range(0, rows, tile):
+                whole = sums[0][n : n + tile, :]
+                for total in sums[1:]:
+                    whole += total[n : n + tile, :]
+                sums[0][n : n + tile, :] = whole
+                copies.append(pltpu.make_async_copy(sums[0].at[pl.ds(n, tile), :], out.at[pl.ds(n, tile), :], sem.at[n // tile]))
+                copies[-1].start()
+            for copy in copies:
+                copy.wait()
 
     return pl.pallas_call(
         body,
@@ -59,25 +73,31 @@
         out_specs=pl.BlockSpec(memory_space=pl.ANY),
         out_shape=jax.ShapeDtypeStruct((rows, width), F32),
         scratch_shapes=[
-            pltpu.VMEM((rows + 8, width), F32),
+            *[pltpu.VMEM((rows + 8, width), F32)] * WAYS,
             pltpu.VMEM((block, width), F32),
-            pltpu.SemaphoreType.DMA,
+            pltpu.SemaphoreType.DMA((rows // 512,)),
         ],
-        cost_estimate=pl.CostEstimate(flops=count * width, bytes_accessed=16 << 20, transcendentals=0),
         name="scatter_rows",
     )(ids, values, own)
 
 
+def column(ref, k, width, rows=slice(None)):
+    chunk = ref.shape[-1]
+    at = (k * width) % chunk
+    return ref[k * width // chunk, rows, at : at + width]
+
+
 def layer_forward(a_ref, mix, gain, w_up, w_down, keep, out_ref, last, ready, send):
     interact, inv_keep, hidden, prod, normed = keep
-    rows, model = a_ref.shape
+    chunks, rows, chunk = a_ref.shape
+    model = chunks * chunk
     width = mix.shape[1]
     embeds = model // width
     inner = w_up.shape[1]
     cols = [slice(k * width, (k + 1) * width) for k in range(embeds)]
     for k in range(embeds):
         for q in range(k, embeds):
-            both = a_ref[:, cols[k]] * a_ref[:, cols[q]]
+            both = column(a_ref, k, width) * column(a_ref, q, width)
             prod[k * rows : (k + 1) * rows, cols[q]] = both
             if q > k:
                 prod[q * rows : (q + 1) * rows, cols[k]] = both
@@ -99,16 +119,15 @@
 
     @pl.when(jnp.logical_not(last))
     def _():
-        tile = 256
-        for n in range(0, model, tile):
-            got = jnp.dot(hidden[...], w_down[:, n : n + tile], preferred_element_type=F32)
-            out_ref[:, n : n + tile] = (got + a_ref[:, n : n + tile].astype(F32)).astype(BF)
-            send(n, tile)
+        for c in range(chunks):
+            got = jnp.dot(hidden[...], w_down[:, c * chunk : (c + 1) * chunk], preferred_element_type=F32)
+            out_ref[c] = (got + a_ref[c].astype(F32)).astype(BF)
+            send(c)
 
 
 def layer_backward(a_ref, g_ref, unmix, gain, up_t, down_t, keep, gated, unit, pulled, spread, out_ref, send):
     interact, inv_keep, hidden, prod, normed = keep
-    rows, model = a_ref.shape
+    rows, model = g_ref.shape
     width = unmix.shape[0]
     embeds = model // width
     inner = down_t.shape[1]
@@ -138,7 +157,7 @@
     part_rows = 16
     for b in range(0, rows, part_rows):
         here = pl.ds(b, part_rows)
-        a = [a_ref[here, cols[k]].astype(F32) for k in range(embeds)]
+        a = [column(a_ref, k, width, here).astype(F32) for k in range(embeds)]
         total = [g_ref[here, cols[k]].astype(F32) for k in range(embeds)]
         for k in range(embeds):
             for q in range(k, embeds):
@@ -152,21 +171,21 @@
             send((b + part_rows) // 32 - 1)
 
 
-def layer_pipeline(shares, top, mix, unmix, gain, w_up, w_down, stages, rows):
-    look, model = shares.shape
+def layer_pipeline(shares, top, proj, gain, w_up, w_down, stages, rows):
+    chunks, look, chunk = shares.shape
+    model = chunks * chunk
     micro = top.shape[0] // rows
     per = rows // look
     inner = w_up.shape[1]
-    width = mix.shape[1]
-    embeds = model // width
-    chunks = model // CHUNK
+    embeds, width = proj.shape
     copy_to = pltpu.make_async_remote_copy
     copy_here = pltpu.make_async_copy
 
     def body(
-        share_in, top_in, mix_ref, unmix_ref, gain_ref, up_in, down_in, out,
+        share_in, top_in, proj_ref, gain_in, up_in, down_in, out,
         acts, cots, acts_out, cots_out, share, up_v, down_v, up_tv, down_tv,
         interact, inv_keep, hidden, prod, normed, gated, unit, pulled, spread,
+        mix_ref, unmix_ref, gain_ref,
         wsem, tsem, fsend, frecv, gsend, grecv, isend, irecv, osend, orecv, lsem,
     ):
         me = lax.axis_index("section")
@@ -178,7 +197,6 @@
             )
         ]
         loads[0].start()
-        loads[1].start()
         tops = [copy_here(top_in.at[pl.ds(m * rows, rows), :], cots.at[m], tsem.at[m]) for m in range(micro)]
 
         @pl.when(last)
@@ -186,6 +204,13 @@
             for m in range(micro):
                 tops[m].start()
 
+        gain_ref[...] = gain_in[...].astype(F32)
+        narrow = proj_ref[...].astype(F32)
+        for k in range(embeds):
+            part = slice(k * width, (k + 1) * width)
+            line = jnp.broadcast_to(narrow[k : k + 1, :], (width, width))
+            mix_ref[part, :] = line.astype(BF)
+            unmix_ref[:, part] = line.T.astype(BF)
         barrier = pltpu.get_barrier_semaphore()
         for d in range(1, stages):
             pl.semaphore_signal(
@@ -197,12 +222,12 @@
         def entry(section):
             slot, off = section // per, lax.rem(section, per) * look
             return copy_to(
-                src_ref=share_in, dst_ref=acts.at[slot, pl.ds(pl.multiple_of(off, look), look), :],
+                src_ref=share_in, dst_ref=acts.at[slot, :, pl.ds(pl.multiple_of(off, look), look), :],
                 send_sem=isend, recv_sem=irecv.at[section],
                 device_id={"section": 0}, device_id_type=pl.DeviceIdType.MESH,
             )
 
-        own = copy_here(share_in, acts.at[0, pl.ds(0, look), :], irecv.at[0])
+        own = copy_here(share_in, acts.at[0, :, pl.ds(0, look), :], irecv.at[0])
 
         @pl.when(first)
         def _():
@@ -214,9 +239,8 @@
             entry(me).start()
 
         def onward(m, c):
-            piece = pl.ds(c * CHUNK, CHUNK)
             return copy_to(
-                src_ref=acts_out.at[m, :, piece], dst_ref=acts.at[m, :, piece],
+                src_ref=acts_out.at[m, c], dst_ref=acts.at[m, c],
                 send_sem=fsend.at[m, c], recv_sem=frecv.at[m, c],
                 device_id={"section": lax.rem(me + 1, stages)}, device_id_type=pl.DeviceIdType.MESH,
             )
@@ -238,6 +262,7 @@
 
         keep_own = copy_here(cots_out.at[0, pl.ds(0, look), :], share, lsem)
         loads[0].wait()
+        loads[1].start()
         late = me > stages // 2
 
         def turn():
@@ -280,7 +305,7 @@
 
                 layer_forward(
                     acts.at[m], mix_ref, gain_ref, up_v, down_v, keep, acts_out.at[m], last, ready,
-                    lambda n, tile: onward(m, n // CHUNK).start() if (n + tile) % CHUNK == 0 else None,
+                    lambda c: onward(m, c).start(),
                 )
 
             @pl.when(jnp.logical_not(ahead))
@@ -352,14 +377,15 @@
     hbm = pl.BlockSpec(memory_space=pl.ANY)
     dma = pltpu.SemaphoreType.DMA
     block = (micro, rows, model)
+    wide = (micro, chunks, rows, chunk)
     tall = embeds * rows
     return pl.pallas_call(
         body,
-        in_specs=[vmem, hbm, vmem, vmem, vmem, hbm, hbm],
+        in_specs=[vmem, hbm, vmem, vmem, hbm, hbm],
         out_specs=vmem,
         out_shape=jax.ShapeDtypeStruct((look, model), BF),
         scratch_shapes=[
-            pltpu.VMEM(block, BF), pltpu.VMEM(block, BF), pltpu.VMEM(block, BF), pltpu.VMEM(block, BF),
+            pltpu.VMEM(wide, BF), pltpu.VMEM(block, BF), pltpu.VMEM(wide, BF), pltpu.VMEM(block, BF),
             pltpu.VMEM((look, model), BF),
             pltpu.VMEM((model, inner), BF), pltpu.VMEM((inner, model), BF),
             pltpu.VMEM((inner, model), BF), pltpu.VMEM((model, inner), BF),
@@ -367,6 +393,7 @@
             pltpu.VMEM((micro, rows, inner), BF),
             pltpu.VMEM((tall, model), BF), pltpu.VMEM((rows, model), BF), pltpu.VMEM((rows, inner), BF),
             pltpu.VMEM((rows, model), F32), pltpu.VMEM((tall, width), BF), pltpu.VMEM((tall, model), F32),
+            pltpu.VMEM((model, width), BF), pltpu.VMEM((width, model), BF), pltpu.VMEM((1, model), F32),
             dma((2,)), dma((micro,)), dma((micro, chunks)), dma((micro, chunks)),
             dma((micro, per)), dma((micro, per)),
             dma, dma((stages,)), dma((stages,)), dma, dma,
@@ -375,14 +402,7 @@
             collective_id=0, has_side_effects=True, vmem_limit_bytes=60 << 20
         ),
         name="layer_pipeline",
-    )(shares, top, mix, unmix, gain, w_up, w_down)
-
-
-def mixers(proj):
-    embeds, width = proj.shape
-    mix = jnp.broadcast_to(proj[:, None, :], (embeds, width, width)).reshape(embeds * width, width)
-    unmix = jnp.broadcast_to(proj.T[:, :, None], (width, embeds, width)).reshape(width, embeds * width)
-    return mix, unmix
+    )(shares, top, proj, gain, w_up, w_down)
 
 
 def partner(j, tables):
@@ -416,17 +436,18 @@
     pl.semaphore_wait(barrier, sections * tables - 1)
 
 
-def fetch_compress(table, ids, slots, lcb, cap):
+def fetch_compress(table, wanted, counts, slots, lcb, chunk):
     sections, tables = lax.axis_size("section"), lax.axis_size("table")
     owners = sections * tables
     pairs = owners // 2
     groups = 8
     rows, width = table.shape
     samples, features = slots.shape
+    cap = wanted.shape[1]
     embeds = lcb.shape[0]
     shift = cap.bit_length() - 1
 
-    def body(idx, tab, slot_ref, lcb_ref, sent_out, mat_out, shares, wide, tmp, stage, landed, mat, acc, ssem, rsem, lsem, osem):
+    def body(idx, tab, wanted_ref, count_ref, slot_ref, lcb_ref, sent_out, mat_out, targets, shares, wide, tmp, stage, landed, mat, acc, ssem, rsem, lsem, osem):
         me_s, me_t = lax.axis_index("section"), lax.axis_index("table")
         me = me_s * tables + me_t
         wide[...] = tab[...].astype(F32)
@@ -479,7 +500,7 @@
         def select(p, carry):
             parts = []
             for h in range(2):
-                slot = slot_ref[p, pl.ds(h, 1), :]
+                slot = slot_ref[pl.ds(p * 2 + h, 1), :]
                 pair = lax.shift_right_logical(slot, shift + 1)
                 spot = slot & (2 * cap - 1)
                 picks = jnp.where(lane == spot, 1.0, 0.0).astype(BF)
@@ -496,6 +517,9 @@
         lax.fori_loop(0, samples // 2, select, 0)
         save = pltpu.make_async_copy(mat, mat_out, osem.at[1])
         save.start()
+        live = jnp.broadcast_to(count_ref[...].astype(F32), (owners, owners)).T
+        spot = lax.broadcasted_iota(jnp.int32, (owners, cap), 1).astype(F32)
+        targets[...] = jnp.where(spot < live[:, :cap], wanted_ref[...], rows)
         acc[...] = jnp.zeros_like(acc)
         own.wait()
 
@@ -525,7 +549,8 @@
 
         lax.fori_loop(0, groups, collect, 0)
         for k in range(embeds):
-            shares[:, k * width : (k + 1) * width] = acc[pl.ds(k, samples, stride=embeds), :].astype(BF)
+            at = (k * width) % chunk
+            shares[k * width // chunk, :, at : at + width] = acc[pl.ds(k, samples, stride=embeds), :].astype(BF)
         part = pl.ds(0, (owners - 1) * cap)
         pltpu.make_async_copy(stage.at[part, :], landed.at[part, :], ssem).wait()
         keep.wait()
@@ -536,12 +561,13 @@
     dma = pltpu.SemaphoreType.DMA
     return pl.pallas_call(
         body,
-        in_specs=[pl.BlockSpec(memory_space=pltpu.SMEM), vmem, vmem, vmem],
-        out_specs=[hbm, hbm, vmem],
+        in_specs=[pl.BlockSpec(memory_space=pltpu.SMEM), vmem, vmem, vmem, vmem, vmem],
+        out_specs=[hbm, hbm, vmem, vmem],
         out_shape=[
             jax.ShapeDtypeStruct((owners * cap, width), BF),
             jax.ShapeDtypeStruct((pairs, samples * embeds, 2 * cap), BF),
-            jax.ShapeDtypeStruct((samples, embeds * width), BF),
+            jax.ShapeDtypeStruct((owners, cap), jnp.int32),
+            jax.ShapeDtypeStruct((embeds * width // chunk, samples, chunk), BF),
         ],
         scratch_shapes=[
             pltpu.VMEM((rows, width), F32), pltpu.VMEM((cap, width), F32),
@@ -551,7 +577,7 @@
         ],
         compiler_params=pltpu.CompilerParams(collective_id=1, has_side_effects=True, vmem_limit_bytes=60 << 20),
         name="fetch_compress",
-    )(ids, table, slots.reshape(samples // 2, 2, features), lcb)
+    )(wanted.reshape(-1), table, wanted, counts, slots, lcb)
 
 
 def expand_return(matrix, grads, cap):
@@ -662,29 +688,23 @@
 ):
     section_count = lax.axis_size("section")
     cap = wanted_rows.shape[2]
-    rows_here = emb_table.shape[0]
-    picked_rows = wanted_rows[0]
 
     model_width = top_grad.shape[3]
-    sent, matrix, shares = fetch_compress(
-        emb_table, picked_rows.reshape(-1), lookup_slot[0], lcb_weight, cap
+    sent, matrix, targets, shares = fetch_compress(
+        emb_table, wanted_rows[0], row_counts, lookup_slot[0], lcb_weight, CHUNK
     )
-    mix, unmix = mixers(fm_proj[0])
     lead_share = layer_pipeline(
         shares,
         top_grad.reshape(-1, model_width),
-        mix,
-        unmix,
-        norm_gain.astype(F32),
+        fm_proj[0],
+        norm_gain,
         w_up[0],
         w_down[0],
         section_count,
         MICRO_ROWS,
     )
     returned = expand_return(matrix, lead_share, cap)
-    live_slots = jnp.arange(cap)[None, :] < row_counts[0][:, None]
-    targets = jnp.where(live_slots, picked_rows, rows_here).reshape(-1)
-    return scatter_rows(returned, sent, targets, rows_here, DECAY_WEIGHT)
+    return scatter_rows(returned, sent, targets.reshape(-1), emb_table.shape[0], DECAY_WEIGHT)
 
 
 def solution(mesh):

time: 280 us -> 264 us (0.943)
  Pallas kernels: 272 us -> 264 us
  local copies, waits for them, and re-layouts: 4.69 us -> 0 us
    pallas_call x1, Pallas kernels: 28.3 us -> 20 us  [scatter_rows(): pl.pallas_call(body, grid=(count // block,), in_specs=[pl.BlockSpec(memor...]
where the time goes in v6:
time: 264 us
  Pallas kernels  264 us (100%)
    pallas_call x1, Pallas kernels, layer_pipeline(): pl.pallas_call(body, in_specs=[vmem, hbm, vmem, vmem, hbm, hbm], out_spec...  108 us
    pallas_call x1, Pallas kernels, expand_return(): pl.pallas_call(body, in_specs=[hbm, vmem], out_specs=[hbm, vmem], out_sha...  69.3 us
    pallas_call x1, Pallas kernels, fetch_compress(): pl.pallas_call(body, in_specs=[pl.BlockSpec(memory_space=pltpu.SMEM), vme...  66.6 us
    pallas_call x1, Pallas kernels, scatter_rows(): pl.pallas_call(body, grid=(count // block,), in_specs=[pl.BlockSpec(memor...  20 us

profile of v6, /device:TPU:1, one launch (start us, length us, event | category | flops | bytes accessed | tf_op | source)
XLA Modules:
  0.0 263.7 jit_solution(17883371637457451710)
XLA Ops:
  0.0 66.6 %fetch_compress.1 = (bf16[16384,128]{1,0:T(8,128)(2,1)}, bf16[64,256,256]{2,1,0:T(8,128)(2,1)}, s32[128,128]{1,0:T(8,128)}, bf16[2,32,512]{2,1,0:T(8,128)(2,1)}) custom-call(s32[16384]{0:T(1024)} %bitcast.11, bf16[4096,128]{1,0:T(8,128)(2,1)} %tab.1, s32[128,128]{1,0:T(8,128)} %bitcast.12, s32[1,128]{1,0:T(1,128)} %count_ref.1, s32[32,512]{1,0:T(8,128)} %bitcast.14, ...), custom_call_target="tpu_custom_call" | custom-call | tf_op jit(solution)/shard_map/fetch_compress/pallas_call | solution.py:562
  66.6 107.8 %layer_pipeline.1.grad = bf16[32,1024]{1,0:T(8,128)(2,1)} custom-call(bf16[2,32,512]{2,1,0:T(8,128)(2,1)} %get-tuple-element.12.share_in, bf16[256,1024]{1,0:T(8,128)(2,1)} %bitcast.10, bf16[8,128]{1,0:T(8,128)(2,1)} %bitcast.15, bf16[1,1024]{1,0:T(2,128)(2,1)} %gain_in.1, bf16[1024,4096]{1,0:T(8,128)(2,1)} %bitcast.8, bf16[4096,1024]{1,0:T(8,128)(2,1)} %bitcast.9), custom_call_target="tpu_custom_call" | custom-call | tf_op jit(solution)/shard_map/layer_pipeline/pallas_call | solution.py:382
  174.4 69.3 %expand_return.1 = (bf16[16384,128]{1,0:T(8,128)(2,1)}, f32[8,128]{1,0:T(8,128)}) custom-call(bf16[64,256,256]{2,1,0:T(8,128)(2,1)} %get-tuple-element.11.mat_in, bf16[32,1024]{1,0:T(8,128)(2,1)} %layer_pipeline.1.grad), custom_call_target="tpu_custom_call" | custom-call | tf_op jit(solution)/shard_map/expand_return/pallas_call | solution.py:660
  243.7 20.0 %scatter_rows.1 = f32[4096,128]{1,0:T(8,128)} custom-call(s32[16384]{0:T(1024)} %bitcast.13, bf16[16384,128]{1,0:T(8,128)(2,1)} %get-tuple-element.13.val, bf16[16384,128]{1,0:T(8,128)(2,1)} %get-tuple-element.14.mine), custom_call_target="tpu_custom_call" | custom-call | tf_op jit(solution)/shard_map/scatter_rows/pallas_call | solution.py:65

commit v7 on v6

--- a/solution.py
+++ b/solution.py
@@ -407,7 +407,7 @@
 
 def partner(j, tables):
     pairs = tables // 2
-    order = lax.rem(j * 37, pairs * lax.axis_size("section"))
+    order = lax.rem(j * 21, pairs * lax.axis_size("section"))
     return order // pairs, lax.rem(order, pairs)
 
 

time: 264 us -> 266 us (level)
  no operation moved by 1% of the time
where the time goes in v7:
time: 266 us; the launch traced here: 265 us
  Pallas kernels  265 us (100%)
    pallas_call x1, Pallas kernels, layer_pipeline(): pl.pallas_call(body, in_specs=[vmem, hbm, vmem, vmem, hbm, hbm], out_spec...  108 us
    pallas_call x1, Pallas kernels, expand_return(): pl.pallas_call(body, in_specs=[hbm, vmem], out_specs=[hbm, vmem], out_sha...  69 us
    pallas_call x1, Pallas kernels, fetch_compress(): pl.pallas_call(body, in_specs=[pl.BlockSpec(memory_space=pltpu.SMEM), vme...  67.8 us
    pallas_call x1, Pallas kernels, scatter_rows(): pl.pallas_call(body, grid=(count // block,), in_specs=[pl.BlockSpec(memor...  20 us

profile of v7, /device:TPU:1, one launch (start us, length us, event | category | flops | bytes accessed | tf_op | source)
XLA Modules:
  0.0 265.0 jit_solution(1502795917538021879)
XLA Ops:
  0.0 67.8 %fetch_compress.1 = (bf16[16384,128]{1,0:T(8,128)(2,1)}, bf16[64,256,256]{2,1,0:T(8,128)(2,1)}, s32[128,128]{1,0:T(8,128)}, bf16[2,32,512]{2,1,0:T(8,128)(2,1)}) custom-call(s32[16384]{0:T(1024)} %bitcast.11, bf16[4096,128]{1,0:T(8,128)(2,1)} %tab.1, s32[128,128]{1,0:T(8,128)} %bitcast.12, s32[1,128]{1,0:T(1,128)} %count_ref.1, s32[32,512]{1,0:T(8,128)} %bitcast.14, ...), custom_call_target="tpu_custom_call" | custom-call | tf_op jit(solution)/shard_map/fetch_compress/pallas_call | solution.py:562
  67.9 108.2 %layer_pipeline.1.grad = bf16[32,1024]{1,0:T(8,128)(2,1)} custom-call(bf16[2,32,512]{2,1,0:T(8,128)(2,1)} %get-tuple-element.12.share_in, bf16[256,1024]{1,0:T(8,128)(2,1)} %bitcast.10, bf16[8,128]{1,0:T(8,128)(2,1)} %bitcast.15, bf16[1,1024]{1,0:T(2,128)(2,1)} %gain_in.1, bf16[1024,4096]{1,0:T(8,128)(2,1)} %bitcast.8, bf16[4096,1024]{1,0:T(8,128)(2,1)} %bitcast.9), custom_call_target="tpu_custom_call" | custom-call | tf_op jit(solution)/shard_map/layer_pipeline/pallas_call | solution.py:382
  176.1 69.0 %expand_return.1 = (bf16[16384,128]{1,0:T(8,128)(2,1)}, f32[8,128]{1,0:T(8,128)}) custom-call(bf16[64,256,256]{2,1,0:T(8,128)(2,1)} %get-tuple-element.11.mat_in, bf16[32,1024]{1,0:T(8,128)(2,1)} %layer_pipeline.1.grad), custom_call_target="tpu_custom_call" | custom-call | tf_op jit(solution)/shard_map/expand_return/pallas_call | solution.py:660
  245.1 20.0 %scatter_rows.1 = f32[4096,128]{1,0:T(8,128)} custom-call(s32[16384]{0:T(1024)} %bitcast.13, bf16[16384,128]{1,0:T(8,128)(2,1)} %get-tuple-element.13.val, bf16[16384,128]{1,0:T(8,128)(2,1)} %get-tuple-element.14.mine), custom_call_target="tpu_custom_call" | custom-call | tf_op jit(solution)/shard_map/scatter_rows/pallas_call | solution.py:65
